TPU v7x, 32 devices: a whole 2x2x4 slice. The times are simulated.
32 devices in a mesh: fsdp: 4 (over z), context: 4 (over y, x), tensor: 2 (over core).
Axes of the slice: x: 2, y: 2, z: 4, core: 2. Of those that a mesh axis runs over, the one named last changes fastest.
Arguments:
- tokens: bfloat16 [4, 1024, 2048], P('fsdp', 'context'), may hold values from -6 to 6
- out_grad: bfloat16 [4, 1024, 2048], P('fsdp', 'context'), may hold values from -6 to 6
- lengths: int32 [4, 4], P('fsdp'), may hold values from 1 to 512, 768 in all within a row
- attention_gain: float32 [2048], P(('fsdp', 'context')), may hold values from 0.5 to 1.5
- query_weight: float32 [2048, 2048], P(('fsdp', 'context'), 'tensor'), may hold values from -0.5 to 0.5
- key_weight: float32 [2048, 512], P(('fsdp', 'context'), 'tensor'), may hold values from -0.5 to 0.5
- value_weight: float32 [2048, 512], P(('fsdp', 'context'), 'tensor'), may hold values from -0.125 to 0.125
- output_weight: float32 [2048, 2048], P(('fsdp', 'context'), 'tensor'), may hold values from -3 to 3
- feed_gain: float32 [2048], P(('fsdp', 'context')), may hold values from 0.5 to 1.5
- gate_weight: float32 [2048, 8192], P(('fsdp', 'context'), 'tensor'), may hold values from -0.125 to 0.125
- up_weight: float32 [2048, 8192], P(('fsdp', 'context'), 'tensor'), may hold values from -0.125 to 0.125
- down_weight: float32 [2048, 8192], P(('fsdp', 'context'), 'tensor'), may hold values from -0.5 to 0.5
Outputs:
- output: bfloat16 [4, 1024, 2048], P('fsdp', 'context')
- input_grad: bfloat16 [4, 1024, 2048], P('fsdp', 'context')
- grad_attention_gain: float32 [2048], P(('fsdp', 'context'))
- grad_query: float32 [2048, 2048], P(('fsdp', 'context'), 'tensor')
- grad_key: float32 [2048, 512], P(('fsdp', 'context'), 'tensor')
- grad_value: float32 [2048, 512], P(('fsdp', 'context'), 'tensor')
- grad_output_weight: float32 [2048, 2048], P(('fsdp', 'context'), 'tensor')
- grad_feed_gain: float32 [2048], P(('fsdp', 'context'))
- grad_gate: float32 [2048, 8192], P(('fsdp', 'context'), 'tensor')
- grad_up: float32 [2048, 8192], P(('fsdp', 'context'), 'tensor')
- grad_down: float32 [2048, 8192], P(('fsdp', 'context'), 'tensor')
Inputs may be any that keep to these rules, and one draw needn't show every extreme that they name: Each group's 4 lengths sum to 768 and the largest is exactly 512; sequences lie one after another from the group's first slot, the remaining slots are padding.
All inputs are finite; a program needn't handle non-finite values.
Results may differ from a plain program's by a relative error of at most 0.02.
Values may be sent and summed in bfloat16 or wider, within the bound.
A program may use at most 256 MiB of HBM per device.

v0:
```python
import jax
import jax.numpy as jnp
from jax import lax
from jax.sharding import PartitionSpec as P

HEAD = 64


norm_eps = 1e-05
attention_mult = 0.015625
residual_mult = 0.22
rope_base = 10000000.0


def slot_layout(seq_lengths, total_rows):
    seq_ends = jnp.cumsum(seq_lengths)
    starts = seq_ends - seq_lengths
    slot_ids = jnp.arange(total_rows, dtype=jnp.int32)
    before = (slot_ids[:, None] >= seq_ends[None, :]).astype(jnp.int32)
    segment = jnp.sum(before, axis=1)
    seq_count = seq_lengths.shape[0]
    valid_rows = segment < seq_count
    inside = (slot_ids[:, None] >= starts[None, :]) & (slot_ids[:, None] < seq_ends[None, :])
    position = jnp.sum(jnp.where(inside, slot_ids[:, None] - starts[None, :], 0), axis=1)
    segment = jnp.where(valid_rows, segment, seq_count + slot_ids)
    return (segment, position, valid_rows)


def rope_tables(position, width):
    half_width = width // 2
    frequency = rope_base ** (-jnp.arange(half_width, dtype=jnp.float32) * 2.0 / width)
    angles = position.astype(jnp.float32)[:, None] * frequency[None, :]
    angles = jnp.concatenate([angles, angles], axis=1)
    return (jnp.cos(angles), jnp.sin(angles))


def turn_half(vectors):
    half_width = vectors.shape[-1] // 2
    return jnp.concatenate([-vectors[..., half_width:], vectors[..., :half_width]], axis=-1)


def rotate(vectors, cos_table, sine_table):
    return vectors * cos_table[:, None, :] + turn_half(vectors) * sine_table[:, None, :]


def rotate_back(grads, cos_table, sine_table):
    return grads * cos_table[:, None, :] - turn_half(grads * sine_table[:, None, :])


def norm_back(normed_grad, unit, gain, inverse):
    scaled = normed_grad * gain
    return inverse * (scaled - unit * jnp.mean(scaled * unit, axis=-1, keepdims=True))


def attention_shards(attention_gain, query_weight, key_weight, value_weight, output_weight):
    return (
        lax.all_gather(
            attention_gain.astype(jnp.bfloat16), ("fsdp", "context"), axis=0, tiled=True
        ),
        lax.all_gather(query_weight.astype(jnp.bfloat16), ("fsdp", "context"), axis=0, tiled=True),
        lax.all_gather(key_weight.astype(jnp.bfloat16), ("fsdp", "context"), axis=0, tiled=True),
        lax.all_gather(value_weight.astype(jnp.bfloat16), ("fsdp", "context"), axis=0, tiled=True),
        lax.all_gather(output_weight.astype(jnp.bfloat16), ("fsdp", "context"), axis=0, tiled=True),
    )


def feed_shards(feed_gain, gate_weight, up_weight, down_weight):
    return (
        lax.all_gather(feed_gain.astype(jnp.bfloat16), ("fsdp", "context"), axis=0, tiled=True),
        lax.all_gather(gate_weight.astype(jnp.bfloat16), ("fsdp", "context"), axis=0, tiled=True),
        lax.all_gather(up_weight.astype(jnp.bfloat16), ("fsdp", "context"), axis=0, tiled=True),
        lax.all_gather(down_weight.astype(jnp.bfloat16), ("fsdp", "context"), axis=0, tiled=True),
    )


def on_device(
    tokens,
    out_grad,
    lengths,
    attention_gain,
    query_weight,
    key_weight,
    value_weight,
    output_weight,
    feed_gain,
    gate_weight,
    up_weight,
    down_weight,
):
    local_rows = tokens.shape[1]
    group_rows = local_rows * lax.axis_size("context")
    first_row = lax.axis_index("context") * local_rows
    segment, position, valid_rows = slot_layout(lengths[0], group_rows)
    local_segment = lax.dynamic_slice_in_dim(segment, first_row, local_rows)
    local_position = lax.dynamic_slice_in_dim(position, first_row, local_rows)
    local_valid = lax.dynamic_slice_in_dim(valid_rows, first_row, local_rows)
    slot_ids = jnp.arange(group_rows, dtype=jnp.int32)
    local_slots = first_row + jnp.arange(local_rows, dtype=jnp.int32)
    allowed = (local_segment[:, None] == segment[None, :]) & (
        local_slots[:, None] >= slot_ids[None, :]
    )
    inputs = tokens[0].astype(jnp.float32)
    attn_set = attention_shards(
        attention_gain, query_weight, key_weight, value_weight, output_weight
    )
    gain_one = attn_set[0].astype(jnp.float32)
    inverse_one = lax.rsqrt(jnp.mean(inputs * inputs, axis=-1, keepdims=True) + norm_eps)
    unit_one = inputs * inverse_one
    normed_one = (unit_one * gain_one).astype(jnp.bfloat16)
    queries = jnp.dot(normed_one, attn_set[1], preferred_element_type=jnp.float32)
    keys_lin = jnp.dot(normed_one, attn_set[2], preferred_element_type=jnp.float32)
    values_low = jnp.dot(normed_one, attn_set[3], preferred_element_type=jnp.float32).astype(
        jnp.bfloat16
    )
    heads_local = queries.shape[1] // HEAD
    kv_local = keys_lin.shape[1] // HEAD
    per_group = heads_local // kv_local
    cos_table, sine_table = rope_tables(local_position, HEAD)
    queries_rot = rotate(
        queries.reshape(local_rows, heads_local, HEAD), cos_table, sine_table
    ).astype(jnp.bfloat16)
    keys_rot = rotate(keys_lin.reshape(local_rows, kv_local, HEAD), cos_table, sine_table).astype(
        jnp.bfloat16
    )
    keys_all, values_all = (
        lax.all_gather(
            keys_rot.reshape(local_rows, kv_local * HEAD), "context", axis=0, tiled=True
        ),
        lax.all_gather(values_low, "context", axis=0, tiled=True),
    )
    query_heads = queries_rot.reshape(local_rows, kv_local, per_group, HEAD).transpose(1, 0, 2, 3)
    key_heads = keys_all.reshape(group_rows, kv_local, HEAD).transpose(1, 0, 2)
    value_heads = values_all.reshape(group_rows, kv_local, HEAD).transpose(1, 0, 2)

    def head_scores(query_head, key_head):
        raw_scores = jnp.einsum(
            "tgd,sd->gts", query_head, key_head, preferred_element_type=jnp.float32
        )
        return jnp.where(allowed[None], raw_scores * attention_mult, -1e30)

    def head_forward(pieces):
        query_head, key_head, value_head = pieces
        scores = head_scores(query_head, key_head)
        highest = jnp.max(scores, axis=-1, keepdims=True)
        weight = jnp.exp(scores - highest)
        row_totals = jnp.sum(weight, axis=-1, keepdims=True)
        probabilities = (weight / row_totals).astype(jnp.bfloat16)
        mixed = jnp.einsum(
            "gts,sd->tgd", probabilities, value_head, preferred_element_type=jnp.float32
        )
        return (mixed, (highest + jnp.log(row_totals))[..., 0])

    mixed_heads, log_totals = lax.map(head_forward, (query_heads, key_heads, value_heads))
    attended = (
        mixed_heads.transpose(1, 0, 2, 3)
        .reshape(local_rows, heads_local * HEAD)
        .astype(jnp.bfloat16)
    )
    attn_part = jnp.einsum("tq,dq->td", attended, attn_set[4], preferred_element_type=jnp.float32)
    attn_out = lax.psum(attn_part.astype(jnp.bfloat16), "tensor").astype(jnp.float32)
    hidden_state = inputs + residual_mult * attn_out
    feed_set = feed_shards(feed_gain, gate_weight, up_weight, down_weight)
    gain_two = feed_set[0].astype(jnp.float32)
    inverse_two = lax.rsqrt(
        jnp.mean(hidden_state * hidden_state, axis=-1, keepdims=True) + norm_eps
    )
    unit_two = hidden_state * inverse_two
    normed_two = (unit_two * gain_two).astype(jnp.bfloat16)
    gate_out = jnp.dot(normed_two, feed_set[1], preferred_element_type=jnp.float32)
    up_out = jnp.dot(normed_two, feed_set[2], preferred_element_type=jnp.float32)
    inner_act = (jax.nn.silu(gate_out) * up_out).astype(jnp.bfloat16)
    feed_part = jnp.einsum("tf,df->td", inner_act, feed_set[3], preferred_element_type=jnp.float32)
    feed_out = lax.psum(feed_part.astype(jnp.bfloat16), "tensor").astype(jnp.float32)
    output = hidden_state + residual_mult * feed_out
    cotangent = out_grad[0].astype(jnp.float32) * local_valid[:, None].astype(jnp.float32)
    feed_back = feed_shards(feed_gain, gate_weight, up_weight, down_weight)
    feed_grad = (residual_mult * cotangent).astype(jnp.bfloat16)
    down_term = jnp.einsum("td,tf->df", feed_grad, inner_act, preferred_element_type=jnp.float32)
    inner_grad = jnp.dot(feed_grad, feed_back[3], preferred_element_type=jnp.float32)
    sigmoid_gate = jax.nn.sigmoid(gate_out)
    gate_grad = (
        inner_grad * up_out * sigmoid_gate * (1.0 + gate_out * (1.0 - sigmoid_gate))
    ).astype(jnp.bfloat16)
    up_grad = (inner_grad * jax.nn.silu(gate_out)).astype(jnp.bfloat16)
    gate_term = jnp.einsum("td,tf->df", normed_two, gate_grad, preferred_element_type=jnp.float32)
    up_term = jnp.einsum("td,tf->df", normed_two, up_grad, preferred_element_type=jnp.float32)
    normed_part_two = jnp.einsum(
        "tf,df->td", gate_grad, feed_back[1], preferred_element_type=jnp.float32
    )
    normed_part_two = normed_part_two + jnp.einsum(
        "tf,df->td", up_grad, feed_back[2], preferred_element_type=jnp.float32
    )
    normed_grad_two = lax.psum(normed_part_two.astype(jnp.bfloat16), "tensor").astype(jnp.float32)
    feed_gain_term = jnp.sum(normed_grad_two * unit_two, axis=0)
    hidden_grad = cotangent + norm_back(normed_grad_two, unit_two, gain_two, inverse_two)
    feed_sums = (
        lax.psum_scatter(feed_gain_term, ("fsdp", "context"), scatter_dimension=0, tiled=True),
        lax.psum_scatter(gate_term, ("fsdp", "context"), scatter_dimension=0, tiled=True),
        lax.psum_scatter(up_term, ("fsdp", "context"), scatter_dimension=0, tiled=True),
        lax.psum_scatter(down_term, ("fsdp", "context"), scatter_dimension=0, tiled=True),
    )
    attn_back = attention_shards(
        attention_gain, query_weight, key_weight, value_weight, output_weight
    )
    attn_grad = (residual_mult * hidden_grad).astype(jnp.bfloat16)
    out_term = jnp.einsum("td,tq->dq", attn_grad, attended, preferred_element_type=jnp.float32)
    mixed_grad = jnp.dot(attn_grad, attn_back[4], preferred_element_type=jnp.float32).astype(
        jnp.bfloat16
    )
    mixed_grad_heads = mixed_grad.reshape(local_rows, kv_local, per_group, HEAD).transpose(
        1, 0, 2, 3
    )

    def head_backward(pieces):
        query_head, key_head, value_head, grad_head, log_head = pieces
        scores = head_scores(query_head, key_head)
        probabilities = jnp.exp(scores - log_head[..., None])
        prob_low = probabilities.astype(jnp.bfloat16)
        prob_grad = jnp.einsum(
            "tgd,sd->gts", grad_head, value_head, preferred_element_type=jnp.float32
        )
        row_dot = jnp.sum(probabilities * prob_grad, axis=-1, keepdims=True)
        score_grad = (attention_mult * probabilities * (prob_grad - row_dot)).astype(jnp.bfloat16)
        query_grad = jnp.einsum(
            "gts,sd->tgd", score_grad, key_head, preferred_element_type=jnp.float32
        )
        key_grad = jnp.einsum(
            "gts,tgd->sd", score_grad, query_head, preferred_element_type=jnp.float32
        )
        value_grad = jnp.einsum(
            "gts,tgd->sd", prob_low, grad_head, preferred_element_type=jnp.float32
        )
        return (query_grad, key_grad, value_grad)

    query_grads, key_grads, value_grads = lax.map(
        head_backward, (query_heads, key_heads, value_heads, mixed_grad_heads, log_totals)
    )
    key_grads = key_grads.transpose(1, 0, 2).reshape(group_rows, kv_local * HEAD)
    value_grads = value_grads.transpose(1, 0, 2).reshape(group_rows, kv_local * HEAD)
    local_key_grad, local_value_grad = (
        lax.psum_scatter(
            key_grads.astype(jnp.bfloat16), "context", scatter_dimension=0, tiled=True
        ).astype(jnp.float32),
        lax.psum_scatter(
            value_grads.astype(jnp.bfloat16), "context", scatter_dimension=0, tiled=True
        ).astype(jnp.float32),
    )
    query_grad_rot = query_grads.transpose(1, 0, 2, 3).reshape(local_rows, heads_local, HEAD)
    query_grad_low = (
        rotate_back(query_grad_rot, cos_table, sine_table)
        .reshape(local_rows, heads_local * HEAD)
        .astype(jnp.bfloat16)
    )
    key_grad_low = (
        rotate_back(local_key_grad.reshape(local_rows, kv_local, HEAD), cos_table, sine_table)
        .reshape(local_rows, kv_local * HEAD)
        .astype(jnp.bfloat16)
    )
    value_grad_low = local_value_grad.astype(jnp.bfloat16)
    query_term = jnp.einsum(
        "td,tq->dq", normed_one, query_grad_low, preferred_element_type=jnp.float32
    )
    key_term = jnp.einsum("td,tq->dq", normed_one, key_grad_low, preferred_element_type=jnp.float32)
    value_term = jnp.einsum(
        "td,tq->dq", normed_one, value_grad_low, preferred_element_type=jnp.float32
    )
    normed_part_one = jnp.einsum(
        "tq,dq->td", query_grad_low, attn_back[1], preferred_element_type=jnp.float32
    )
    normed_part_one = normed_part_one + jnp.einsum(
        "tq,dq->td", key_grad_low, attn_back[2], preferred_element_type=jnp.float32
    )
    normed_part_one = normed_part_one + jnp.einsum(
        "tq,dq->td", value_grad_low, attn_back[3], preferred_element_type=jnp.float32
    )
    normed_grad_one = lax.psum(normed_part_one.astype(jnp.bfloat16), "tensor").astype(jnp.float32)
    attn_gain_term = jnp.sum(normed_grad_one * unit_one, axis=0)
    input_grad = hidden_grad + norm_back(normed_grad_one, unit_one, gain_one, inverse_one)
    attn_sums = (
        lax.psum_scatter(attn_gain_term, ("fsdp", "context"), scatter_dimension=0, tiled=True),
        lax.psum_scatter(query_term, ("fsdp", "context"), scatter_dimension=0, tiled=True),
        lax.psum_scatter(key_term, ("fsdp", "context"), scatter_dimension=0, tiled=True),
        lax.psum_scatter(value_term, ("fsdp", "context"), scatter_dimension=0, tiled=True),
        lax.psum_scatter(out_term, ("fsdp", "context"), scatter_dimension=0, tiled=True),
    )
    return (
        output.astype(jnp.bfloat16)[None],
        input_grad.astype(jnp.bfloat16)[None],
        attn_sums[0],
        attn_sums[1],
        attn_sums[2],
        attn_sums[3],
        attn_sums[4],
        feed_sums[0],
        feed_sums[1],
        feed_sums[2],
        feed_sums[3],
    )


def solution(mesh):
    return jax.shard_map(
        on_device,
        mesh=mesh,
        in_specs=(
            P("fsdp", "context", None),
            P("fsdp", "context", None),
            P("fsdp", None),
            P(("fsdp", "context")),
            P(("fsdp", "context"), "tensor"),
            P(("fsdp", "context"), "tensor"),
            P(("fsdp", "context"), "tensor"),
            P(("fsdp", "context"), "tensor"),
            P(("fsdp", "context")),
            P(("fsdp", "context"), "tensor"),
            P(("fsdp", "context"), "tensor"),
            P(("fsdp", "context"), "tensor"),
        ),
        out_specs=(
            P("fsdp", "context", None),
            P("fsdp", "context", None),
            P(("fsdp", "context")),
            P(("fsdp", "context"), "tensor"),
            P(("fsdp", "context"), "tensor"),
            P(("fsdp", "context"), "tensor"),
            P(("fsdp", "context"), "tensor"),
            P(("fsdp", "context")),
            P(("fsdp", "context"), "tensor"),
            P(("fsdp", "context"), "tensor"),
            P(("fsdp", "context"), "tensor"),
        ),
        check_vma=False,
    )
```

profile of v0, /device:TPU:0, one launch (start us, length us, event | category | flops | bytes accessed | tf_op | source)
XLA Modules:
  0.0 3686.5 jit_solution(1155907496614948670)
XLA Ops:
  15.2 42.4 %all-gather = bf16[16,1,128]{2,1,0:T(2,128)(2,1)S(1)} all-gather(bf16[1,1,128]{2,1,0:T(2,128)(2,1)S(1)} %convert_bitcast_fusion.2), channel_id=1, replica_groups=mesh['fsdp'=4,'context'=4,'tensor'=2] {'fsdp','context'}, dimensions={0}, use_global_device_ids=true | all-gather | bytes 4352 | tf_op jit(solution)/shard_map/all_gather | solution.py:57
  58.6 10.6 all-gather.10.cloned.1.call-done
  70.9 10.2 all_gather.42
  81.4 45.1 %all-gather.12.cloned.1.call-done = bf16[2048,256]{1,0:T(8,128)(2,1)} async-done(((bf16[128,256]{1,0:T(8,128)(2,1)}), bf16[2048,256]{1,0:T(8,128)(2,1)}) %all-gather.12.cloned.1.call-update) | async-done | bytes 1048592 | tf_op jit(solution)/shard_map/all_gather | solution.py:61
  130.6 14.0 all_gather.44
  144.6 60.3 %all-gather.14.cloned.1.call-done = bf16[2048,1024]{1,0:T(8,128)(2,1)} async-done(((bf16[128,1024]{1,0:T(8,128)(2,1)}), bf16[2048,1024]{1,0:T(8,128)(2,1)}) %all-gather.14.cloned.1.call-update) | async-done | bytes 4194320 | tf_op jit(solution)/shard_map/all_gather | solution.py:60
  215.3 16.9 while.30
  232.2 50.1 %all-gather.16.cloned.1.call-done = bf16[2048,1024]{1,0:T(8,128)(2,1)} async-done(((bf16[128,1024]{1,0:T(8,128)(2,1)}), bf16[2048,1024]{1,0:T(8,128)(2,1)}) %all-gather.16.cloned.1.call-update) | async-done | bytes 4194320 | tf_op jit(solution)/shard_map/all_gather | solution.py:63
  294.0 38.8 %all-gather.1 = bf16[16,1,128]{2,1,0:T(2,128)(2,1)S(1)} all-gather(bf16[1,1,128]{2,1,0:T(2,128)(2,1)S(1)} %convert_bitcast_fusion.1), channel_id=1, replica_groups=mesh['fsdp'=4,'context'=4,'tensor'=2] {'fsdp','context'}, dimensions={0}, use_global_device_ids=true | all-gather | bytes 4352 | tf_op jit(solution)/shard_map/all_gather | solution.py:69
  335.3 165.3 %all-gather.18.cloned.1.call-done = bf16[2048,4096]{1,0:T(8,128)(2,1)} async-done(((bf16[128,4096]{1,0:T(8,128)(2,1)}), bf16[2048,4096]{1,0:T(8,128)(2,1)}) %all-gather.18.cloned.1.call-update) | async-done | bytes 16777232 | tf_op jit(solution)/shard_map/all_gather | solution.py:70
  500.6 10.1 fusion.130
  510.8 182.4 %all-gather.20.cloned.1.call-done = bf16[2048,4096]{1,0:T(8,128)(2,1)} async-done(((bf16[128,4096]{1,0:T(8,128)(2,1)}), bf16[2048,4096]{1,0:T(8,128)(2,1)}) %all-gather.20.cloned.1.call-update) | async-done | bytes 16777232 | tf_op jit(solution)/shard_map/all_gather | solution.py:71
  693.2 12.6 fusion.131
  705.8 180.0 %all-gather.22.cloned.1.call-done = bf16[2048,4096]{1,0:T(8,128)(2,1)} async-done(((bf16[128,4096]{1,0:T(8,128)(2,1)}), bf16[2048,4096]{1,0:T(8,128)(2,1)}) %all-gather.22.cloned.1.call-update) | async-done | bytes 16777232 | tf_op jit(solution)/shard_map/all_gather | solution.py:72
  885.8 16.4 multiply_convert_fusion
  902.1 12.3 fusion.132
  914.4 12.4 fusion.70
  927.0 17.7 all-reduce.10.cloned.1.call-done
  954.4 46.3 %while.31 = (s32[]{:T(128)}, f32[4,256,4,64]{1,3,2,0:T(8,128)}, bf16[4,1024,64]{1,2,0:T(8,128)(2,1)}, bf16[4,1024,64]{1,2,0:T(8,128)(2,1)}, bf16[4,1024,64]{1,2,...) while((s32[]{:T(128)}, f32[4,256,4,64]{1,3,2,0:T(8,128)}, ...), condition=%wide.region_15.16_spmd.clone.clone, body=%wide.region_13.15_spmd.clone.sunk.clone | while | flops 688651264 | bytes 44735756 | solution.py:235
  1000.7 11.9 convolution_convert_fusion
  1032.6 22.4 reduce-scatter.12.cloned.1.call-done
  1069.1 6.8 fusion.104
  1075.9 18.0 fusion.134
  1094.3 17.7 fusion.135
  1112.0 15.0 fusion.105
  1131.0 76.1 %all-reduce.2 = (f32[2048]{0:T(1024)S(1)}, f32[2048]{0:T(1024)S(1)}) all-reduce(f32[2048]{0:T(1024)S(1)} %get-tuple-element.162, f32[2048]{0:T(1024)S(1)} %copy-done.27), channel_id=4, replica_groups=mesh['fsdp'=4,'context'=4,'tensor'=2] {'fsdp','context'}, use_global_device_ids=true, to_apply=%region_21.22.clone | all-reduce | flops 4096 | bytes 32768
  1212.7 33.7 reduce-scatter.18.cloned.1.call-done
  1246.4 177.4 %reduce-scatter.14.cloned.1.call-done = f32[128,1024]{1,0:T(8,128)} async-done(((f32[2048,1024]{1,0:T(8,128)}), f32[128,1024]{1,0:T(8,128)}) %reduce-scatter.14.cloned.1.call-update) | async-done | bytes 524304 | tf_op jit(solution)/shard_map/reduce_scatter | solution.py:281
  1423.8 183.0 %reduce-scatter.20.cloned.1.call-done = f32[128,1024]{1,0:T(8,128)} async-done(((f32[2048,1024]{1,0:T(8,128)}), f32[128,1024]{1,0:T(8,128)}) %reduce-scatter.20.cloned.1.call-update) | async-done | bytes 524304 | tf_op jit(solution)/shard_map/reduce_scatter | solution.py:284
  1606.8 688.8 %reduce-scatter.22.cloned.1.call-done = f32[128,4096]{1,0:T(8,128)} async-done(((f32[2048,4096]{1,0:T(8,128)}), f32[128,4096]{1,0:T(8,128)}) %reduce-scatter.22.cloned.1.call-update) | async-done | bytes 2097168 | tf_op jit(solution)/shard_map/reduce_scatter | solution.py:198
  2295.6 691.9 %reduce-scatter.24.cloned.1.call-done = f32[128,4096]{1,0:T(8,128)} async-done(((f32[2048,4096]{1,0:T(8,128)}), f32[128,4096]{1,0:T(8,128)}) %reduce-scatter.24.cloned.1.call-update) | async-done | bytes 2097168 | tf_op jit(solution)/shard_map/reduce_scatter | solution.py:199
  2987.5 692.1 %reduce-scatter.26.cloned.1.call-done = f32[128,4096]{1,0:T(8,128)} async-done(((f32[2048,4096]{1,0:T(8,128)}), f32[128,4096]{1,0:T(8,128)}) %reduce-scatter.26.cloned.1.call-update) | async-done | bytes 2097168 | tf_op jit(solution)/shard_map/reduce_scatter | solution.py:200
  (268 shorter events, 154.7 us)
Async XLA Ops:
  7.2 8.0 copy-start.28
  7.2 50.4 %copy-start = (bf16[1,256,2048]{2,1,0:T(8,128)(2,1)S(1)}, bf16[1,256,2048]{2,1,0:T(8,128)(2,1)}, u32[]{:S(2)}) copy-start(bf16[1,256,2048]{2,1,0:T(8,128)(2,1)} %param.16) | copy-start | bytes 3145732
  7.2 50.7 %copy-start.29 = (s32[1,4]{1,0:T(1,128)S(1)}, s32[1,4]{1,0:T(1,128)}, u32[]{:S(2)}) copy-start(s32[1,4]{1,0:T(1,128)} %param.18) | copy-start | bytes 52
  7.2 62.0 %all-gather.10.cloned.1.call-start = ((), (), s32[]{:S(2)}) async-start(), calls=%async_computation.9 | async-start | bytes 1114112 | tf_op jit(solution)/shard_map/all_gather | solution.py:62
  8.9 117.6 %all-gather.12.cloned.1.call-start = ((), (), s32[]{:S(2)}) async-start(), calls=%async_computation.10 | async-start | bytes 1114112 | tf_op jit(solution)/shard_map/all_gather | solution.py:61
  10.5 194.4 %all-gather.14.cloned.1.call-start = ((), (), s32[]{:S(2)}) async-start(), calls=%async_computation.11 | async-start | bytes 4456448 | tf_op jit(solution)/shard_map/all_gather | solution.py:60
  12.4 270.0 %all-gather.16.cloned.1.call-start = ((), (), s32[]{:S(2)}) async-start(), calls=%async_computation.12 | async-start | bytes 4456448 | tf_op jit(solution)/shard_map/all_gather | solution.py:63
  14.2 318.8 %all-reduce.8.cloned.1.call-start = ((), (), s32[]{:S(2)}) async-start(), calls=%async_computation.13 | async-start | bytes 2097152 | tf_op jit(solution)/shard_map/psum | solution.py:160
  57.6 153.8 %copy-start.23 = (f32[16,1,128]{2,1,0:T(1,128)}, f32[16,1,128]{2,1,0:T(1,128)S(1)}, u32[]{:S(2)}) copy-start(f32[16,1,128]{2,1,0:T(1,128)S(1)} %convert_element_type.253) | copy-start | bytes 24580
  57.9 153.5 %copy-start.25 = (f32[256]{0:T(256)}, f32[256]{0:T(256)S(1)}, u32[]{:S(2)}) copy-start(f32[256]{0:T(256)S(1)} %add_rsqrt_fusion.1) | copy-start | bytes 3076
  58.5 156.6 %copy-start.11 = (f32[256,64]{0,1:T(8,128)}, f32[256,64]{0,1:T(8,128)S(1)}, u32[]{:S(2)}) copy-start(f32[256,64]{0,1:T(8,128)S(1)} %get-tuple-element.231) | copy-start | bytes 196612
  58.5 156.6 %copy-start.16 = (f32[256,64]{0,1:T(8,128)}, f32[256,64]{0,1:T(8,128)S(1)}, u32[]{:S(2)}) copy-start(f32[256,64]{0,1:T(8,128)S(1)} %get-tuple-element.232) | copy-start | bytes 196612
  232.2 54.8 %copy-start.6 = (bf16[4,1024,64]{1,2,0:T(8,128)(2,1)}, bf16[4,1024,64]{1,2,0:T(8,128)(2,1)S(1)}, u32[]{:S(2)}) copy-start(bf16[4,1024,64]{1,2,0:T(8,128)(2,1)S(1)} %get-tuple-element.520) | copy-start | bytes 1572868
  232.2 54.8 %copy-start.7 = (bf16[4,256,4,64]{1,3,2,0:T(8,128)(2,1)}, bf16[4,256,4,64]{1,3,2,0:T(8,128)(2,1)S(1)}, u32[]{:S(2)}) copy-start(bf16[4,256,4,64]{1,3,2,0:T(8,128)(2,1)S(1)} %get-tuple-element.521) | copy-start | bytes 1572868
  232.2 54.8 %copy-start.9 = (bf16[4,1024,64]{1,2,0:T(8,128)(2,1)}, bf16[4,1024,64]{1,2,0:T(8,128)(2,1)S(1)}, u32[]{:S(2)}) copy-start(bf16[4,1024,64]{1,2,0:T(8,128)(2,1)S(1)} %get-tuple-element.534) | copy-start | bytes 1572868
  287.0 213.6 %all-gather.18.cloned.1.call-start = ((), (), s32[]{:S(2)}) async-start(), calls=%async_computation.14 | async-start | bytes 17825792 | tf_op jit(solution)/shard_map/all_gather | solution.py:70
  289.9 403.3 %all-gather.20.cloned.1.call-start = ((), (), s32[]{:S(2)}) async-start(), calls=%async_computation.15 | async-start | bytes 17825792 | tf_op jit(solution)/shard_map/all_gather | solution.py:71
  291.1 594.6 %all-gather.22.cloned.1.call-start = ((), (), s32[]{:S(2)}) async-start(), calls=%async_computation.16 | async-start | bytes 17825792 | tf_op jit(solution)/shard_map/all_gather | solution.py:72
  294.0 650.7 %all-reduce.10.cloned.1.call-start = ((), (), s32[]{:S(2)}) async-start(), calls=%async_computation.17 | async-start | bytes 2097152 | tf_op jit(solution)/shard_map/psum | solution.py:193
  335.3 165.3 %copy-start.4 = (bf16[256,2048]{1,0:T(8,128)(2,1)}, bf16[256,2048]{1,0:T(8,128)(2,1)S(1)}, u32[]{:S(2)}) copy-start(bf16[256,2048]{1,0:T(8,128)(2,1)S(1)} %multiply_convert_fusion.4) | copy-start | bytes 3145732
  510.8 375.0 %copy-start.2 = (bf16[1,256,2048]{2,1,0:T(8,128)(2,1)S(1)}, bf16[1,256,2048]{2,1,0:T(8,128)(2,1)}, u32[]{:S(2)}) copy-start(bf16[1,256,2048]{2,1,0:T(8,128)(2,1)} %param.17) | copy-start | bytes 3145732
  926.9 100.2 %reduce-scatter.10.cloned.1.call-start = ((), (), s32[]{:S(2)}) async-start(), calls=%async_computation.18 | async-start | bytes 655360 | tf_op jit(solution)/shard_map/reduce_scatter | solution.py:241
  1000.7 54.4 %reduce-scatter.12.cloned.1.call-start = ((), (), s32[]{:S(2)}) async-start(), calls=%async_computation.19 | async-start | bytes 655360 | tf_op jit(solution)/shard_map/reduce_scatter | solution.py:244
  1000.7 11.9 copy-start.17
  1016.4 112.5 %all-reduce.12.cloned.1.call-start = ((), (), s32[]{:S(2)}) async-start(), calls=%async_computation.27 | async-start | bytes 4194304 | tf_op jit(solution)/shard_map/psum | solution.py:173
  1058.6 154.2 %reduce-scatter.16.cloned.1.call-start = ((), (), s32[]{:S(2)}) async-start(), calls=%async_computation.21 | async-start | bytes 2228224 | tf_op jit(solution)/shard_map/reduce_scatter | solution.py:282
  1061.2 185.2 %reduce-scatter.18.cloned.1.call-start = ((), (), s32[]{:S(2)}) async-start(), calls=%async_computation.22 | async-start | bytes 2228224 | tf_op jit(solution)/shard_map/reduce_scatter | solution.py:283
  1063.2 360.6 %reduce-scatter.14.cloned.1.call-start = ((), (), s32[]{:S(2)}) async-start(), calls=%async_computation.20 | async-start | bytes 8912896 | tf_op jit(solution)/shard_map/reduce_scatter | solution.py:281
  1069.0 537.8 %reduce-scatter.20.cloned.1.call-start = ((), (), s32[]{:S(2)}) async-start(), calls=%async_computation.23 | async-start | bytes 8912896 | tf_op jit(solution)/shard_map/reduce_scatter | solution.py:284
  1075.9 1219.7 %reduce-scatter.22.cloned.1.call-start = ((), (), s32[]{:S(2)}) async-start(), calls=%async_computation.24 | async-start | bytes 35651584 | tf_op jit(solution)/shard_map/reduce_scatter | solution.py:198
  1094.0 1893.5 %reduce-scatter.24.cloned.1.call-start = ((), (), s32[]{:S(2)}) async-start(), calls=%async_computation.25 | async-start | bytes 35651584 | tf_op jit(solution)/shard_map/reduce_scatter | solution.py:199
  1112.0 2567.5 %reduce-scatter.26.cloned.1.call-start = ((), (), s32[]{:S(2)}) async-start(), calls=%async_computation.26 | async-start | bytes 35651584 | tf_op jit(solution)/shard_map/reduce_scatter | solution.py:200
  (40 other events, 72.6 us)
Sparse Core Ops, SparseCore 0:
  11.3 57.8 all-gather.9
  72.5 53.9 all-gather.11
  129.8 75.0 all-gather.13
  208.1 74.1 all-gather.15
  287.1 18.0 all-reduce.7
  308.4 192.1 all-gather.17
  504.0 189.1 all-gather.19
  696.5 189.1 all-gather.21
  927.0 17.6 all-reduce.9
  1000.8 26.2 reduce-scatter.9
  1029.9 25.0 reduce-scatter.11
  1058.7 21.3 all-reduce.11
  1082.9 82.7 reduce-scatter.15
  1168.4 77.9 reduce-scatter.17
  1249.1 174.5 reduce-scatter.13
  1426.5 180.2 reduce-scatter.19
  1609.6 685.9 reduce-scatter.21
  2298.3 689.0 reduce-scatter.23
  2990.4 689.0 reduce-scatter.25
where the time goes:
time: 3700 us; the launch traced here: 3690 us
  waiting for transfers between devices  3210 us (87%)
  matrix products  216 us (6%)
  blocking collectives  182 us (5%)
  other arithmetic  44 us (1%)
    reduce_scatter x1, waiting for transfers between devices, on_device(): lax.psum_scatter(down_term, ('fsdp', 'context'), scatter_dimension=0, til...  692 us
    reduce_scatter x1, waiting for transfers between devices, on_device(): lax.psum_scatter(up_term, ('fsdp', 'context'), scatter_dimension=0, tiled...  692 us
    reduce_scatter x1, waiting for transfers between devices, on_device(): lax.psum_scatter(gate_term, ('fsdp', 'context'), scatter_dimension=0, til...  689 us
    reduce_scatter x1, waiting for transfers between devices, on_device(): lax.psum_scatter(out_term, ('fsdp', 'context'), scatter_dimension=0, tile...  183 us
    all_gather x1, waiting for transfers between devices, feed_shards(): lax.all_gather(up_weight.astype(jnp.bfloat16), ('fsdp', 'context'), axis=...  182 us
    all_gather x1, waiting for transfers between devices, feed_shards(): lax.all_gather(down_weight.astype(jnp.bfloat16), ('fsdp', 'context'), axi...  180 us
    reduce_scatter x1, waiting for transfers between devices, on_device(): lax.psum_scatter(query_term, ('fsdp', 'context'), scatter_dimension=0, ti...  177 us
    all_gather x1, waiting for transfers between devices, feed_shards(): lax.all_gather(gate_weight.astype(jnp.bfloat16), ('fsdp', 'context'), axi...  165 us
  transfers between devices with their start and end apart: 19, of which 16 were waited for; matrix products, arithmetic and copies ran while one was open for 5% of the time, Pallas kernels for 0%

commit v1 on v0

--- a/solution.py
+++ b/solution.py
@@ -4,6 +4,7 @@
 from jax.sharding import PartitionSpec as P
 
 HEAD = 64
+FSDP, CONTEXT, TENSOR = "fsdp", "context", "tensor"
 
 
 norm_eps = 1e-05
@@ -52,24 +53,32 @@
     return inverse * (scaled - unit * jnp.mean(scaled * unit, axis=-1, keepdims=True))
 
 
+def dot_first(left, right):
+    return lax.dot_general(left, right, (((0,), (0,)), ((), ())), preferred_element_type=jnp.float32)
+
+
+def dot_last(left, right):
+    return lax.dot_general(left, right, (((1,), (1,)), ((), ())), preferred_element_type=jnp.float32)
+
+
 def attention_shards(attention_gain, query_weight, key_weight, value_weight, output_weight):
     return (
         lax.all_gather(
-            attention_gain.astype(jnp.bfloat16), ("fsdp", "context"), axis=0, tiled=True
+            attention_gain.astype(jnp.bfloat16), (FSDP, CONTEXT), axis=0, tiled=True
         ),
-        lax.all_gather(query_weight.astype(jnp.bfloat16), ("fsdp", "context"), axis=0, tiled=True),
-        lax.all_gather(key_weight.astype(jnp.bfloat16), ("fsdp", "context"), axis=0, tiled=True),
-        lax.all_gather(value_weight.astype(jnp.bfloat16), ("fsdp", "context"), axis=0, tiled=True),
-        lax.all_gather(output_weight.astype(jnp.bfloat16), ("fsdp", "context"), axis=0, tiled=True),
+        lax.all_gather(query_weight.astype(jnp.bfloat16), (FSDP, CONTEXT), axis=0, tiled=True),
+        lax.all_gather(key_weight.astype(jnp.bfloat16), (FSDP, CONTEXT), axis=0, tiled=True),
+        lax.all_gather(value_weight.astype(jnp.bfloat16), (FSDP, CONTEXT), axis=0, tiled=True),
+        lax.all_gather(output_weight.astype(jnp.bfloat16), (FSDP, CONTEXT), axis=0, tiled=True),
     )
 
 
 def feed_shards(feed_gain, gate_weight, up_weight, down_weight):
     return (
-        lax.all_gather(feed_gain.astype(jnp.bfloat16), ("fsdp", "context"), axis=0, tiled=True),
-        lax.all_gather(gate_weight.astype(jnp.bfloat16), ("fsdp", "context"), axis=0, tiled=True),
-        lax.all_gather(up_weight.astype(jnp.bfloat16), ("fsdp", "context"), axis=0, tiled=True),
-        lax.all_gather(down_weight.astype(jnp.bfloat16), ("fsdp", "context"), axis=0, tiled=True),
+        lax.all_gather(feed_gain.astype(jnp.bfloat16), (FSDP, CONTEXT), axis=0, tiled=True),
+        lax.all_gather(gate_weight.astype(jnp.bfloat16), (FSDP, CONTEXT), axis=0, tiled=True),
+        lax.all_gather(up_weight.astype(jnp.bfloat16), (FSDP, CONTEXT), axis=0, tiled=True),
+        lax.all_gather(down_weight.astype(jnp.bfloat16), (FSDP, CONTEXT), axis=0, tiled=True),
     )
 
 
@@ -88,8 +97,8 @@
     down_weight,
 ):
     local_rows = tokens.shape[1]
-    group_rows = local_rows * lax.axis_size("context")
-    first_row = lax.axis_index("context") * local_rows
+    group_rows = local_rows * lax.axis_size(CONTEXT)
+    first_row = lax.axis_index(CONTEXT) * local_rows
     segment, position, valid_rows = slot_layout(lengths[0], group_rows)
     local_segment = lax.dynamic_slice_in_dim(segment, first_row, local_rows)
     local_position = lax.dynamic_slice_in_dim(position, first_row, local_rows)
@@ -124,9 +133,9 @@
     )
     keys_all, values_all = (
         lax.all_gather(
-            keys_rot.reshape(local_rows, kv_local * HEAD), "context", axis=0, tiled=True
+            keys_rot.reshape(local_rows, kv_local * HEAD), CONTEXT, axis=0, tiled=True
         ),
-        lax.all_gather(values_low, "context", axis=0, tiled=True),
+        lax.all_gather(values_low, CONTEXT, axis=0, tiled=True),
     )
     query_heads = queries_rot.reshape(local_rows, kv_local, per_group, HEAD).transpose(1, 0, 2, 3)
     key_heads = keys_all.reshape(group_rows, kv_local, HEAD).transpose(1, 0, 2)
@@ -156,8 +165,8 @@
         .reshape(local_rows, heads_local * HEAD)
         .astype(jnp.bfloat16)
     )
-    attn_part = jnp.einsum("tq,dq->td", attended, attn_set[4], preferred_element_type=jnp.float32)
-    attn_out = lax.psum(attn_part.astype(jnp.bfloat16), "tensor").astype(jnp.float32)
+    attn_part = dot_last(attended, attn_set[4])
+    attn_out = lax.psum(attn_part.astype(jnp.bfloat16), TENSOR).astype(jnp.float32)
     hidden_state = inputs + residual_mult * attn_out
     feed_set = feed_shards(feed_gain, gate_weight, up_weight, down_weight)
     gain_two = feed_set[0].astype(jnp.float32)
@@ -169,41 +178,37 @@
     gate_out = jnp.dot(normed_two, feed_set[1], preferred_element_type=jnp.float32)
     up_out = jnp.dot(normed_two, feed_set[2], preferred_element_type=jnp.float32)
     inner_act = (jax.nn.silu(gate_out) * up_out).astype(jnp.bfloat16)
-    feed_part = jnp.einsum("tf,df->td", inner_act, feed_set[3], preferred_element_type=jnp.float32)
-    feed_out = lax.psum(feed_part.astype(jnp.bfloat16), "tensor").astype(jnp.float32)
+    feed_part = dot_last(inner_act, feed_set[3])
+    feed_out = lax.psum(feed_part.astype(jnp.bfloat16), TENSOR).astype(jnp.float32)
     output = hidden_state + residual_mult * feed_out
     cotangent = out_grad[0].astype(jnp.float32) * local_valid[:, None].astype(jnp.float32)
     feed_back = feed_shards(feed_gain, gate_weight, up_weight, down_weight)
     feed_grad = (residual_mult * cotangent).astype(jnp.bfloat16)
-    down_term = jnp.einsum("td,tf->df", feed_grad, inner_act, preferred_element_type=jnp.float32)
+    down_term = dot_first(feed_grad, inner_act)
     inner_grad = jnp.dot(feed_grad, feed_back[3], preferred_element_type=jnp.float32)
     sigmoid_gate = jax.nn.sigmoid(gate_out)
     gate_grad = (
         inner_grad * up_out * sigmoid_gate * (1.0 + gate_out * (1.0 - sigmoid_gate))
     ).astype(jnp.bfloat16)
     up_grad = (inner_grad * jax.nn.silu(gate_out)).astype(jnp.bfloat16)
-    gate_term = jnp.einsum("td,tf->df", normed_two, gate_grad, preferred_element_type=jnp.float32)
-    up_term = jnp.einsum("td,tf->df", normed_two, up_grad, preferred_element_type=jnp.float32)
-    normed_part_two = jnp.einsum(
-        "tf,df->td", gate_grad, feed_back[1], preferred_element_type=jnp.float32
-    )
-    normed_part_two = normed_part_two + jnp.einsum(
-        "tf,df->td", up_grad, feed_back[2], preferred_element_type=jnp.float32
-    )
-    normed_grad_two = lax.psum(normed_part_two.astype(jnp.bfloat16), "tensor").astype(jnp.float32)
+    gate_term = dot_first(normed_two, gate_grad)
+    up_term = dot_first(normed_two, up_grad)
+    normed_part_two = dot_last(gate_grad, feed_back[1])
+    normed_part_two = normed_part_two + dot_last(up_grad, feed_back[2])
+    normed_grad_two = lax.psum(normed_part_two.astype(jnp.bfloat16), TENSOR).astype(jnp.float32)
     feed_gain_term = jnp.sum(normed_grad_two * unit_two, axis=0)
     hidden_grad = cotangent + norm_back(normed_grad_two, unit_two, gain_two, inverse_two)
     feed_sums = (
-        lax.psum_scatter(feed_gain_term, ("fsdp", "context"), scatter_dimension=0, tiled=True),
-        lax.psum_scatter(gate_term, ("fsdp", "context"), scatter_dimension=0, tiled=True),
-        lax.psum_scatter(up_term, ("fsdp", "context"), scatter_dimension=0, tiled=True),
-        lax.psum_scatter(down_term, ("fsdp", "context"), scatter_dimension=0, tiled=True),
+        lax.psum_scatter(feed_gain_term, (FSDP, CONTEXT), scatter_dimension=0, tiled=True),
+        lax.psum_scatter(gate_term, (FSDP, CONTEXT), scatter_dimension=0, tiled=True),
+        lax.psum_scatter(up_term, (FSDP, CONTEXT), scatter_dimension=0, tiled=True),
+        lax.psum_scatter(down_term, (FSDP, CONTEXT), scatter_dimension=0, tiled=True),
     )
     attn_back = attention_shards(
         attention_gain, query_weight, key_weight, value_weight, output_weight
     )
     attn_grad = (residual_mult * hidden_grad).astype(jnp.bfloat16)
-    out_term = jnp.einsum("td,tq->dq", attn_grad, attended, preferred_element_type=jnp.float32)
+    out_term = dot_first(attn_grad, attended)
     mixed_grad = jnp.dot(attn_grad, attn_back[4], preferred_element_type=jnp.float32).astype(
         jnp.bfloat16
     )
@@ -239,10 +244,10 @@
     value_grads = value_grads.transpose(1, 0, 2).reshape(group_rows, kv_local * HEAD)
     local_key_grad, local_value_grad = (
         lax.psum_scatter(
-            key_grads.astype(jnp.bfloat16), "context", scatter_dimension=0, tiled=True
+            key_grads.astype(jnp.bfloat16), CONTEXT, scatter_dimension=0, tiled=True
         ).astype(jnp.float32),
         lax.psum_scatter(
-            value_grads.astype(jnp.bfloat16), "context", scatter_dimension=0, tiled=True
+            value_grads.astype(jnp.bfloat16), CONTEXT, scatter_dimension=0, tiled=True
         ).astype(jnp.float32),
     )
     query_grad_rot = query_grads.transpose(1, 0, 2, 3).reshape(local_rows, heads_local, HEAD)
@@ -257,31 +262,21 @@
         .astype(jnp.bfloat16)
     )
     value_grad_low = local_value_grad.astype(jnp.bfloat16)
-    query_term = jnp.einsum(
-        "td,tq->dq", normed_one, query_grad_low, preferred_element_type=jnp.float32
-    )
-    key_term = jnp.einsum("td,tq->dq", normed_one, key_grad_low, preferred_element_type=jnp.float32)
-    value_term = jnp.einsum(
-        "td,tq->dq", normed_one, value_grad_low, preferred_element_type=jnp.float32
-    )
-    normed_part_one = jnp.einsum(
-        "tq,dq->td", query_grad_low, attn_back[1], preferred_element_type=jnp.float32
-    )
-    normed_part_one = normed_part_one + jnp.einsum(
-        "tq,dq->td", key_grad_low, attn_back[2], preferred_element_type=jnp.float32
-    )
-    normed_part_one = normed_part_one + jnp.einsum(
-        "tq,dq->td", value_grad_low, attn_back[3], preferred_element_type=jnp.float32
-    )
-    normed_grad_one = lax.psum(normed_part_one.astype(jnp.bfloat16), "tensor").astype(jnp.float32)
+    query_term = dot_first(normed_one, query_grad_low)
+    key_term = dot_first(normed_one, key_grad_low)
+    value_term = dot_first(normed_one, value_grad_low)
+    normed_part_one = dot_last(query_grad_low, attn_back[1])
+    normed_part_one = normed_part_one + dot_last(key_grad_low, attn_back[2])
+    normed_part_one = normed_part_one + dot_last(value_grad_low, attn_back[3])
+    normed_grad_one = lax.psum(normed_part_one.astype(jnp.bfloat16), TENSOR).astype(jnp.float32)
     attn_gain_term = jnp.sum(normed_grad_one * unit_one, axis=0)
     input_grad = hidden_grad + norm_back(normed_grad_one, unit_one, gain_one, inverse_one)
     attn_sums = (
-        lax.psum_scatter(attn_gain_term, ("fsdp", "context"), scatter_dimension=0, tiled=True),
-        lax.psum_scatter(query_term, ("fsdp", "context"), scatter_dimension=0, tiled=True),
-        lax.psum_scatter(key_term, ("fsdp", "context"), scatter_dimension=0, tiled=True),
-        lax.psum_scatter(value_term, ("fsdp", "context"), scatter_dimension=0, tiled=True),
-        lax.psum_scatter(out_term, ("fsdp", "context"), scatter_dimension=0, tiled=True),
+        lax.psum_scatter(attn_gain_term, (FSDP, CONTEXT), scatter_dimension=0, tiled=True),
+        lax.psum_scatter(query_term, (FSDP, CONTEXT), scatter_dimension=0, tiled=True),
+        lax.psum_scatter(key_term, (FSDP, CONTEXT), scatter_dimension=0, tiled=True),
+        lax.psum_scatter(value_term, (FSDP, CONTEXT), scatter_dimension=0, tiled=True),
+        lax.psum_scatter(out_term, (FSDP, CONTEXT), scatter_dimension=0, tiled=True),
     )
     return (
         output.astype(jnp.bfloat16)[None],
@@ -298,36 +293,219 @@
     )
 
 
+def pick_block(x, axis_name, axis):
+    n = lax.axis_size(axis_name)
+    size = x.shape[axis] // n
+    return lax.dynamic_slice_in_dim(x, lax.axis_index(axis_name) * size, size, axis)
+
+
+def gather_tokens(x, axes):
+    return lax.all_gather(x, axes, axis=0, tiled=True)
+
+
+def scatter_tokens(x, axes):
+    return lax.psum_scatter(x, axes, scatter_dimension=0, tiled=True)
+
+
+def on_device_split(
+    tokens,
+    out_grad,
+    lengths,
+    attention_gain,
+    query_weight,
+    key_weight,
+    value_weight,
+    output_weight,
+    feed_gain,
+    gate_weight,
+    up_weight,
+    down_weight,
+):
+    f32, bf16 = jnp.float32, jnp.bfloat16
+    nz, nc, nt = (lax.axis_size(a) for a in (FSDP, CONTEXT, TENSOR))
+    local_rows, width = tokens.shape[1:]
+    group_rows = local_rows * nc
+    filled = group_rows * 3 // 4
+    part_rows = local_rows // nt
+    wrows = query_weight.shape[0]
+    kv_cols = key_weight.shape[1] // nc
+    q_cols = query_weight.shape[1] // nc
+    ff_cols = gate_weight.shape[1] // nz
+    per_group = q_cols // kv_cols
+    segment, position, valid_rows = slot_layout(lengths[0], group_rows)
+    cos_table, sine_table = rope_tables(position, HEAD)
+
+    attn_cols = jnp.concatenate(
+        [w.astype(bf16).reshape(wrows, nc, -1) for w in (query_weight, key_weight, value_weight, output_weight)],
+        axis=2,
+    ).transpose(1, 0, 2)
+    attn_cols = lax.all_to_all(attn_cols, CONTEXT, 0, 0, tiled=True)
+    attn_all = lax.all_gather(attn_cols.reshape(nc * wrows, -1), FSDP, axis=0, tiled=True)
+    w_qkv = attn_all[:, : q_cols + 2 * kv_cols]
+    w_out = attn_all[:, q_cols + 2 * kv_cols :]
+    gains = lax.all_gather(
+        jnp.stack([attention_gain, feed_gain]).astype(bf16), (FSDP, CONTEXT), axis=1, tiled=True
+    ).astype(f32)
+    gain_one, gain_two = gains[0], gains[1]
+
+    ff_part = jnp.concatenate(
+        [w.astype(bf16).reshape(wrows, nz, -1) for w in (gate_weight, up_weight, down_weight)], axis=2
+    ).transpose(1, 0, 2)
+    ff_part = lax.all_to_all(ff_part, FSDP, 0, 0, tiled=True)
+    ff_all = lax.all_gather(ff_part.reshape(nz * wrows, -1), CONTEXT, axis=0, tiled=True)
+    w_gate_up = ff_all[:, : 2 * ff_cols]
+    w_down = ff_all[:, 2 * ff_cols :]
+
+    def to_ff(x):
+        return x.reshape(-1, nz, nc, wrows).transpose(0, 2, 1, 3).reshape(x.shape)
+
+    def from_ff(x):
+        return x.reshape(-1, nc, nz, wrows).transpose(0, 2, 1, 3).reshape(x.shape)
+
+    my_tokens = pick_block(tokens[0], TENSOR, 0)
+    all_tokens = gather_tokens(my_tokens, (CONTEXT, TENSOR)).astype(f32)
+    cotangent = pick_block(out_grad[0], TENSOR, 0)
+    first_row = lax.axis_index(CONTEXT) * local_rows + lax.axis_index(TENSOR) * part_rows
+    my_valid = lax.dynamic_slice_in_dim(valid_rows, first_row, part_rows)
+    cotangent = cotangent.astype(f32) * my_valid[:, None].astype(f32)
+    feed_grad = gather_tokens(to_ff((residual_mult * cotangent).astype(bf16)), (FSDP, TENSOR))
+
+    inverse_all = lax.rsqrt(jnp.mean(all_tokens * all_tokens, axis=-1, keepdims=True) + norm_eps)
+    normed_one = (all_tokens * inverse_all * gain_one).astype(bf16)
+    qkv = jnp.dot(normed_one, w_qkv, preferred_element_type=f32)
+    queries = rotate(qkv[:, :q_cols].reshape(group_rows, per_group, HEAD), cos_table, sine_table).astype(bf16)
+    keys = rotate(qkv[:, q_cols : q_cols + kv_cols].reshape(group_rows, 1, HEAD), cos_table, sine_table).astype(bf16)[:, 0]
+    values = qkv[:, q_cols + kv_cols :].astype(bf16)
+    slot_ids = jnp.arange(filled, dtype=jnp.int32)
+    allowed = (segment[:filled, None] == segment[None, :filled]) & (slot_ids[:, None] >= slot_ids[None, :])
+    q_f, k_f, v_f = queries[:filled], keys[:filled], values[:filled]
+    scores = jnp.einsum("tgd,sd->gts", q_f, k_f, preferred_element_type=f32)
+    scores = jnp.where(allowed[None], scores * attention_mult, -1e30)
+    highest = jnp.max(scores, axis=-1, keepdims=True)
+    weight = jnp.exp(scores - highest)
+    totals = jnp.sum(weight, axis=-1, keepdims=True)
+    probabilities = weight / totals
+    prob_low = probabilities.astype(bf16)
+    mixed = jnp.einsum("gts,sd->tgd", prob_low, v_f, preferred_element_type=f32).astype(bf16)
+    attended_f = mixed.reshape(filled, q_cols)
+    attended = jnp.concatenate([attended_f, jnp.tile(values[filled:], (1, per_group))], axis=0)
+    attn_part = dot_last(attended, w_out)
+    attn_out = scatter_tokens(attn_part.astype(bf16), (CONTEXT, TENSOR)).astype(f32)
+    my_inputs = my_tokens.astype(f32)
+    hidden = my_inputs + residual_mult * attn_out
+    inverse_two = lax.rsqrt(jnp.mean(hidden * hidden, axis=-1, keepdims=True) + norm_eps)
+    unit_two = hidden * inverse_two
+    normed_two = gather_tokens(to_ff((unit_two * gain_two).astype(bf16)), (FSDP, TENSOR))
+    gate_up = jnp.dot(normed_two, w_gate_up, preferred_element_type=f32)
+    gate_out, up_out = gate_up[:, :ff_cols], gate_up[:, ff_cols:]
+    sig = jax.nn.sigmoid(gate_out)
+    inner = (gate_out * sig * up_out).astype(bf16)
+    feed_part = dot_last(inner, w_down)
+    feed_out = from_ff(scatter_tokens(feed_part.astype(bf16), (FSDP, TENSOR)).astype(f32))
+    output = (hidden + residual_mult * feed_out).astype(bf16)
+    output = lax.all_gather(output, TENSOR, axis=0, tiled=True)
+
+    inner_grad = jnp.dot(feed_grad, w_down, preferred_element_type=f32)
+    gate_grad = (inner_grad * up_out * sig * (1.0 + gate_out * (1.0 - sig))).astype(bf16)
+    up_grad = (inner_grad * gate_out * sig).astype(bf16)
+    both_grad = jnp.concatenate([gate_grad, up_grad], axis=1)
+    normed_part = dot_last(both_grad, w_gate_up)
+    normed_grad_two = from_ff(scatter_tokens(normed_part.astype(bf16), (FSDP, TENSOR)).astype(f32))
+    feed_gain_term = jnp.sum(normed_grad_two * unit_two, axis=0)
+    hidden_grad = cotangent + norm_back(normed_grad_two, unit_two, gain_two, inverse_two)
+    down_term = dot_first(feed_grad, inner).astype(bf16)
+    gate_term = dot_first(normed_two, gate_grad).astype(bf16)
+    up_term = dot_first(normed_two, up_grad).astype(bf16)
+    ff_terms = jnp.concatenate(
+        [
+            lax.psum_scatter(t, CONTEXT, scatter_dimension=0, tiled=True).reshape(nz, wrows, -1)
+            for t in (gate_term, up_term, down_term)
+        ],
+        axis=2,
+    )
+    ff_terms = lax.all_to_all(ff_terms, FSDP, 0, 0, tiled=True).astype(f32)
+
+    def ff_out(i):
+        return ff_terms[:, :, i * ff_cols : (i + 1) * ff_cols].transpose(1, 0, 2).reshape(wrows, -1)
+
+    attn_grad = gather_tokens((residual_mult * hidden_grad).astype(bf16), (CONTEXT, TENSOR))[:filled]
+    out_term = dot_first(attn_grad, attended_f)
+    mixed_grad = jnp.dot(attn_grad, w_out, preferred_element_type=f32).astype(bf16).reshape(filled, per_group, HEAD)
+    prob_grad = jnp.einsum("tgd,sd->gts", mixed_grad, v_f, preferred_element_type=f32)
+    row_dot = jnp.sum(probabilities * prob_grad, axis=-1, keepdims=True)
+    score_grad = (attention_mult * probabilities * (prob_grad - row_dot)).astype(bf16)
+    query_grad = jnp.einsum("gts,sd->tgd", score_grad, k_f, preferred_element_type=f32)
+    key_grad = jnp.einsum("gts,tgd->sd", score_grad, q_f, preferred_element_type=f32)
+    value_grad = jnp.einsum("gts,tgd->sd", prob_low, mixed_grad, preferred_element_type=f32).astype(bf16)
+    cos_f, sine_f = cos_table[:filled], sine_table[:filled]
+    query_grad = rotate_back(query_grad, cos_f, sine_f).reshape(filled, q_cols).astype(bf16)
+    key_grad = rotate_back(key_grad[:, None], cos_f, sine_f)[:, 0].astype(bf16)
+    qkv_grad = jnp.concatenate([query_grad, key_grad, value_grad], axis=1)
+    qkv_term = dot_first(normed_one[:filled], qkv_grad)
+    attn_terms = jnp.concatenate([qkv_term, out_term], axis=1).astype(bf16)
+    attn_terms = lax.psum_scatter(attn_terms, FSDP, scatter_dimension=0, tiled=True)
+    attn_terms = lax.all_to_all(attn_terms.reshape(nc, wrows, -1), CONTEXT, 0, 0, tiled=True).astype(f32)
+
+    def attn_out_cols(first, size):
+        return attn_terms[:, :, first : first + size].transpose(1, 0, 2).reshape(wrows, -1)
+
+    normed_part = dot_last(qkv_grad, w_qkv).astype(bf16)
+    normed_part = jnp.pad(normed_part, ((0, group_rows - filled), (0, 0)))
+    normed_grad_one = scatter_tokens(normed_part, (CONTEXT, TENSOR)).astype(f32)
+    inverse_one = lax.rsqrt(jnp.mean(my_inputs * my_inputs, axis=-1, keepdims=True) + norm_eps)
+    unit_one = my_inputs * inverse_one
+    attn_gain_term = jnp.sum(normed_grad_one * unit_one, axis=0)
+    input_grad = hidden_grad + norm_back(normed_grad_one, unit_one, gain_one, inverse_one)
+    input_grad = lax.all_gather(input_grad.astype(bf16), TENSOR, axis=0, tiled=True)
+    gain_terms = lax.psum(jnp.stack([attn_gain_term, feed_gain_term]), (FSDP, CONTEXT, TENSOR))
+    gain_terms = pick_block(gain_terms, (FSDP, CONTEXT), 1)
+    return (
+        output[None],
+        input_grad[None],
+        gain_terms[0],
+        attn_out_cols(0, q_cols),
+        attn_out_cols(q_cols, kv_cols),
+        attn_out_cols(q_cols + kv_cols, kv_cols),
+        attn_out_cols(q_cols + 2 * kv_cols, q_cols),
+        gain_terms[1],
+        ff_out(0),
+        ff_out(1),
+        ff_out(2),
+    )
+
+
 def solution(mesh):
+    kv_heads_local = 8 // mesh.shape[TENSOR]
+    split = kv_heads_local == mesh.shape[CONTEXT]
     return jax.shard_map(
-        on_device,
+        on_device_split if split else on_device,
         mesh=mesh,
         in_specs=(
-            P("fsdp", "context", None),
-            P("fsdp", "context", None),
-            P("fsdp", None),
-            P(("fsdp", "context")),
-            P(("fsdp", "context"), "tensor"),
-            P(("fsdp", "context"), "tensor"),
-            P(("fsdp", "context"), "tensor"),
-            P(("fsdp", "context"), "tensor"),
-            P(("fsdp", "context")),
-            P(("fsdp", "context"), "tensor"),
-            P(("fsdp", "context"), "tensor"),
-            P(("fsdp", "context"), "tensor"),
+            P(FSDP, CONTEXT, None),
+            P(FSDP, CONTEXT, None),
+            P(FSDP, None),
+            P((FSDP, CONTEXT)),
+            P((FSDP, CONTEXT), TENSOR),
+            P((FSDP, CONTEXT), TENSOR),
+            P((FSDP, CONTEXT), TENSOR),
+            P((FSDP, CONTEXT), TENSOR),
+            P((FSDP, CONTEXT)),
+            P((FSDP, CONTEXT), TENSOR),
+            P((FSDP, CONTEXT), TENSOR),
+            P((FSDP, CONTEXT), TENSOR),
         ),
         out_specs=(
-            P("fsdp", "context", None),
-            P("fsdp", "context", None),
-            P(("fsdp", "context")),
-            P(("fsdp", "context"), "tensor"),
-            P(("fsdp", "context"), "tensor"),
-            P(("fsdp", "context"), "tensor"),
-            P(("fsdp", "context"), "tensor"),
-            P(("fsdp", "context")),
-            P(("fsdp", "context"), "tensor"),
-            P(("fsdp", "context"), "tensor"),
-            P(("fsdp", "context"), "tensor"),
+            P(FSDP, CONTEXT, None),
+            P(FSDP, CONTEXT, None),
+            P((FSDP, CONTEXT)),
+            P((FSDP, CONTEXT), TENSOR),
+            P((FSDP, CONTEXT), TENSOR),
+            P((FSDP, CONTEXT), TENSOR),
+            P((FSDP, CONTEXT), TENSOR),
+            P((FSDP, CONTEXT)),
+            P((FSDP, CONTEXT), TENSOR),
+            P((FSDP, CONTEXT), TENSOR),
+            P((FSDP, CONTEXT), TENSOR),
         ),
         check_vma=False,
     )

time: 3700 us -> 1050 us (0.28)
  waiting for transfers between devices: 3210 us -> 595 us
  matrix products: 216 us -> 124 us
    reduce_scatter x9 -> x8, waiting for transfers between devices: 2490 us -> 294 us  [the longest x4 170 us: scatter_tokens(): return lax.psum_scatter(x, axes, scatter_dimension=0, tiled=True)]
    all_gather x7 -> x8, waiting for transfers between devices: 694 us -> 190 us  [the longest x1 119 us: on_device_split(): lax.all_gather(ff_part.reshape(nz * wrows, -1), CONTEXT, axis=0, tiled=True)]
    all_to_all x0 -> x2, blocking collectives: none -> 125 us  [the longest x1 105 us: on_device_split(): ff_part = lax.all_to_all(ff_part, FSDP, 0, 0, tiled=True)]
    all_to_all x0 -> x2, waiting for transfers between devices: none -> 110 us  [the longest x1 110 us: on_device_split(): ff_terms = lax.all_to_all(ff_terms, FSDP, 0, 0, tiled=True).astype(f32)]
    dot_general x49 -> x18, matrix products: 216 us -> 118 us  [the longest x5 31.3 us: dot_first(): lax.dot_general(left, right, (((0,), (0,)), ((), ())), preferred_element_...]
    unnamed x1 -> x0, blocking collectives: 76.1 us -> none
    all_gather x4 -> x1, blocking collectives: 105 us -> 40 us  [on_device_split(): lax.all_gather(jnp.stack([attention_gain, feed_gain]).astype(bf16), (FSDP...]
    psum x0 -> x1, blocking collectives: none -> 39.4 us  [on_device_split(): lax.psum(jnp.stack([attn_gain_term, feed_gain_term]), (FSDP, CONTEXT, TEN...]
  transfers between devices with their start and end apart: 19 -> 18, of which waited for: 16 -> 13; matrix products, arithmetic and copies ran while one was open for 5% -> 14% of each run, Pallas kernels for 0% -> 0%
where the time goes in v1:
time: 1050 us; the launch traced here: 1040 us
  waiting for transfers between devices  595 us (57%)
  blocking collectives  205 us (20%)
  matrix products  124 us (12%)
  local copies, waits for them, and re-layouts  50.3 us (5%)
  other arithmetic  40.7 us (4%)
  between operations  15.2 us (1%)
    reduce_scatter x4, waiting for transfers between devices, scatter_tokens(): return lax.psum_scatter(x, axes, scatter_dimension=0, tiled=True)  170 us
    reduce_scatter x3, waiting for transfers between devices, on_device_split(): lax.psum_scatter(t, CONTEXT, scatter_dimension=0, tiled=True)  124 us
    all_gather x1, waiting for transfers between devices, on_device_split(): lax.all_gather(ff_part.reshape(nz * wrows, -1), CONTEXT, axis=0, tiled=True)  119 us
    all_to_all x1, waiting for transfers between devices, on_device_split(): ff_terms = lax.all_to_all(ff_terms, FSDP, 0, 0, tiled=True).astype(f32)  110 us
    all_to_all x1, blocking collectives, on_device_split(): ff_part = lax.all_to_all(ff_part, FSDP, 0, 0, tiled=True)  105 us
    all_gather x4, waiting for transfers between devices, gather_tokens(): return lax.all_gather(x, axes, axis=0, tiled=True)  40 us
    all_gather x1, blocking collectives, on_device_split(): lax.all_gather(jnp.stack([attention_gain, feed_gain]).astype(bf16), (FSDP...  40 us
    psum x1, blocking collectives, on_device_split(): lax.psum(jnp.stack([attn_gain_term, feed_gain_term]), (FSDP, CONTEXT, TEN...  39.4 us
  transfers between devices with their start and end apart: 18, of which 13 were waited for; matrix products, arithmetic and copies ran while one was open for 14% of the time, Pallas kernels for 0%

profile of v1, /device:TPU:0, one launch (start us, length us, event | category | flops | bytes accessed | tf_op | source)
XLA Modules:
  0.0 1039.1 jit_solution(12940486437680197399)
XLA Ops:
  13.8 20.3 %all_to_all.20 = bf16[4,128,640]{1,2,0:T(8,128)(2,1)S(1)} all-to-all(bf16[4,128,640]{1,2,0:T(8,128)(2,1)S(1)} %maximum_bitcast_fusion.1), channel_id=1, replica_groups=mesh['fsdp'=4,'context'=4,'tensor'=2] {'context'}, dimensions={0} | all-to-all | bytes 1310720 | tf_op jit(solution)/shard_map/all_to_all | solution.py:342
  35.6 40.0 %all_gather.28 = bf16[2,2048]{1,0:T(2,128)(2,1)S(1)} all-gather(bf16[2,128]{1,0:T(2,128)(2,1)S(1)} %pad_maximum_fusion.9), channel_id=1, replica_groups=mesh['fsdp'=4,'context'=4,'tensor'=2] {'fsdp','context'}, dimensions={1}, use_global_device_ids=true | all-gather | bytes 8704 | tf_op jit(solution)/shard_map/all_gather | solution.py:346
  83.6 27.9 %all-gather.10.cloned.1.call-done = bf16[2048,640]{1,0:T(8,128)(2,1)} async-done(((bf16[512,640]{1,0:T(8,128)(2,1)}), bf16[2048,640]{1,0:T(8,128)(2,1)}) %all-gather.10.cloned.1.call-update) | async-done | bytes 2621456 | tf_op jit(solution)/shard_map/all_gather | solution.py:343
  111.5 4.5 fusion.104
  117.1 5.8 fusion.105
  123.0 4.6 fusion.51
  127.6 4.6 convolution_convert_fusion
  132.3 50.0 %reduce-scatter.9.cloned.1.call-done = bf16[128,2048]{1,0:T(8,128)(2,1)} async-done(((bf16[1024,2048]{1,0:T(8,128)(2,1)}), bf16[128,2048]{1,0:T(8,128)(2,1)}) %reduce-scatter.9.cloned.1.call-update) | async-done | bytes 524304 | tf_op jit(solution)/shard_map/reduce_scatter | solution.py:307
  194.5 105.1 %all_to_all.21 = bf16[4,128,3072]{1,2,0:T(8,128)(2,1)} all-to-all(bf16[4,128,3072]{1,2,0:T(8,128)(2,1)S(1)} %maximum_bitcast_fusion), channel_id=1, replica_groups=mesh['fsdp'=4,'context'=4,'tensor'=2] {'fsdp'}, dimensions={0} | all-to-all | bytes 6291456 | tf_op jit(solution)/shard_map/all_to_all | solution.py:354
  299.6 4.7 copy.97
  306.8 118.8 %all-gather.14.cloned.1.call-done = bf16[2048,3072]{1,0:T(8,128)(2,1)} async-done(((bf16[512,3072]{1,0:T(8,128)(2,1)}), bf16[2048,3072]{1,0:T(8,128)(2,1)}) %all-gather.14.cloned.1.call-update) | async-done | bytes 12582928 | tf_op jit(solution)/shard_map/all_gather | solution.py:355
  425.6 14.8 %fusion.9 = f32[1024,2048]{1,0:T(8,128)} fusion(bf16[1024,2048]{0,1:T(8,128)(2,1)} %all-gather.12.cloned.1.call-done, bf16[2048,3072]{1,0:T(8,128)(2,1)} %all-gather.14.cloned.1.call-done), kind=kOutput, calls=%fused_computation.15 | convolution fusion | flops 8589934592 | bytes 20971520 | tf_op jit(solution)/shard_map/dot_general | solution.py:399
  440.3 35.1 %all-gather.18.cloned.1.call-done = bf16[1024,2048]{0,1:T(8,128)(2,1)} async-done(((bf16[128,2048]{0,1:T(8,128)(2,1)}), bf16[1024,2048]{0,1:T(8,128)(2,1)}) %all-gather.18.cloned.1.call-update) | async-done | bytes 4194320 | tf_op jit(solution)/shard_map/all_gather | solution.py:303
  475.4 13.6 %multiply_convert_fusion.1 = (bf16[1024,1024]{1,0:T(8,128)(2,1)S(1)}, bf16[1024,1024]{1,0:T(8,128)(2,1)}, bf16[1024,1024]{1,0:T(8,128)(2,1)S(1)}) fusion(f32[1024,2048]{1,0:T(8,128)} %fusion.9, bf16[1024,2048]{0,1:T(8,128)(2,1)} %all-gather.18.cloned.1.call-done, bf16[2048,3072]{1,0:T(8,128)(2,1)} %all-gather.14.cloned.1.call-done), kind=kOutput, calls=%fused_computation.26 | convolution fusion | flops 4311744512 | bytes 23068672 | tf_op jit(solution)/shard_map/dot_general | solution.py:408
  490.4 8.6 convolution_convert_fusion.4
  499.1 13.4 %fusion.18 = bf16[1024,2048]{1,0:T(8,128)(2,1)} fusion(bf16[2048,3072]{1,0:T(8,128)(2,1)} %all-gather.14.cloned.1.call-done, bf16[1024,1024]{1,0:T(8,128)(2,1)} %get-tuple-element.54, bf16[1024,1024]{1,0:T(8,128)(2,1)S(1)} %get-tuple-element.53), kind=kOutput, calls=%fused_computation.29 | convolution fusion | flops 8600420352 | bytes 16777216 | tf_op jit(solution)/shard_map/dot_general | solution.py:61
  512.6 34.8 %reduce-scatter.11.cloned.1.call-done = bf16[128,2048]{1,0:T(8,128)(2,1)} async-done(((bf16[1024,2048]{1,0:T(8,128)(2,1)}), bf16[128,2048]{1,0:T(8,128)(2,1)}) %reduce-scatter.11.cloned.1.call-update) | async-done | bytes 524304 | tf_op jit(solution)/shard_map/reduce_scatter | solution.py:307
  550.9 47.1 %reduce-scatter.13.cloned.1.call-done = bf16[128,2048]{1,0:T(8,128)(2,1)} async-done(((bf16[1024,2048]{1,0:T(8,128)(2,1)}), bf16[128,2048]{1,0:T(8,128)(2,1)}) %reduce-scatter.13.cloned.1.call-update) | async-done | bytes 524304 | tf_op jit(solution)/shard_map/reduce_scatter | solution.py:307
  606.8 9.4 convolution_convert_fusion.1
  616.3 9.3 convolution_convert_fusion.2
  625.7 10.2 convolution_convert_fusion.3
  637.0 4.9 all-gather.20.cloned.1.call-done
  645.2 5.4 fusion.61
  650.6 5.4 fusion.1
  656.0 10.5 %fusion.3 = bf16[4,768,768]{1,2,0:T(8,128)(2,1)} fusion(f32[768,768,4]{1,0,2:T(8,128)} %get-tuple-element.88, f32[4,768]{1,0:T(4,128)S(1)} %get-tuple-element.87, f32[4,768,768]{1,2,0:T(8,128)} %get-tuple-element.86, f32[4,768]{1,0:T(4,128)S(1)} %copy-done.23), kind=kLoop, calls=%fused_computation.7 | loop fusion | flops 11796480 | bytes 23617536 | tf_op jit(solution)/shard_map/convert_element_type | solution.py:436
  684.3 13.1 %reduce-scatter.23.cloned.1.call-done = bf16[512,1024]{1,0:T(8,128)(2,1)} async-done(((bf16[2048,1024]{1,0:T(8,128)(2,1)}), bf16[512,1024]{1,0:T(8,128)(2,1)}) %reduce-scatter.23.cloned.1.call-update) | async-done | bytes 1048592 | tf_op jit(solution)/shard_map/reduce_scatter | solution.py:421
  697.3 55.6 %reduce-scatter.21.cloned.1.call-done = bf16[512,1024]{1,0:T(8,128)(2,1)} async-done(((bf16[2048,1024]{1,0:T(8,128)(2,1)}), bf16[512,1024]{1,0:T(8,128)(2,1)}) %reduce-scatter.21.cloned.1.call-update) | async-done | bytes 1048592 | tf_op jit(solution)/shard_map/reduce_scatter | solution.py:421
  752.9 55.5 %reduce-scatter.19.cloned.1.call-done = bf16[512,1024]{1,0:T(8,128)(2,1)} async-done(((bf16[2048,1024]{1,0:T(8,128)(2,1)}), bf16[512,1024]{1,0:T(8,128)(2,1)}) %reduce-scatter.19.cloned.1.call-update) | async-done | bytes 1048592 | tf_op jit(solution)/shard_map/reduce_scatter | solution.py:421
  811.5 4.7 all-to-all-start.3
  819.6 109.6 %all-to-all-done.3 = bf16[4,128,3072]{2,1,0:T(8,128)(2,1)} async-done(((bf16[4,128,3072]{2,1,0:T(8,128)(2,1)}), bf16[4,128,3072]{2,1,0:T(8,128)(2,1)}, u32[]{:S(2)}, u32[]{:S(2)}) %all-to-all-start.3) | async-done | bytes 3145760 | tf_op jit(solution)/shard_map/all_to_all | solution.py:426
  943.3 38.3 %reduce-scatter.15.cloned.1.call-done = bf16[128,2048]{1,0:T(8,128)(2,1)} async-done(((bf16[1024,2048]{1,0:T(8,128)(2,1)}), bf16[128,2048]{1,0:T(8,128)(2,1)}) %reduce-scatter.15.cloned.1.call-update) | async-done | bytes 524304 | tf_op jit(solution)/shard_map/reduce_scatter | solution.py:307
  989.0 39.4 %psum.7 = f32[2,2048]{1,0:T(2,128)S(1)} all-reduce(f32[2,2048]{1,0:T(2,128)S(1)} %pad_maximum_fusion.8), channel_id=1, replica_groups=mesh['fsdp'=4,'context'=4,'tensor'=2] {'fsdp','context','tensor'}, use_global_device_ids=true, to_apply=%region_17.18 | all-reduce | flops 4096 | bytes 32768 | tf_op jit(solution)/shard_map/psum | solution.py:460
  (198 shorter events, 99.0 us)
Async XLA Ops:
  7.2 28.0 %copy-start.28 = (s32[1,4]{1,0:T(1,128)S(1)}, s32[1,4]{1,0:T(1,128)}, u32[]{:S(2)}) copy-start(s32[1,4]{1,0:T(1,128)} %param.14) | copy-start | bytes 52
  7.2 28.3 %copy-start.25 = (f32[128]{0:T(128)S(1)}, f32[128]{0:T(128)}, u32[]{:S(2)}) copy-start(f32[128]{0:T(128)} %param.20) | copy-start | bytes 1540
  7.2 28.3 %copy-start.26 = (f32[128]{0:T(128)S(1)}, f32[128]{0:T(128)}, u32[]{:S(2)}) copy-start(f32[128]{0:T(128)} %param.15) | copy-start | bytes 1540
  7.2 69.9 %all-gather.24.cloned.1.call-start = ((), (), s32[]{:S(2)}) async-start(), calls=%async_computation.27 | async-start | bytes 4718592 | tf_op jit(solution)/shard_map/all_gather | solution.py:303
  9.2 102.3 %all-gather.10.cloned.1.call-start = ((), (), s32[]{:S(2)}) async-start(), calls=%async_computation.12 | async-start | bytes 3276800 | tf_op jit(solution)/shard_map/all_gather | solution.py:343
  35.2 147.2 %reduce-scatter.9.cloned.1.call-start = ((), (), s32[]{:S(2)}) async-start(), calls=%async_computation.13 | async-start | bytes 4718592 | tf_op jit(solution)/shard_map/reduce_scatter | solution.py:307
  76.6 39.6 %copy-start.10 = (f32[1024,64]{0,1:T(8,128)}, f32[1024,64]{0,1:T(8,128)S(1)}, u32[]{:S(2)}) copy-start(f32[1024,64]{0,1:T(8,128)S(1)} %get-tuple-element.77) | copy-start | bytes 786436
  76.6 39.6 %copy-start.12 = (f32[1024,64]{0,1:T(8,128)}, f32[1024,64]{0,1:T(8,128)S(1)}, u32[]{:S(2)}) copy-start(f32[1024,64]{0,1:T(8,128)S(1)} %get-tuple-element.78) | copy-start | bytes 786436
  132.2 50.1 %copy-start.2 = (bf16[1,256,2048]{2,1,0:T(8,128)(2,1)S(1)}, bf16[1,256,2048]{2,1,0:T(8,128)(2,1)}, u32[]{:S(2)}) copy-start(bf16[1,256,2048]{2,1,0:T(8,128)(2,1)} %param.12) | copy-start | bytes 3145732
  132.2 174.6 %all-gather.12.cloned.1.call-start = ((), (), s32[]{:S(2)}) async-start(), calls=%async_computation.14 | async-start | bytes 4718592 | tf_op jit(solution)/shard_map/all_gather | solution.py:303
  186.6 239.0 %all-gather.14.cloned.1.call-start = ((), (), s32[]{:S(2)}) async-start(), calls=%async_computation.15 | async-start | bytes 15728640 | tf_op jit(solution)/shard_map/all_gather | solution.py:355
  304.3 171.1 %all-gather.18.cloned.1.call-start = ((), (), s32[]{:S(2)}) async-start(), calls=%async_computation.18 | async-start | bytes 4718592 | tf_op jit(solution)/shard_map/all_gather | solution.py:303
  306.7 240.6 %reduce-scatter.11.cloned.1.call-start = ((), (), s32[]{:S(2)}) async-start(), calls=%async_computation.16 | async-start | bytes 4718592 | tf_op jit(solution)/shard_map/reduce_scatter | solution.py:307
  489.1 10.0 copy-start.30
  499.1 99.0 %reduce-scatter.13.cloned.1.call-start = ((), (), s32[]{:S(2)}) async-start(), calls=%async_computation.19 | async-start | bytes 4718592 | tf_op jit(solution)/shard_map/reduce_scatter | solution.py:307
  512.5 129.3 %all-gather.20.cloned.1.call-start = ((), (), s32[]{:S(2)}) async-start(), calls=%async_computation.20 | async-start | bytes 4718592 | tf_op jit(solution)/shard_map/all_gather | solution.py:303
  549.5 53.3 %copy-start.3 = (bf16[128,2048]{1,0:T(8,128)(2,1)S(1)}, bf16[128,2048]{1,0:T(8,128)(2,1)}, u32[]{:S(2)}) copy-start(bf16[128,2048]{1,0:T(8,128)(2,1)} %reduce-scatter.9.cloned.1.call-done) | copy-start | bytes 1572868
  606.6 90.7 %reduce-scatter.23.cloned.1.call-start = ((), (), s32[]{:S(2)}) async-start(), calls=%async_computation.26 | async-start | bytes 5242880 | tf_op jit(solution)/shard_map/reduce_scatter | solution.py:421
  616.3 136.6 %reduce-scatter.21.cloned.1.call-start = ((), (), s32[]{:S(2)}) async-start(), calls=%async_computation.25 | async-start | bytes 5242880 | tf_op jit(solution)/shard_map/reduce_scatter | solution.py:421
  625.7 182.7 %reduce-scatter.19.cloned.1.call-start = ((), (), s32[]{:S(2)}) async-start(), calls=%async_computation.24 | async-start | bytes 5242880 | tf_op jit(solution)/shard_map/reduce_scatter | solution.py:421
  635.9 9.3 copy-start.23
  635.9 183.6 %all-gather.16.cloned.1.call-start = ((), (), s32[]{:S(2)}) async-start(), calls=%async_computation.17 | async-start | bytes 1572864 | tf_op jit(solution)/shard_map/all_gather | solution.py:406
  636.7 300.7 %reduce-scatter.17.cloned.1.call-start = ((), (), s32[]{:S(2)}) async-start(), calls=%async_computation.23 | async-start | bytes 3276800 | tf_op jit(solution)/shard_map/reduce_scatter | solution.py:446
  641.8 8.8 slice-start
  656.0 10.6 %copy-start.15 = (bf16[768,4,64]{0,2,1:T(8,128)(2,1)S(1)}, bf16[768,4,64]{0,2,1:T(8,128)(2,1)}, u32[]{:S(2)}) copy-start(bf16[768,4,64]{0,2,1:T(8,128)(2,1)} %copy-done.14) | copy-start | bytes 1179652
  678.5 303.0 %reduce-scatter.15.cloned.1.call-start = ((), (), s32[]{:S(2)}) async-start(), calls=%async_computation.21 | async-start | bytes 4718592 | tf_op jit(solution)/shard_map/reduce_scatter | solution.py:307
  811.5 117.7 %all-to-all-start.3 = ((bf16[4,128,3072]{2,1,0:T(8,128)(2,1)}), bf16[4,128,3072]{2,1,0:T(8,128)(2,1)}, u32[]{:S(2)}, u32[]{:S(2)}) async-start(bf16[4,128,3072]{2,1,0:T(8,128)(2,1)} %pad_maximum_fusion), calls=%async_computation.11 | async-start | bytes 6291456 | tf_op jit(solution)/shard_map/all_to_all | solution.py:426
  935.9 45.6 %copy-start.21 = (f32[1,2048]{1,0:T(1,128)S(1)}, f32[1,2048]{1,0:T(1,128)}, u32[]{:S(2)}) copy-start(f32[1,2048]{1,0:T(1,128)} %copy-done.20) | copy-start | bytes 24580
  935.9 47.1 %copy-start.5 = (f32[128,2048]{1,0:T(8,128)S(1)}, f32[128,2048]{1,0:T(8,128)}, u32[]{:S(2)}) copy-start(f32[128,2048]{1,0:T(8,128)} %get-tuple-element.52) | copy-start | bytes 3145732
  939.5 45.8 %all-to-all-start.2 = ((bf16[4,128,640]{1,2,0:T(8,128)(2,1)}), bf16[4,128,640]{1,2,0:T(8,128)(2,1)S(1)}, u32[]{:S(2)}, u32[]{:S(2)}) async-start(bf16[4,128,640]{1,2,0:T(8,128)(2,1)} %copy_bitcast_fusion.2), calls=%async_computation.7 | async-start | bytes 1310720 | tf_op jit(solution)/shard_map/all_to_all | solution.py:447
  943.3 85.6 %all-gather.22.cloned.1.call-start = ((), (), s32[]{:S(2)}) async-start(), calls=%async_computation.22 | async-start | bytes 1572864 | tf_op jit(solution)/shard_map/all_gather | solution.py:459
  985.3 43.6 %copy-start.16 = (bf16[256,2048]{1,0:T(8,128)(2,1)S(1)}, bf16[256,2048]{1,0:T(8,128)(2,1)}, u32[]{:S(2)}) copy-start(bf16[256,2048]{1,0:T(8,128)(2,1)} %all-gather.16.cloned.1.call-done) | copy-start | bytes 3145732
  (20 other events, 73.5 us)
Sparse Core Ops, SparseCore 0:
  10.5 44.0 all-gather.23
  56.7 54.7 all-gather.9
  132.4 49.9 reduce-scatter.8
  186.7 94.8 all-gather.11
  304.5 121.0 all-gather.13
  427.6 47.8 all-gather.17
  499.2 48.0 reduce-scatter.10
  549.6 48.3 reduce-scatter.12
  606.7 35.0 all-gather.19
  644.6 52.6 reduce-scatter.22
  700.3 52.5 reduce-scatter.20
  755.8 52.5 reduce-scatter.18
  810.5 9.0 all-gather.15
  821.7 99.0 reduce-scatter.16
  924.0 57.5 reduce-scatter.14
  985.5 9.0 all-gather.21

commit v2 on v1

--- a/solution.py
+++ b/solution.py
@@ -1,6 +1,8 @@
 import jax
 import jax.numpy as jnp
 from jax import lax
+from jax.experimental import pallas as pl
+from jax.experimental.pallas import tpu as pltpu
 from jax.sharding import PartitionSpec as P
 
 HEAD = 64
@@ -293,18 +295,302 @@
     )
 
 
-def pick_block(x, axis_name, axis):
-    n = lax.axis_size(axis_name)
-    size = x.shape[axis] // n
-    return lax.dynamic_slice_in_dim(x, lax.axis_index(axis_name) * size, size, axis)
-
-
-def gather_tokens(x, axes):
-    return lax.all_gather(x, axes, axis=0, tiled=True)
-
-
-def scatter_tokens(x, axes):
-    return lax.psum_scatter(x, axes, scatter_dimension=0, tiled=True)
+def flip(i, k):
+    if k == 0:
+        return i
+    if k == 1:
+        return i + 1 - 2 * lax.rem(i, 2)
+    if k == 2:
+        return lax.rem(i + 2, 4)
+    return 3 - i
+
+
+class Copies:
+    def __init__(self, send, receive):
+        self.send, self.receive = send, receive
+        self.count, self.started = 0, []
+
+    def index(self):
+        self.count += 1
+        return self.count - 1
+
+    def make(self, i, source, target, device):
+        return pltpu.make_async_remote_copy(
+            src_ref=source,
+            dst_ref=target,
+            send_sem=self.send.at[i],
+            recv_sem=self.receive.at[i],
+            device_id=device,
+            device_id_type=pl.DeviceIdType.MESH,
+        )
+
+    def start(self, source, target, device, i=None):
+        i = self.index() if i is None else i
+        copy = self.make(i, source, target, device)
+        copy.start()
+        self.started.append(copy)
+        return copy
+
+
+def greet(partners):
+    barrier = pltpu.get_barrier_semaphore()
+    for device in partners:
+        pl.semaphore_signal(barrier, inc=1, device_id=device, device_id_type=pl.DeviceIdType.MESH)
+    pl.semaphore_wait(barrier, len(partners))
+
+
+def weights_in_kernel(wa, wf, xt, gain, wa_all, wf_all, x_all, gain_all, send, receive, local):
+    z, c, t = (lax.axis_index(a) for a in (FSDP, CONTEXT, TENSOR))
+    peers = [(flip(z, i), flip(c, j), t) for i in range(4) for j in range(4) if i or j]
+    core = (z, c, 1 - t)
+    greet(peers + [core])
+    net = Copies(send, receive)
+    ends = []
+    own = []
+    for i, (source, target) in enumerate(
+        (
+            (wa.at[c], wa_all.at[z, c]),
+            (xt, x_all.at[c]),
+            (wf.at[z], wf_all.at[z, c]),
+            (gain, gain_all.at[z, c]),
+        )
+    ):
+        own.append(pltpu.make_async_copy(source, target, local.at[i]))
+        own[-1].start()
+
+    attn_in = [net.start(wa.at[flip(c, k)], wa_all.at[z, c], (z, flip(c, k), t)) for k in (1, 2, 3)]
+    tokens_in = [net.start(xt.at[t], x_all.at[c, t], (z, flip(c, k), t)) for k in (1, 2, 3)]
+    for device in peers:
+        ends.append(net.start(gain, gain_all.at[z, c], device))
+    own[2].wait()
+    forward = []
+    middle = (z == 1) | (z == 2)
+    for j in range(4):
+        if j:
+            attn_in[j - 1].wait_recv()
+        else:
+            own[0].wait()
+        piece = wa_all.at[z, flip(c, j)]
+        ends.append(net.start(piece, piece, (flip(z, 1), c, t)))
+        two = net.start(piece, piece, (flip(z, 2), c, t))
+        three = net.index()
+        direct = net.make(three, piece, piece, (3 - z, c, t))
+        pl.when(middle)(direct.start)
+        passed_piece = wa_all.at[flip(z, 2), flip(c, j)]
+        passed = pltpu.make_async_remote_copy(
+            src_ref=passed_piece,
+            dst_ref=passed_piece,
+            send_sem=send.at[net.index()],
+            recv_sem=receive.at[three],
+            device_id=(flip(z, 1), c, t),
+            device_id_type=pl.DeviceIdType.MESH,
+        )
+        forward.append((two, direct, passed))
+    ff_in = {k: net.start(wf.at[flip(z, k)], wf_all.at[z, c], (flip(z, k), c, t)) for k in (3, 2)}
+    ff_out = {0: [net.start(wf_all.at[z, c], wf_all.at[z, c], (z, flip(c, k), t)) for k in (1, 2)]}
+    swaps = []
+    for k, copy in zip((1, 2, 3), tokens_in):
+        copy.wait_recv()
+        piece = x_all.at[flip(c, k), t]
+        swaps.append(net.start(piece, piece, core))
+    for two, direct, passed in forward:
+        two.wait_recv()
+        pl.when(middle)(passed.start)
+    ff_in[1] = net.start(wf.at[flip(z, 1)], wf_all.at[z, c], (flip(z, 1), c, t))
+    halves = []
+
+    def corner(k):
+        zs = flip(z, k)
+        one, two = ff_out[k]
+        two.wait_recv()
+        piece = wf_all.at[zs, flip(c, 2), pl.ds(0, 64)]
+        halves.append(net.start(piece, piece, (z, flip(c, 1), t)))
+        one.wait_recv()
+        piece = wf_all.at[zs, flip(c, 1), pl.ds(64, 64)]
+        halves.append(net.start(piece, piece, (z, flip(c, 2), t)))
+
+    last = 0
+    for k in (3, 2, 1):
+        ff_in[k].wait_recv()
+        piece = wf_all.at[flip(z, k), c]
+        ff_out[k] = [net.start(piece, piece, (z, flip(c, j), t)) for j in (1, 2)]
+        corner(last)
+        last = k
+    corner(last)
+    for copy in halves + swaps + ends:
+        copy.wait_recv()
+    for _, direct, passed in forward:
+        direct.wait_recv()
+        pl.when(middle)(direct.wait_send)
+        pl.when(middle)(passed.wait_send)
+    for copy in net.started:
+        copy.wait_send()
+    own[1].wait()
+    own[3].wait()
+
+
+def weights_in(wa, wf, xt, gain):
+    bf16 = jnp.bfloat16
+    shapes = ((4, 4) + wa.shape[1:], (4, 4) + wf.shape[1:], (4,) + xt.shape, (4, 4) + gain.shape)
+    copies = 128
+    return pl.pallas_call(
+        weights_in_kernel,
+        out_shape=[jax.ShapeDtypeStruct(s, bf16) for s in shapes],
+        in_specs=[pl.BlockSpec(memory_space=pltpu.VMEM)] * 4,
+        out_specs=[pl.BlockSpec(memory_space=pl.ANY)] * 4,
+        scratch_shapes=[
+            pltpu.SemaphoreType.DMA((copies,)),
+            pltpu.SemaphoreType.DMA((copies,)),
+            pltpu.SemaphoreType.DMA((4,)),
+        ],
+        compiler_params=pltpu.CompilerParams(collective_id=1, has_side_effects=True, vmem_limit_bytes=48 * 2**20),
+    )(wa, wf, xt, gain)
+
+
+def swap(x, axis, k):
+    return lax.ppermute(x, axis, [(i, i ^ k) for i in range(lax.axis_size(axis))])
+
+
+def after(x, *others):
+    return lax.optimization_barrier((x, *others))[0]
+
+
+def put(buffer, block, *index):
+    lead = len(index)
+    block = block.reshape((1,) * lead + buffer.shape[lead:])
+    zero = jnp.int32(0)
+    start = tuple(jnp.asarray(i, jnp.int32) for i in index) + (zero,) * (buffer.ndim - lead)
+    return lax.dynamic_update_slice(buffer, block, start)
+
+
+def cut(x, index, size, axis):
+    return lax.dynamic_slice_in_dim(x, index * size, size, axis)
+
+
+def fsdp_blocks(x):
+    one = swap(x, FSDP, 1)
+    two = swap(x, FSDP, 2)
+    three = lax.ppermute(x, FSDP, [(1, 2), (2, 1)]) + lax.ppermute(two, FSDP, [(2, 3), (1, 0)])
+    return [x, one, two, three]
+
+
+def context_blocks(x, axis):
+    one = swap(x, CONTEXT, 1)
+    two = swap(x, CONTEXT, 2)
+    half = x.shape[axis] // 2
+    low = swap(lax.slice_in_dim(two, 0, half, axis=axis), CONTEXT, 1)
+    high = swap(lax.slice_in_dim(one, half, 2 * half, axis=axis), CONTEXT, 2)
+    return one, two, low, high
+
+
+def grads_out_kernel(
+    ff, at, gate_out, up_out, down_out, query_out, key_out, value_out, output_out,
+    terms, corner_x, corner_y, side_x, side_y, landed, at_terms, at_in, at_total, at_landed, send, receive, local,
+):
+    f32, bf16 = jnp.float32, jnp.bfloat16
+    z, c, t = (lax.axis_index(a) for a in (FSDP, CONTEXT, TENSOR))
+    greet([(flip(z, k), c, t) for k in (1, 2, 3)] + [(z, flip(c, k), t) for k in (1, 2, 3)])
+    net = Copies(send, receive)
+    rows = ff.shape[2]
+    half = rows // 2
+    order = (3, 2, 1, 0)
+    loads = {}
+    for k in order:
+        zs = flip(z, k)
+        loads[k] = pltpu.make_async_copy(ff.at[zs], terms.at[zs], local.at[k])
+        loads[k].start()
+    attn_load = pltpu.make_async_copy(at, at_terms, local.at[4])
+    attn_load.start()
+    attn_load.wait()
+    attn_in = [net.start(at_terms.at[flip(z, k)], at_in.at[k - 1], (flip(z, k), c, t)) for k in (3, 2, 1)]
+    first = {}
+    for k in order:
+        zs = flip(z, k)
+        loads[k].wait()
+        first[k] = (
+            net.start(terms.at[zs, flip(c, 3), pl.ds(0, half)], corner_x.at[k], (z, flip(c, 1), t)),
+            net.start(terms.at[zs, flip(c, 3), pl.ds(half, half)], corner_y.at[k], (z, flip(c, 2), t)),
+        )
+    second = {}
+    for k in order:
+        zs = flip(z, k)
+        for copy in first[k]:
+            copy.wait_recv()
+        low, high = pl.ds(0, half), pl.ds(half, half)
+        xb, yb = flip(c, 1), flip(c, 2)
+        terms[zs, yb, low] = (terms[zs, yb, low].astype(f32) + corner_x[k].astype(f32)).astype(bf16)
+        terms[zs, xb, high] = (terms[zs, xb, high].astype(f32) + corner_y[k].astype(f32)).astype(bf16)
+        second[k] = (
+            net.start(terms.at[zs, yb], side_y.at[k], (z, yb, t)),
+            net.start(terms.at[zs, xb], side_x.at[k], (z, xb, t)),
+        )
+    for copy in attn_in:
+        copy.wait_recv()
+    for j in range(4):
+        total = at_terms[z, j].astype(f32)
+        for i in range(3):
+            total = total + at_in[i, j].astype(f32)
+        at_total[j] = total.astype(bf16)
+    attn_out = [net.start(at_total.at[flip(c, k)], at_landed.at[c], (z, flip(c, k), t)) for k in (1, 2, 3)]
+    at_landed[c] = at_total[c]
+    third = {}
+    for k in order:
+        zs = flip(z, k)
+        for copy in second[k]:
+            copy.wait_recv()
+        total = terms[zs, c].astype(f32) + side_x[k].astype(f32) + side_y[k].astype(f32)
+        if k:
+            terms[zs, c] = total.astype(bf16)
+            third[k] = net.start(terms.at[zs, c], landed.at[k], (zs, c, t))
+        else:
+            landed[0] = total.astype(bf16)
+    size = gate_out.shape[1] // 4
+    for k in (0, 3, 2, 1):
+        if k:
+            third[k].wait_recv()
+        zs = flip(z, k)
+        columns = pl.ds(pl.multiple_of(zs * size, size), size)
+        for i, out in enumerate((gate_out, up_out, down_out)):
+            out[:, columns] = landed[k, :, i * size : (i + 1) * size].astype(f32)
+    for copy in attn_out:
+        copy.wait_recv()
+    begin = 0
+    for out in (query_out, key_out, value_out, output_out):
+        size = out.shape[1] // 4
+        for j in range(4):
+            out[:, j * size : (j + 1) * size] = at_landed[j, :, begin : begin + size].astype(f32)
+        begin += size
+    for copy in net.started:
+        copy.wait_send()
+
+
+def grads_out(ff, at, sizes):
+    bf16, f32 = jnp.bfloat16, jnp.float32
+    rows, cols = ff.shape[2:]
+    attn_cols = at.shape[3]
+    copies = 32
+    return pl.pallas_call(
+        grads_out_kernel,
+        out_shape=[jax.ShapeDtypeStruct((rows, s), f32) for s in sizes],
+        in_specs=[pl.BlockSpec(memory_space=pl.ANY)] * 2,
+        out_specs=[pl.BlockSpec(memory_space=pltpu.VMEM)] * len(sizes),
+        scratch_shapes=[
+            pltpu.VMEM((4, 4, rows, cols), bf16),
+            pltpu.VMEM((4, rows // 2, cols), bf16),
+            pltpu.VMEM((4, rows // 2, cols), bf16),
+            pltpu.VMEM((4, rows, cols), bf16),
+            pltpu.VMEM((4, rows, cols), bf16),
+            pltpu.VMEM((4, rows, cols), bf16),
+            pltpu.VMEM((4, 4, rows, attn_cols), bf16),
+            pltpu.VMEM((3, 4, rows, attn_cols), bf16),
+            pltpu.VMEM((4, rows, attn_cols), bf16),
+            pltpu.VMEM((4, rows, attn_cols), bf16),
+            pltpu.SemaphoreType.DMA((copies,)),
+            pltpu.SemaphoreType.DMA((copies,)),
+            pltpu.SemaphoreType.DMA((5,)),
+        ],
+        compiler_params=pltpu.CompilerParams(collective_id=2, has_side_effects=True, vmem_limit_bytes=60 * 2**20),
+    )(ff, at)
 
 
 def on_device_split(
@@ -323,58 +609,54 @@
 ):
     f32, bf16 = jnp.float32, jnp.bfloat16
     nz, nc, nt = (lax.axis_size(a) for a in (FSDP, CONTEXT, TENSOR))
+    z, c, t = (lax.axis_index(a) for a in (FSDP, CONTEXT, TENSOR))
     local_rows, width = tokens.shape[1:]
     group_rows = local_rows * nc
     filled = group_rows * 3 // 4
-    part_rows = local_rows // nt
+    part = local_rows // nt
     wrows = query_weight.shape[0]
     kv_cols = key_weight.shape[1] // nc
     q_cols = query_weight.shape[1] // nc
+    qkv_cols = q_cols + 2 * kv_cols
     ff_cols = gate_weight.shape[1] // nz
     per_group = q_cols // kv_cols
     segment, position, valid_rows = slot_layout(lengths[0], group_rows)
     cos_table, sine_table = rope_tables(position, HEAD)
 
-    attn_cols = jnp.concatenate(
-        [w.astype(bf16).reshape(wrows, nc, -1) for w in (query_weight, key_weight, value_weight, output_weight)],
+    wa = jnp.concatenate(
+        [
+            w.astype(bf16).reshape(wrows, nc, -1).transpose(1, 0, 2)
+            for w in (query_weight, key_weight, value_weight, output_weight)
+        ],
         axis=2,
-    ).transpose(1, 0, 2)
-    attn_cols = lax.all_to_all(attn_cols, CONTEXT, 0, 0, tiled=True)
-    attn_all = lax.all_gather(attn_cols.reshape(nc * wrows, -1), FSDP, axis=0, tiled=True)
-    w_qkv = attn_all[:, : q_cols + 2 * kv_cols]
-    w_out = attn_all[:, q_cols + 2 * kv_cols :]
-    gains = lax.all_gather(
-        jnp.stack([attention_gain, feed_gain]).astype(bf16), (FSDP, CONTEXT), axis=1, tiled=True
-    ).astype(f32)
+    )
+    wf = jnp.concatenate(
+        [w.astype(bf16).reshape(wrows, nz, ff_cols).transpose(1, 0, 2) for w in (gate_weight, up_weight, down_weight)],
+        axis=2,
+    )
+    gain = jnp.pad(jnp.stack([attention_gain, feed_gain]).astype(bf16), ((0, 14), (0, 0)))
+    wa, wf, all_tokens, gains = weights_in(wa, wf, tokens[0].reshape(nt, part, width), gain)
+    gains = gains[:, :, :2].transpose(2, 0, 1, 3).reshape(2, width).astype(f32)
     gain_one, gain_two = gains[0], gains[1]
-
-    ff_part = jnp.concatenate(
-        [w.astype(bf16).reshape(wrows, nz, -1) for w in (gate_weight, up_weight, down_weight)], axis=2
-    ).transpose(1, 0, 2)
-    ff_part = lax.all_to_all(ff_part, FSDP, 0, 0, tiled=True)
-    ff_all = lax.all_gather(ff_part.reshape(nz * wrows, -1), CONTEXT, axis=0, tiled=True)
-    w_gate_up = ff_all[:, : 2 * ff_cols]
-    w_down = ff_all[:, 2 * ff_cols :]
-
-    def to_ff(x):
-        return x.reshape(-1, nz, nc, wrows).transpose(0, 2, 1, 3).reshape(x.shape)
-
-    def from_ff(x):
-        return x.reshape(-1, nc, nz, wrows).transpose(0, 2, 1, 3).reshape(x.shape)
-
-    my_tokens = pick_block(tokens[0], TENSOR, 0)
-    all_tokens = gather_tokens(my_tokens, (CONTEXT, TENSOR)).astype(f32)
-    cotangent = pick_block(out_grad[0], TENSOR, 0)
-    first_row = lax.axis_index(CONTEXT) * local_rows + lax.axis_index(TENSOR) * part_rows
-    my_valid = lax.dynamic_slice_in_dim(valid_rows, first_row, part_rows)
-    cotangent = cotangent.astype(f32) * my_valid[:, None].astype(f32)
-    feed_grad = gather_tokens(to_ff((residual_mult * cotangent).astype(bf16)), (FSDP, TENSOR))
+    w_qkv = wa[..., :qkv_cols].reshape(width, qkv_cols)
+    w_out = wa[..., qkv_cols:].reshape(width, q_cols)
+    my_tokens = cut(tokens[0], t, part, 0)
+    all_tokens = all_tokens.reshape(group_rows, width).astype(f32)
+    w_gate_up = wf[..., : 2 * ff_cols].reshape(width, 2 * ff_cols)
+    w_down = wf[..., 2 * ff_cols :].reshape(width, ff_cols)
+
+    my_valid = lax.dynamic_slice_in_dim(valid_rows, c * local_rows + t * part, part)
+    cotangent = cut(out_grad[0], t, part, 0).astype(f32) * my_valid[:, None].astype(f32)
+    feed_grads = fsdp_blocks((residual_mult * cotangent).astype(bf16))
+    feed_grads = [jnp.concatenate([b, swap(b, TENSOR, 1)], axis=0) for b in feed_grads]
 
     inverse_all = lax.rsqrt(jnp.mean(all_tokens * all_tokens, axis=-1, keepdims=True) + norm_eps)
-    normed_one = (all_tokens * inverse_all * gain_one).astype(bf16)
+    unit_all = all_tokens * inverse_all
+    normed_one = (unit_all * gain_one).astype(bf16)
     qkv = jnp.dot(normed_one, w_qkv, preferred_element_type=f32)
     queries = rotate(qkv[:, :q_cols].reshape(group_rows, per_group, HEAD), cos_table, sine_table).astype(bf16)
-    keys = rotate(qkv[:, q_cols : q_cols + kv_cols].reshape(group_rows, 1, HEAD), cos_table, sine_table).astype(bf16)[:, 0]
+    keys = rotate(qkv[:, q_cols : q_cols + kv_cols].reshape(group_rows, 1, HEAD), cos_table, sine_table)
+    keys = keys.astype(bf16)[:, 0]
     values = qkv[:, q_cols + kv_cols :].astype(bf16)
     slot_ids = jnp.arange(filled, dtype=jnp.int32)
     allowed = (segment[:filled, None] == segment[None, :filled]) & (slot_ids[:, None] >= slot_ids[None, :])
@@ -389,46 +671,74 @@
     mixed = jnp.einsum("gts,sd->tgd", prob_low, v_f, preferred_element_type=f32).astype(bf16)
     attended_f = mixed.reshape(filled, q_cols)
     attended = jnp.concatenate([attended_f, jnp.tile(values[filled:], (1, per_group))], axis=0)
-    attn_part = dot_last(attended, w_out)
-    attn_out = scatter_tokens(attn_part.astype(bf16), (CONTEXT, TENSOR)).astype(f32)
+
+    def scatter_context(partial):
+        partial = partial.reshape(nc, nt, part, width)
+        mine = cut(partial, t, 1, 1)[:, 0]
+        other = cut(partial, 1 - t, 1, 1)[:, 0].astype(bf16)
+        mine = mine + swap(other, TENSOR, 1).astype(f32)
+        total = cut(mine, c, 1, 0)[0]
+        for k in range(1, nc):
+            total = total + swap(cut(mine, c ^ k, 1, 0)[0].astype(bf16), CONTEXT, k).astype(f32)
+        return total
+
+    attn_out = scatter_context(dot_last(attended, w_out))
     my_inputs = my_tokens.astype(f32)
     hidden = my_inputs + residual_mult * attn_out
     inverse_two = lax.rsqrt(jnp.mean(hidden * hidden, axis=-1, keepdims=True) + norm_eps)
     unit_two = hidden * inverse_two
-    normed_two = gather_tokens(to_ff((unit_two * gain_two).astype(bf16)), (FSDP, TENSOR))
-    gate_up = jnp.dot(normed_two, w_gate_up, preferred_element_type=f32)
-    gate_out, up_out = gate_up[:, :ff_cols], gate_up[:, ff_cols:]
-    sig = jax.nn.sigmoid(gate_out)
-    inner = (gate_out * sig * up_out).astype(bf16)
-    feed_part = dot_last(inner, w_down)
-    feed_out = from_ff(scatter_tokens(feed_part.astype(bf16), (FSDP, TENSOR)).astype(f32))
+
+    def scatter_block(partial, k):
+        mine = partial[:part] + swap(partial[part:].astype(bf16), TENSOR, 1).astype(f32)
+        return mine if k == 0 else swap(mine.astype(bf16), FSDP, k).astype(f32)
+
+    normed_blocks = [
+        jnp.concatenate([b, swap(b, TENSOR, 1)], axis=0) for b in fsdp_blocks((unit_two * gain_two).astype(bf16))
+    ]
+    inner_blocks, gate_blocks, up_blocks, back_parts, feed_parts = [], [], [], [], []
+    for k in range(nz):
+        gate_up = jnp.dot(normed_blocks[k], w_gate_up, preferred_element_type=f32)
+        gate_out, up_out = gate_up[:, :ff_cols], gate_up[:, ff_cols:]
+        inner_grad = jnp.dot(feed_grads[k], w_down, preferred_element_type=f32)
+        sig = jax.nn.sigmoid(gate_out)
+        inner_blocks.append((gate_out * sig * up_out).astype(bf16))
+        gate_blocks.append((inner_grad * up_out * sig * (1.0 + gate_out * (1.0 - sig))).astype(bf16))
+        up_blocks.append((inner_grad * gate_out * sig).astype(bf16))
+        both = jnp.concatenate([gate_blocks[k], up_blocks[k]], axis=1)
+        back_parts.append(scatter_block(dot_last(both, w_gate_up), k))
+        feed_parts.append(dot_last(inner_blocks[k], w_down))
+    normed_grad_two = sum(back_parts)
+    feed_out = sum(scatter_block(p, k) for k, p in enumerate(feed_parts))
     output = (hidden + residual_mult * feed_out).astype(bf16)
-    output = lax.all_gather(output, TENSOR, axis=0, tiled=True)
-
-    inner_grad = jnp.dot(feed_grad, w_down, preferred_element_type=f32)
-    gate_grad = (inner_grad * up_out * sig * (1.0 + gate_out * (1.0 - sig))).astype(bf16)
-    up_grad = (inner_grad * gate_out * sig).astype(bf16)
-    both_grad = jnp.concatenate([gate_grad, up_grad], axis=1)
-    normed_part = dot_last(both_grad, w_gate_up)
-    normed_grad_two = from_ff(scatter_tokens(normed_part.astype(bf16), (FSDP, TENSOR)).astype(f32))
+
+    def both_cores(x):
+        out = put(jnp.zeros((nt,) + x.shape, x.dtype), x, t)
+        return put(out, swap(x, TENSOR, 1), 1 - t).reshape(1, local_rows, width)
+
+    output = both_cores(output)
     feed_gain_term = jnp.sum(normed_grad_two * unit_two, axis=0)
     hidden_grad = cotangent + norm_back(normed_grad_two, unit_two, gain_two, inverse_two)
-    down_term = dot_first(feed_grad, inner).astype(bf16)
-    gate_term = dot_first(normed_two, gate_grad).astype(bf16)
-    up_term = dot_first(normed_two, up_grad).astype(bf16)
+
+    attn_low = (residual_mult * hidden_grad).astype(bf16)
+    attn_grad = jnp.zeros((nc, nt, part, width), bf16)
+    attn_grad = put(attn_grad, attn_low, c, t)
+    attn_grad = put(attn_grad, swap(attn_low, TENSOR, 1), c, 1 - t)
+    for k in range(1, nc):
+        block = swap(attn_low, CONTEXT, k)
+        attn_grad = put(attn_grad, block, c ^ k, t)
+        attn_grad = put(attn_grad, swap(block, TENSOR, 1), c ^ k, 1 - t)
+    attn_grad = attn_grad.reshape(group_rows, width)[:filled]
+
+    normed_two = jnp.concatenate(normed_blocks, axis=0)
     ff_terms = jnp.concatenate(
         [
-            lax.psum_scatter(t, CONTEXT, scatter_dimension=0, tiled=True).reshape(nz, wrows, -1)
-            for t in (gate_term, up_term, down_term)
+            dot_first(normed_two, jnp.concatenate(gate_blocks, axis=0)).astype(bf16),
+            dot_first(normed_two, jnp.concatenate(up_blocks, axis=0)).astype(bf16),
+            dot_first(jnp.concatenate(feed_grads, axis=0), jnp.concatenate(inner_blocks, axis=0)).astype(bf16),
         ],
-        axis=2,
-    )
-    ff_terms = lax.all_to_all(ff_terms, FSDP, 0, 0, tiled=True).astype(f32)
-
-    def ff_out(i):
-        return ff_terms[:, :, i * ff_cols : (i + 1) * ff_cols].transpose(1, 0, 2).reshape(wrows, -1)
-
-    attn_grad = gather_tokens((residual_mult * hidden_grad).astype(bf16), (CONTEXT, TENSOR))[:filled]
+        axis=1,
+    ).reshape(nz, nc, wrows, 3 * ff_cols)
+
     out_term = dot_first(attn_grad, attended_f)
     mixed_grad = jnp.dot(attn_grad, w_out, preferred_element_type=f32).astype(bf16).reshape(filled, per_group, HEAD)
     prob_grad = jnp.einsum("tgd,sd->gts", mixed_grad, v_f, preferred_element_type=f32)
@@ -441,42 +751,29 @@
     query_grad = rotate_back(query_grad, cos_f, sine_f).reshape(filled, q_cols).astype(bf16)
     key_grad = rotate_back(key_grad[:, None], cos_f, sine_f)[:, 0].astype(bf16)
     qkv_grad = jnp.concatenate([query_grad, key_grad, value_grad], axis=1)
-    qkv_term = dot_first(normed_one[:filled], qkv_grad)
-    attn_terms = jnp.concatenate([qkv_term, out_term], axis=1).astype(bf16)
-    attn_terms = lax.psum_scatter(attn_terms, FSDP, scatter_dimension=0, tiled=True)
-    attn_terms = lax.all_to_all(attn_terms.reshape(nc, wrows, -1), CONTEXT, 0, 0, tiled=True).astype(f32)
-
-    def attn_out_cols(first, size):
-        return attn_terms[:, :, first : first + size].transpose(1, 0, 2).reshape(wrows, -1)
-
-    normed_part = dot_last(qkv_grad, w_qkv).astype(bf16)
+    normed_part = dot_last(qkv_grad, w_qkv)
+    attn_gain_term = jnp.sum(normed_part * unit_all[:filled], axis=0)
     normed_part = jnp.pad(normed_part, ((0, group_rows - filled), (0, 0)))
-    normed_grad_one = scatter_tokens(normed_part, (CONTEXT, TENSOR)).astype(f32)
+    normed_grad_one = scatter_context(normed_part)
     inverse_one = lax.rsqrt(jnp.mean(my_inputs * my_inputs, axis=-1, keepdims=True) + norm_eps)
     unit_one = my_inputs * inverse_one
-    attn_gain_term = jnp.sum(normed_grad_one * unit_one, axis=0)
-    input_grad = hidden_grad + norm_back(normed_grad_one, unit_one, gain_one, inverse_one)
-    input_grad = lax.all_gather(input_grad.astype(bf16), TENSOR, axis=0, tiled=True)
-    gain_terms = lax.psum(jnp.stack([attn_gain_term, feed_gain_term]), (FSDP, CONTEXT, TENSOR))
-    gain_terms = pick_block(gain_terms, (FSDP, CONTEXT), 1)
-    return (
-        output[None],
-        input_grad[None],
-        gain_terms[0],
-        attn_out_cols(0, q_cols),
-        attn_out_cols(q_cols, kv_cols),
-        attn_out_cols(q_cols + kv_cols, kv_cols),
-        attn_out_cols(q_cols + 2 * kv_cols, q_cols),
-        gain_terms[1],
-        ff_out(0),
-        ff_out(1),
-        ff_out(2),
-    )
+    input_grad = both_cores((hidden_grad + norm_back(normed_grad_one, unit_one, gain_one, inverse_one)).astype(bf16))
+
+    gain_terms = jnp.stack([attn_gain_term, feed_gain_term])
+    for axis, k in ((TENSOR, 1), (CONTEXT, 1), (CONTEXT, 2), (FSDP, 1), (FSDP, 2)):
+        gain_terms = gain_terms + swap(gain_terms, axis, k)
+    gain_terms = cut(gain_terms, z * nc + c, wrows, 1)
+
+    qkv_term = dot_first(normed_one[:filled], qkv_grad)
+    terms = jnp.concatenate([qkv_term, out_term], axis=1).astype(bf16).reshape(nz, nc, wrows, -1)
+    sizes = [w.shape[1] for w in (gate_weight, up_weight, down_weight)]
+    sizes += [w.shape[1] for w in (query_weight, key_weight, value_weight, output_weight)]
+    grad_gate, grad_up, grad_down, *attn_terms = grads_out(ff_terms, terms, sizes)
+    return (output, input_grad, gain_terms[0], *attn_terms, gain_terms[1], grad_gate, grad_up, grad_down)
 
 
 def solution(mesh):
-    kv_heads_local = 8 // mesh.shape[TENSOR]
-    split = kv_heads_local == mesh.shape[CONTEXT]
+    split = tuple(mesh.shape[a] for a in (FSDP, CONTEXT, TENSOR)) == (4, 4, 2)
     return jax.shard_map(
         on_device_split if split else on_device,
         mesh=mesh,

time: 1050 us -> 839 us (0.80)
  waiting for transfers between devices: 595 us -> 168 us
  Pallas kernels: 0 us -> 321 us
  blocking collectives: 205 us -> 0 us
  local copies, waits for them, and re-layouts: 50.3 us -> 101 us
  other arithmetic: 40.7 us -> 76.6 us
  starting transfers between devices: 9.7 us -> 45.2 us
  between operations: 15.2 us -> 2.8 us
    pallas_call x0 -> x2, Pallas kernels: none -> 321 us  [the longest x1 185 us: weights_in(): pl.pallas_call(weights_in_kernel, out_shape=[jax.ShapeDtypeStruct(s, bf16...]
    reduce_scatter x8 -> x0, waiting for transfers between devices: 294 us -> none  [the longest x4 170 us: scatter_tokens(): return lax.psum_scatter(x, axes, scatter_dimension=0, tiled=True)]
    all_gather x8 -> x0, waiting for transfers between devices: 190 us -> none  [the longest x1 119 us: on_device_split(): lax.all_gather(ff_part.reshape(nz * wrows, -1), CONTEXT, axis=0, tiled=True)]
    ppermute x0 -> x52, waiting for transfers between devices: none -> 168 us  [the longest x48 157 us: swap(): lax.ppermute(x, axis, [(i, i ^ k) for i in range(lax.axis_size(axis))])]
    all_to_all x2 -> x0, blocking collectives: 125 us -> none  [the longest x1 105 us: on_device_split(): ff_part = lax.all_to_all(ff_part, FSDP, 0, 0, tiled=True)]
    all_to_all x2 -> x0, waiting for transfers between devices: 110 us -> none  [the longest x1 110 us: on_device_split(): ff_terms = lax.all_to_all(ff_terms, FSDP, 0, 0, tiled=True).astype(f32)]
    ppermute x0 -> x52, starting transfers between devices: none -> 45.2 us  [the longest x48 39.9 us: swap(): lax.ppermute(x, axis, [(i, i ^ k) for i in range(lax.axis_size(axis))])]
    all_gather x1 -> x0, blocking collectives: 40 us -> none  [on_device_split(): lax.all_gather(jnp.stack([attention_gain, feed_gain]).astype(bf16), (FSDP...]
  transfers between devices with their start and end apart: 18 -> 52, of which waited for: 13 -> 15; matrix products, arithmetic and copies ran while one was open for 14% -> 26% of each run, Pallas kernels for 0% -> 16%
where the time goes in v2:
time: 839 us; the launch traced here: 831 us
  Pallas kernels  321 us (38%)
  waiting for transfers between devices  168 us (20%)
  matrix products  116 us (14%)
  local copies, waits for them, and re-layouts  101 us (12%)
  other arithmetic  76.6 us (9%)
  starting transfers between devices  45.2 us (5%)
    pallas_call x1, Pallas kernels, weights_in(): pl.pallas_call(weights_in_kernel, out_shape=[jax.ShapeDtypeStruct(s, bf16...  185 us
    ppermute x48, waiting for transfers between devices, swap(): lax.ppermute(x, axis, [(i, i ^ k) for i in range(lax.axis_size(axis))])  157 us
    pallas_call x1, Pallas kernels, grads_out(): pl.pallas_call(grads_out_kernel, out_shape=[jax.ShapeDtypeStruct((rows, s...  137 us
    unnamed x196, local copies, waits for them, and re-layouts  45.3 us
    ppermute x48, starting transfers between devices, swap(): lax.ppermute(x, axis, [(i, i ^ k) for i in range(lax.axis_size(axis))])  39.9 us
    dot_general x5, matrix products, dot_first(): lax.dot_general(left, right, (((0,), (0,)), ((), ())), preferred_element_...  33.6 us
    dot_general x10, matrix products, dot_last(): lax.dot_general(left, right, (((1,), (1,)), ((), ())), preferred_element_...  27.7 us
    concatenate x1, other arithmetic, on_device_split(): jnp.concatenate([dot_first(normed_two, jnp.concatenate(gate_blocks, axis=...  21 us
  transfers between devices with their start and end apart: 52, of which 15 were waited for; matrix products, arithmetic and copies ran while one was open for 26% of the time, Pallas kernels for 16%

profile of v2, /device:TPU:0, one launch (start us, length us, event | category | flops | bytes accessed | tf_op | source)
XLA Modules:
  0.0 830.7 jit_solution(8981140538522983590)
XLA Ops:
  17.7 184.5 %shard_map.203 = (bf16[4,4,128,640]{3,2,1,0:T(8,128)(2,1)S(1)}, bf16[4,4,128,3072]{3,2,1,0:T(8,128)(2,1)}, bf16[4,2,128,2048]{3,2,1,0:T(8,128)(2,1)}, bf16[4,4,16,128]{3,2,1,0:T(8,128)(2,1)S(1)}) custom-call(bf16[4,128,640]{2,1,0:T(8,128)(2,1)S(1)} %pad_maximum_fusion.4.wa, bf16[4,128,3072]{2,1,0:T(8,128)(2,1)} %pad_maximum_fusion.1.wf, ...), custom_call_target="tpu_custom_call" | custom-call | tf_op jit(solution)/shard_map/pallas_call | solution.py:436
  216.9 8.1 fusion.186
  225.6 4.7 fusion.41
  231.4 4.6 fusion.187
  240.9 9.0 %collective-permute-start.22 = (bf16[128,2048]{1,0:T(8,128)(2,1)}, bf16[128,2048]{1,0:T(8,128)(2,1)}, u32[]{:S(2)}, u32[]{:S(2)}) collective-permute-start(bf16[128,2048]{1,0:T(8,128)(2,1)} %get-tuple-element.44), channel_id=1, source_target_pairs={{0,8},{8,0},{16,24},{24,16},{1,9},{9,1},{17,25},{25,17},{2,10},{10... | collective-permute-start | bytes 1572872 | tf_op jit(solution)/shard_map/ppermute | solution.py:451
  251.2 22.8 %collective-permute-done.22 = bf16[128,2048]{1,0:T(8,128)(2,1)} collective-permute-done((bf16[128,2048]{1,0:T(8,128)(2,1)}, bf16[128,2048]{1,0:T(8,128)(2,1)}, u32[]{:S(2)}, u32[]{:S(2)}) %collective-permute-start.22) | collective-permute-done | bytes 524320 | tf_op jit(solution)/shard_map/ppermute | solution.py:451
  296.0 8.9 %collective-permute-done.3 = bf16[128,2048]{1,0:T(8,128)(2,1)S(1)} collective-permute-done((bf16[128,2048]{1,0:T(8,128)(2,1)S(1)}, bf16[128,2048]{1,0:T(8,128)(2,1)S(1)}, u32[]{:S(2)}, u32[]{:S(2)}) %collective-permute-start.3) | collective-permute-done | bytes 524320 | tf_op jit(solution)/shard_map/ppermute | solution.py:451
  304.9 10.6 %collective-permute-done.2 = bf16[128,2048]{1,0:T(8,128)(2,1)S(1)} collective-permute-done((bf16[128,2048]{1,0:T(8,128)(2,1)S(1)}, bf16[128,2048]{1,0:T(8,128)(2,1)S(1)}, u32[]{:S(2)}, u32[]{:S(2)}) %collective-permute-start.2) | collective-permute-done | bytes 524320 | tf_op jit(solution)/shard_map/ppermute | solution.py:451
  321.0 8.4 %slice.195 = bf16[4,4,128,2048]{3,2,1,0:T(8,128)(2,1)} slice(bf16[4,4,128,3072]{3,2,1,0:T(8,128)(2,1)} %get-tuple-element.25), slice={[0:4], [0:4], [0:128], [0:2048]} | slice | bytes 16777216 | tf_op jit(solution)/shard_map/slice | solution.py:645
  329.4 4.8 slice.198
  340.1 5.9 fusion.73
  351.4 9.4 %collective-permute-done.6 = bf16[128,2048]{1,0:T(8,128)(2,1)S(1)} collective-permute-done((bf16[128,2048]{1,0:T(8,128)(2,1)S(1)}, bf16[128,2048]{1,0:T(8,128)(2,1)S(1)}, u32[]{:S(2)}, u32[]{:S(2)}) %collective-permute-start.6) | collective-permute-done | bytes 524320 | tf_op jit(solution)/shard_map/ppermute | solution.py:451
  370.1 10.5 %collective-permute-done.15 = bf16[128,2048]{1,0:T(8,128)(2,1)S(1)} collective-permute-done((bf16[128,2048]{1,0:T(8,128)(2,1)S(1)}, bf16[128,2048]{1,0:T(8,128)(2,1)S(1)}, u32[]{:S(2)}, u32[]{:S(2)}) %collective-permute-start.15) | collective-permute-done | bytes 524320 | tf_op jit(solution)/shard_map/ppermute | solution.py:473
  411.4 9.1 %convolution_convert_fusion.1 = bf16[2048,1024]{0,1:T(8,128)(2,1)} fusion(bf16[1024,2048]{1,0:T(8,128)(2,1)} %constant_dynamic-update-slice_fusion, bf16[256,1024]{1,0:T(8,128)(2,1)} %get-tuple-element.68, bf16[256,1024]{1,0:T(8,128)(2,1)S(1)} %copy-done.78, bf16[256,1024]{1,0:T(8,128)(2,1)} %get-tuple-element.64, bf16[256,1024]{1,0:T(8,128)(2,1)S(1)} %copy-done.74), kind=kOutput, calls=%fused_computation.24 | convolution fusion | flops 4305453056 | bytes 10485760 | tf_op jit(solution)/shard_map/dot_general | solution.py:59
  420.5 9.3 %convolution_convert_fusion.2 = bf16[2048,1024]{0,1:T(8,128)(2,1)} fusion(bf16[1024,2048]{1,0:T(8,128)(2,1)} %constant_dynamic-update-slice_fusion, bf16[256,1024]{1,0:T(8,128)(2,1)} %get-tuple-element.67, bf16[256,1024]{1,0:T(8,128)(2,1)S(1)} %copy-done.76, bf16[256,1024]{1,0:T(8,128)(2,1)} %copy-done.79, bf16[256,1024]{1,0:T(8,128)(2,1)S(1)} %copy-done.72), kind=kOutput, calls=%fused_computation.25 | convolution fusion | flops 4305453056 | bytes 10485760 | tf_op jit(solution)/shard_map/dot_general | solution.py:59
  429.8 8.4 %convolution_convert_fusion = bf16[2048,1024]{0,1:T(8,128)(2,1)} fusion(bf16[1024,2048]{1,0:T(8,128)(2,1)} %constant_dynamic-update-slice_fusion.8, bf16[256,1024]{1,0:T(8,128)(2,1)S(1)} %get-tuple-element.72, bf16[256,1024]{1,0:T(8,128)(2,1)S(1)} %get-tuple-element.71, bf16[256,1024]{1,0:T(8,128)(2,1)S(1)} %get-tuple-element.70, ...), kind=kOutput, calls=%fused_computation.23 | convolution fusion | flops 4305453056 | bytes 10485760 | tf_op jit(solution)/shard_map/dot_general | solution.py:59
  438.2 4.8 fusion.117
  455.0 19.2 %collective-permute-done.29 = bf16[128,2048]{1,0:T(8,128)(2,1)S(1)} collective-permute-done((bf16[128,2048]{1,0:T(8,128)(2,1)S(1)}, bf16[128,2048]{1,0:T(8,128)(2,1)S(1)}, u32[]{:S(2)}, u32[]{:S(2)}) %collective-permute-start.29) | collective-permute-done | bytes 524320 | tf_op jit(solution)/shard_map/ppermute | solution.py:451
  474.2 12.8 %collective-permute-done.25 = bf16[128,2048]{1,0:T(8,128)(2,1)S(1)} collective-permute-done((bf16[128,2048]{1,0:T(8,128)(2,1)S(1)}, bf16[128,2048]{1,0:T(8,128)(2,1)S(1)}, u32[]{:S(2)}, u32[]{:S(2)}) %collective-permute-start.25) | collective-permute-done | bytes 524320 | tf_op jit(solution)/shard_map/ppermute | solution.py:451
  491.7 38.4 %collective-permute-done.13 = bf16[128,2048]{1,0:T(8,128)(2,1)S(1)} collective-permute-done((bf16[128,2048]{1,0:T(8,128)(2,1)S(1)}, bf16[128,2048]{1,0:T(8,128)(2,1)S(1)}, u32[]{:S(2)}, u32[]{:S(2)}) %collective-permute-start.13) | collective-permute-done | bytes 524320 | tf_op jit(solution)/shard_map/ppermute | solution.py:451
  534.8 20.3 %collective-permute-done.38 = bf16[128,2048]{1,0:T(8,128)(2,1)S(1)} collective-permute-done((bf16[128,2048]{1,0:T(8,128)(2,1)S(1)}, bf16[128,2048]{1,0:T(8,128)(2,1)S(1)}, u32[]{:S(2)}, u32[]{:S(2)}) %collective-permute-start.38) | collective-permute-done | bytes 524320 | tf_op jit(solution)/shard_map/ppermute | solution.py:451
  561.0 5.6 fusion.1
  566.6 10.0 %fusion.3 = bf16[4,768,768]{1,2,0:T(8,128)(2,1)} fusion(f32[768,768,4]{1,0,2:T(8,128)} %get-tuple-element.98, f32[4,768]{1,0:T(4,128)S(1)} %get-tuple-element.97, f32[4,768,768]{1,2,0:T(8,128)} %get-tuple-element.96, f32[4,768]{1,0:T(4,128)S(1)} %copy-done.61), kind=kLoop, calls=%fused_computation.6 | loop fusion | flops 11796480 | bytes 23617536 | tf_op jit(solution)/shard_map/convert_element_type | solution.py:746
  576.7 4.0 convolution_bitcast_fusion.1
  583.2 4.7 multiply_reduce_fusion.1
  589.1 4.2 copy-done.5
  595.8 21.0 %pad_maximum_fusion = bf16[2048,3072]{0,1:T(8,128)(2,1)} fusion(bf16[2048,1024]{0,1:T(8,128)(2,1)S(1)} %copy-done.15, bf16[2048,1024]{0,1:T(8,128)(2,1)S(1)} %copy-done.13, bf16[2048,1024]{0,1:T(8,128)(2,1)S(1)} %copy-done.14), kind=kLoop, calls=%fused_computation.1 | loop fusion | flops 37748736 | bytes 25165824 | tf_op jit(solution)/shard_map/concatenate | solution.py:733
  616.8 16.9 %copy.73 = bf16[2048,3072]{1,0:T(8,128)(2,1)} copy(bf16[2048,3072]{0,1:T(8,128)(2,1)} %pad_maximum_fusion) | data formatting | bytes 25165824 | tf_op jit(solution)/shard_map/concatenate | solution.py:733
  646.8 5.8 fusion.12
  652.6 4.8 copy.74
  657.4 11.4 %collective-permute-done.49 = f32[2,2048]{1,0:T(2,128)} collective-permute-done((f32[2,2048]{1,0:T(2,128)}, f32[2,2048]{1,0:T(2,128)}, u32[]{:S(2)}, u32[]{:S(2)}) %collective-permute-start.49) | collective-permute-done | bytes 16416 | tf_op jit(solution)/shard_map/ppermute | solution.py:451
  679.7 136.7 %shard_map.204 = (f32[128,4096]{1,0:T(8,128)}, f32[128,4096]{1,0:T(8,128)}, f32[128,4096]{1,0:T(8,128)}, f32[128,1024]{1,0:T(8,128)}, f32[128,256]{1,0:T(8,128)}...) custom-call(bf16[4,4,128,3072]{3,2,1,0:T(8,128)(2,1)} %bitcast.246, bf16[4,4,128,640]{3,2,1,0:T(8,128)(2,1)} %pad_maximum_fusion.2.at), custom_call_target="tpu_custom_call" | custom-call | tf_op jit(solution)/shard_map/pallas_call | solution.py:572
  (412 shorter events, 188.2 us)
Async XLA Ops:
  238.5 46.9 %collective-permute-start = (bf16[4,128,2048]{2,1,0:T(8,128)(2,1)S(1)}, bf16[4,128,2048]{2,1,0:T(8,128)(2,1)}, u32[]{:S(2)}, u32[]{:S(2)}) collective-permute-start(bf16[4,128,2048]{2,1,0:T(8,128)(2,1)S(1)} %fusion.18), channel_id=1, source_target_pairs={{0,1},{1,0},{2,3},{3,2},{4,5},{5,4},{6,7},{7,6},{8,9},{9,8},{10,11... | collective-permute-start | bytes 6291464 | tf_op jit(solution)/shard_map/ppermute | solution.py:451
  240.9 33.1 %collective-permute-start.22 = (bf16[128,2048]{1,0:T(8,128)(2,1)}, bf16[128,2048]{1,0:T(8,128)(2,1)}, u32[]{:S(2)}, u32[]{:S(2)}) collective-permute-start(bf16[128,2048]{1,0:T(8,128)(2,1)} %get-tuple-element.44), channel_id=1, source_target_pairs={{0,8},{8,0},{16,24},{24,16},{1,9},{9,1},{17,25},{25,17},{2,10},{10... | collective-permute-start | bytes 1572872 | tf_op jit(solution)/shard_map/ppermute | solution.py:451
  249.9 26.5 %collective-permute-start.26 = (bf16[128,2048]{1,0:T(8,128)(2,1)}, bf16[128,2048]{1,0:T(8,128)(2,1)}, u32[]{:S(2)}, u32[]{:S(2)}) collective-permute-start(bf16[128,2048]{1,0:T(8,128)(2,1)} %get-tuple-element.44), channel_id=1, source_target_pairs={{0,16},{8,24},{16,0},{24,8},{1,17},{9,25},{17,1},{25,9},{2,18},{10... | collective-permute-start | bytes 1572872 | tf_op jit(solution)/shard_map/ppermute | solution.py:451
  251.0 25.4 %collective-permute-start.20 = (bf16[128,2048]{1,0:T(8,128)(2,1)}, bf16[128,2048]{1,0:T(8,128)(2,1)}, u32[]{:S(2)}, u32[]{:S(2)}) collective-permute-start(bf16[128,2048]{1,0:T(8,128)(2,1)} %get-tuple-element.44), channel_id=1, source_target_pairs={{0,1},{1,0},{2,3},{3,2},{4,5},{5,4},{6,7},{7,6},{8,9},{9,8},{10,11... | collective-permute-start | bytes 1572872 | tf_op jit(solution)/shard_map/ppermute | solution.py:451
  290.1 25.4 %collective-permute-start.2 = (bf16[128,2048]{1,0:T(8,128)(2,1)S(1)}, bf16[128,2048]{1,0:T(8,128)(2,1)S(1)}, u32[]{:S(2)}, u32[]{:S(2)}) collective-permute-start(bf16[128,2048]{1,0:T(8,128)(2,1)S(1)} %get-tuple-element.60), channel_id=1, source_target_pairs={{0,4},{2,6},{4,0},{6,2},{1,5},{3,7},{5,1},{7,3},{8,12},{10,14},{12... | collective-permute-start | bytes 1572872 | tf_op jit(solution)/shard_map/ppermute | solution.py:451
  296.0 38.2 %collective-permute-start.32 = (bf16[128,2048]{1,0:T(8,128)(2,1)}, bf16[128,2048]{1,0:T(8,128)(2,1)S(1)}, u32[]{:S(2)}, u32[]{:S(2)}) collective-permute-start(bf16[128,2048]{1,0:T(8,128)(2,1)} %get-tuple-element.42), channel_id=1, source_target_pairs={{0,1},{1,0},{2,3},{3,2},{4,5},{5,4},{6,7},{7,6},{8,9},{9,8},{10,11... | collective-permute-start | bytes 1572872 | tf_op jit(solution)/shard_map/ppermute | solution.py:451
  335.0 25.8 %collective-permute-start.6 = (bf16[128,2048]{1,0:T(8,128)(2,1)S(1)}, bf16[128,2048]{1,0:T(8,128)(2,1)S(1)}, u32[]{:S(2)}, u32[]{:S(2)}) collective-permute-start(bf16[128,2048]{1,0:T(8,128)(2,1)S(1)} %get-tuple-element.40), channel_id=1, source_target_pairs={{0,8},{8,0},{16,24},{24,16},{1,9},{9,1},{17,25},{25,17},{2,10},{10... | collective-permute-start | bytes 1572872 | tf_op jit(solution)/shard_map/ppermute | solution.py:451
  337.4 27.0 %collective-permute-start.10 = (bf16[128,2048]{1,0:T(8,128)(2,1)S(1)}, bf16[128,2048]{1,0:T(8,128)(2,1)S(1)}, u32[]{:S(2)}, u32[]{:S(2)}) collective-permute-start(bf16[128,2048]{1,0:T(8,128)(2,1)S(1)} %get-tuple-element.40), channel_id=1, source_target_pairs={{0,16},{8,24},{16,0},{24,8},{1,17},{9,25},{17,1},{25,9},{2,18},{10... | collective-permute-start | bytes 1572872 | tf_op jit(solution)/shard_map/ppermute | solution.py:451
  338.5 31.6 %collective-permute-start.14 = (bf16[128,2048]{1,0:T(8,128)(2,1)S(1)}, bf16[128,2048]{1,0:T(8,128)(2,1)S(1)}, u32[]{:S(2)}, u32[]{:S(2)}) collective-permute-start(bf16[128,2048]{1,0:T(8,128)(2,1)S(1)} %get-tuple-element.40), channel_id=1, source_target_pairs={{8,16},{16,8},{9,17},{17,9},{10,18},{18,10},{11,19},{19,11},{12,20... | collective-permute-start | bytes 1572872 | tf_op jit(solution)/shard_map/ppermute | solution.py:473
  363.2 91.5 %collective-permute-start.21 = (bf16[128,2048]{1,0:T(8,128)(2,1)S(1)}, bf16[128,2048]{1,0:T(8,128)(2,1)S(1)}, u32[]{:S(2)}, u32[]{:S(2)}) collective-permute-start(bf16[128,2048]{1,0:T(8,128)(2,1)S(1)} %slice.389), channel_id=1, source_target_pairs={{0,1},{1,0},{2,3},{3,2},{4,5},{5,4},{6,7},{7,6},{8,9},{9,8},{10,11... | collective-permute-start | bytes 1572872 | tf_op jit(solution)/shard_map/ppermute | solution.py:451
  387.9 56.4 %collective-permute-start.12 = (bf16[128,2048]{1,0:T(8,128)(2,1)S(1)}, bf16[128,2048]{1,0:T(8,128)(2,1)}, u32[]{:S(2)}, u32[]{:S(2)}) collective-permute-start(bf16[128,2048]{1,0:T(8,128)(2,1)S(1)} %slice.391), channel_id=1, source_target_pairs={{0,1},{1,0},{2,3},{3,2},{4,5},{5,4},{6,7},{7,6},{8,9},{9,8},{10,11... | collective-permute-start | bytes 1572872 | tf_op jit(solution)/shard_map/ppermute | solution.py:451
  396.6 55.3 %collective-permute-start.8 = (bf16[128,2048]{1,0:T(8,128)(2,1)}, bf16[128,2048]{1,0:T(8,128)(2,1)}, u32[]{:S(2)}, u32[]{:S(2)}) collective-permute-start(bf16[128,2048]{1,0:T(8,128)(2,1)} %slice.392), channel_id=1, source_target_pairs={{0,1},{1,0},{2,3},{3,2},{4,5},{5,4},{6,7},{7,6},{8,9},{9,8},{10,11... | collective-permute-start | bytes 1572872 | tf_op jit(solution)/shard_map/ppermute | solution.py:451
  399.9 46.2 %collective-permute-start.28 = (bf16[128,2048]{1,0:T(8,128)(2,1)}, bf16[128,2048]{1,0:T(8,128)(2,1)}, u32[]{:S(2)}, u32[]{:S(2)}) collective-permute-start(bf16[128,2048]{1,0:T(8,128)(2,1)} %slice.387), channel_id=1, source_target_pairs={{0,1},{1,0},{2,3},{3,2},{4,5},{5,4},{6,7},{7,6},{8,9},{9,8},{10,11... | collective-permute-start | bytes 1572872 | tf_op jit(solution)/shard_map/ppermute | solution.py:451
  404.3 43.1 %collective-permute-start.24 = (bf16[128,2048]{1,0:T(8,128)(2,1)S(1)}, bf16[128,2048]{1,0:T(8,128)(2,1)}, u32[]{:S(2)}, u32[]{:S(2)}) collective-permute-start(bf16[128,2048]{1,0:T(8,128)(2,1)S(1)} %slice.388), channel_id=1, source_target_pairs={{0,1},{1,0},{2,3},{3,2},{4,5},{5,4},{6,7},{7,6},{8,9},{9,8},{10,11... | collective-permute-start | bytes 1572872 | tf_op jit(solution)/shard_map/ppermute | solution.py:451
  447.4 26.8 %collective-permute-start.29 = (bf16[128,2048]{1,0:T(8,128)(2,1)S(1)}, bf16[128,2048]{1,0:T(8,128)(2,1)S(1)}, u32[]{:S(2)}, u32[]{:S(2)}) collective-permute-start(bf16[128,2048]{1,0:T(8,128)(2,1)S(1)} %fusion.59), channel_id=1, source_target_pairs={{0,16},{8,24},{16,0},{24,8},{1,17},{9,25},{17,1},{25,9},{2,18},{10... | collective-permute-start | bytes 1572872 | tf_op jit(solution)/shard_map/ppermute | solution.py:451
  449.3 37.7 %collective-permute-start.25 = (bf16[128,2048]{1,0:T(8,128)(2,1)S(1)}, bf16[128,2048]{1,0:T(8,128)(2,1)S(1)}, u32[]{:S(2)}, u32[]{:S(2)}) collective-permute-start(bf16[128,2048]{1,0:T(8,128)(2,1)S(1)} %fusion.60), channel_id=1, source_target_pairs={{0,8},{8,0},{16,24},{24,16},{1,9},{9,1},{17,25},{25,17},{2,10},{10... | collective-permute-start | bytes 1572872 | tf_op jit(solution)/shard_map/ppermute | solution.py:451
  451.9 36.6 %collective-permute-start.34 = (bf16[128,2048]{1,0:T(8,128)(2,1)S(1)}, bf16[128,2048]{1,0:T(8,128)(2,1)S(1)}, u32[]{:S(2)}, u32[]{:S(2)}) collective-permute-start(bf16[128,2048]{1,0:T(8,128)(2,1)S(1)} %fusion.58), channel_id=1, source_target_pairs={{0,24},{8,16},{16,8},{24,0},{1,25},{9,17},{17,9},{25,1},{2,26},{10... | collective-permute-start | bytes 1572872 | tf_op jit(solution)/shard_map/ppermute | solution.py:451
  454.4 35.8 %collective-permute-start.5 = (bf16[128,2048]{1,0:T(8,128)(2,1)}, bf16[128,2048]{1,0:T(8,128)(2,1)S(1)}, u32[]{:S(2)}, u32[]{:S(2)}) collective-permute-start(bf16[128,2048]{1,0:T(8,128)(2,1)} %slice.393), channel_id=1, source_target_pairs={{0,1},{1,0},{2,3},{3,2},{4,5},{5,4},{6,7},{7,6},{8,9},{9,8},{10,11... | collective-permute-start | bytes 1572872 | tf_op jit(solution)/shard_map/ppermute | solution.py:451
  454.7 75.4 %collective-permute-start.13 = (bf16[128,2048]{1,0:T(8,128)(2,1)S(1)}, bf16[128,2048]{1,0:T(8,128)(2,1)S(1)}, u32[]{:S(2)}, u32[]{:S(2)}) collective-permute-start(bf16[128,2048]{1,0:T(8,128)(2,1)S(1)} %fusion.65), channel_id=1, source_target_pairs={{0,16},{8,24},{16,0},{24,8},{1,17},{9,25},{17,1},{25,9},{2,18},{10... | collective-permute-start | bytes 1572872 | tf_op jit(solution)/shard_map/ppermute | solution.py:451
  474.2 57.3 %collective-permute-start.9 = (bf16[128,2048]{1,0:T(8,128)(2,1)S(1)}, bf16[128,2048]{1,0:T(8,128)(2,1)S(1)}, u32[]{:S(2)}, u32[]{:S(2)}) collective-permute-start(bf16[128,2048]{1,0:T(8,128)(2,1)S(1)} %fusion.66), channel_id=1, source_target_pairs={{0,8},{8,0},{16,24},{24,16},{1,9},{9,1},{17,25},{25,17},{2,10},{10... | collective-permute-start | bytes 1572872 | tf_op jit(solution)/shard_map/ppermute | solution.py:451
  487.0 46.0 %collective-permute-start.18 = (bf16[128,2048]{1,0:T(8,128)(2,1)S(1)}, bf16[128,2048]{1,0:T(8,128)(2,1)S(1)}, u32[]{:S(2)}, u32[]{:S(2)}) collective-permute-start(bf16[128,2048]{1,0:T(8,128)(2,1)S(1)} %fusion.64), channel_id=1, source_target_pairs={{0,24},{8,16},{16,8},{24,0},{1,25},{9,17},{17,9},{25,1},{2,26},{10... | collective-permute-start | bytes 1572872 | tf_op jit(solution)/shard_map/ppermute | solution.py:451
  490.2 65.5 %collective-permute-start.35 = (bf16[128,2048]{1,0:T(8,128)(2,1)S(1)}, bf16[128,2048]{1,0:T(8,128)(2,1)S(1)}, u32[]{:S(2)}, u32[]{:S(2)}) collective-permute-start(bf16[128,2048]{1,0:T(8,128)(2,1)S(1)} %get-tuple-element.48), channel_id=1, source_target_pairs={{0,1},{1,0},{2,3},{3,2},{4,5},{5,4},{6,7},{7,6},{8,9},{9,8},{10,11... | collective-permute-start | bytes 1572872 | tf_op jit(solution)/shard_map/ppermute | solution.py:451
  490.3 44.1 %collective-permute-start.36 = (bf16[128,2048]{1,0:T(8,128)(2,1)S(1)}, bf16[128,2048]{1,0:T(8,128)(2,1)S(1)}, u32[]{:S(2)}, u32[]{:S(2)}) collective-permute-start(bf16[128,2048]{1,0:T(8,128)(2,1)S(1)} %get-tuple-element.48), channel_id=1, source_target_pairs={{0,2},{2,0},{4,6},{6,4},{1,3},{3,1},{5,7},{7,5},{8,10},{10,8},{12,... | collective-permute-start | bytes 1572872 | tf_op jit(solution)/shard_map/ppermute | solution.py:451
  530.1 25.1 %collective-permute-start.38 = (bf16[128,2048]{1,0:T(8,128)(2,1)S(1)}, bf16[128,2048]{1,0:T(8,128)(2,1)S(1)}, u32[]{:S(2)}, u32[]{:S(2)}) collective-permute-start(bf16[128,2048]{1,0:T(8,128)(2,1)S(1)} %get-tuple-element.48), channel_id=1, source_target_pairs={{0,4},{2,6},{4,0},{6,2},{1,5},{3,7},{5,1},{7,3},{8,12},{10,14},{12... | collective-permute-start | bytes 1572872 | tf_op jit(solution)/shard_map/ppermute | solution.py:451
  531.5 23.7 %collective-permute-start.40 = (bf16[128,2048]{1,0:T(8,128)(2,1)S(1)}, bf16[128,2048]{1,0:T(8,128)(2,1)S(1)}, u32[]{:S(2)}, u32[]{:S(2)}) collective-permute-start(bf16[128,2048]{1,0:T(8,128)(2,1)S(1)} %get-tuple-element.48), channel_id=1, source_target_pairs={{0,6},{2,4},{4,2},{6,0},{1,7},{3,5},{5,3},{7,1},{8,14},{10,12},{12... | collective-permute-start | bytes 1572872 | tf_op jit(solution)/shard_map/ppermute | solution.py:451
  534.3 99.6 %collective-permute-start.19 = (bf16[128,2048]{1,0:T(8,128)(2,1)}, bf16[128,2048]{1,0:T(8,128)(2,1)}, u32[]{:S(2)}, u32[]{:S(2)}) collective-permute-start(bf16[128,2048]{1,0:T(8,128)(2,1)} %get-tuple-element.52), channel_id=1, source_target_pairs={{0,1},{1,0},{2,3},{3,2},{4,5},{5,4},{6,7},{7,6},{8,9},{9,8},{10,11... | collective-permute-start | bytes 1572872 | tf_op jit(solution)/shard_map/ppermute | solution.py:451
  593.6 43.7 %collective-permute-start.42 = (bf16[4,128,2048]{2,1,0:T(8,128)(2,1)S(1)}, bf16[4,128,2048]{2,1,0:T(8,128)(2,1)}, u32[]{:S(2)}, u32[]{:S(2)}) collective-permute-start(bf16[4,128,2048]{2,1,0:T(8,128)(2,1)S(1)} %fusion.19), channel_id=1, source_target_pairs={{0,1},{1,0},{2,3},{3,2},{4,5},{5,4},{6,7},{7,6},{8,9},{9,8},{10,11... | collective-permute-start | bytes 6291464 | tf_op jit(solution)/shard_map/ppermute | solution.py:451
  642.1 27.6 %collective-permute-start.45 = (bf16[128,2048]{1,0:T(8,128)(2,1)}, bf16[128,2048]{1,0:T(8,128)(2,1)S(1)}, u32[]{:S(2)}, u32[]{:S(2)}) collective-permute-start(bf16[128,2048]{1,0:T(8,128)(2,1)} %get-tuple-element.56), channel_id=1, source_target_pairs={{0,6},{2,4},{4,2},{6,0},{1,7},{3,5},{5,3},{7,1},{8,14},{10,12},{12... | collective-permute-start | bytes 1572872 | tf_op jit(solution)/shard_map/ppermute | solution.py:451
  643.6 26.1 %collective-permute-start.44 = (bf16[128,2048]{1,0:T(8,128)(2,1)}, bf16[128,2048]{1,0:T(8,128)(2,1)S(1)}, u32[]{:S(2)}, u32[]{:S(2)}) collective-permute-start(bf16[128,2048]{1,0:T(8,128)(2,1)} %get-tuple-element.57), channel_id=1, source_target_pairs={{0,4},{2,6},{4,0},{6,2},{1,5},{3,7},{5,1},{7,3},{8,12},{10,14},{12... | collective-permute-start | bytes 1572872 | tf_op jit(solution)/shard_map/ppermute | solution.py:451
  644.2 25.5 %collective-permute-start.43 = (bf16[128,2048]{1,0:T(8,128)(2,1)}, bf16[128,2048]{1,0:T(8,128)(2,1)}, u32[]{:S(2)}, u32[]{:S(2)}) collective-permute-start(bf16[128,2048]{1,0:T(8,128)(2,1)} %get-tuple-element.55), channel_id=1, source_target_pairs={{0,2},{2,0},{4,6},{6,4},{1,3},{3,1},{5,7},{7,5},{8,10},{10,8},{12,... | collective-permute-start | bytes 1572872 | tf_op jit(solution)/shard_map/ppermute | solution.py:451
  674.7 142.3 %collective-permute-start.46 = (bf16[128,2048]{1,0:T(8,128)(2,1)}, bf16[128,2048]{1,0:T(8,128)(2,1)S(1)}, u32[]{:S(2)}, u32[]{:S(2)}) collective-permute-start(bf16[128,2048]{1,0:T(8,128)(2,1)} %get-tuple-element.46), channel_id=1, source_target_pairs={{0,1},{1,0},{2,3},{3,2},{4,5},{5,4},{6,7},{7,6},{8,9},{9,8},{10,11... | collective-permute-start | bytes 1572872 | tf_op jit(solution)/shard_map/ppermute | solution.py:451
  675.8 140.6 %collective-permute-start.51 = (f32[2,2048]{1,0:T(2,128)S(1)}, f32[2,2048]{1,0:T(2,128)S(1)}, u32[]{:S(2)}, u32[]{:S(2)}) collective-permute-start(f32[2,2048]{1,0:T(2,128)S(1)} %add.282), channel_id=1, source_target_pairs={{0,16},{8,24},{16,0},{24,8},{1,17},{9,25},{17,1},{25,9},{2,18},{10... | collective-permute-start | bytes 49160 | tf_op jit(solution)/shard_map/ppermute | solution.py:451
  (106 other events, 1123.8 us)

commit v3 on v2

--- a/solution.py
+++ b/solution.py
@@ -447,6 +447,173 @@
     )(wa, wf, xt, gain)
 
 
+def dot_tile(left, right, left_axis, right_axis):
+    return lax.dot_general(left, right, (((left_axis,), (right_axis,)), ((), ())), preferred_element_type=jnp.float32)
+
+
+TILE = 256
+
+
+def feed_kernel(
+    x, fg, w, back, feed_own, feed_send, terms,
+    xs, wv, gate_g, up_g, inner, mine, cross, crossed, totals, landed, send, receive, local,
+):
+    f32, bf16 = jnp.float32, jnp.bfloat16
+    z, c, t = (lax.axis_index(a) for a in (FSDP, CONTEXT, TENSOR))
+    core = (z, c, 1 - t)
+    greet([(flip(z, k), c, t) for k in (1, 2, 3)] + [core])
+    net = Copies(send, receive)
+    part, width = x.shape
+    hidden = wv.shape[1] // 3
+    load = pltpu.make_async_copy(w, wv, local.at[0])
+    load.start()
+    middle = (z == 1) | (z == 2)
+    swaps = {0: net.start(x, xs.at[0, 1], core)}
+    arrive = {2: net.start(x, xs.at[2, 0], (flip(z, 2), c, t))}
+    three = net.index()
+    direct = net.make(three, x, xs.at[3, 0], (3 - z, c, t))
+    pl.when(middle)(direct.start)
+    arrive[3] = direct
+    arrive[1] = net.start(x, xs.at[1, 0], (flip(z, 1), c, t))
+    passed = pltpu.make_async_remote_copy(
+        src_ref=xs.at[2, 0],
+        dst_ref=xs.at[3, 0],
+        send_sem=send.at[net.index()],
+        recv_sem=receive.at[three],
+        device_id=(flip(z, 1), c, t),
+        device_id_type=pl.DeviceIdType.MESH,
+    )
+    xs[0, 0] = x[...]
+    load.wait()
+
+    def first(k):
+        swaps[k].wait_recv()
+        rows = xs[k].reshape(2 * part, width)
+        grads = fg[k]
+
+        def step(n, carry):
+            at = pl.multiple_of(n * TILE, TILE)
+            g = dot_tile(rows, wv[:, pl.ds(at, TILE)], 1, 0)
+            u = dot_tile(rows, wv[:, pl.ds(hidden + at, TILE)], 1, 0)
+            d = dot_tile(grads, wv[:, pl.ds(2 * hidden + at, TILE)], 1, 0)
+            sig = jax.nn.sigmoid(g)
+            here = pl.ds(at, TILE)
+            inner[k, :, here] = (g * sig * u).astype(bf16)
+            gate_g[k, :, here] = (d * u * sig * (1.0 + g * (1.0 - sig))).astype(bf16)
+            up_g[k, :, here] = (d * g * sig).astype(bf16)
+            return carry
+
+        lax.fori_loop(0, hidden // TILE, step, 0)
+
+    crosses = {}
+
+    def second(k):
+        def step(n, carry):
+            here = pl.ds(pl.multiple_of(n * TILE, TILE), TILE)
+            b = dot_tile(gate_g[k], wv[here, 0:hidden], 1, 1) + dot_tile(up_g[k], wv[here, hidden : 2 * hidden], 1, 1)
+            f = dot_tile(inner[k], wv[here, 2 * hidden :], 1, 1)
+            mine[k, 0, :, here] = b[:part]
+            mine[k, 1, :, here] = f[:part]
+            cross[k, 0, :, here] = b[part:].astype(bf16)
+            cross[k, 1, :, here] = f[part:].astype(bf16)
+            return carry
+
+        lax.fori_loop(0, width // TILE, step, 0)
+        crosses[k] = net.start(cross.at[k], crossed.at[k], core)
+
+    sums = {}
+
+    def finish(k):
+        crosses[k].wait_recv()
+        if k:
+            totals[k - 1] = (mine[k, 0] + crossed[k, 0].astype(f32)).astype(bf16)
+            sums[k] = net.start(totals.at[k - 1], landed.at[k - 1], (flip(z, k), c, t))
+            feed_send[k - 1] = (mine[k, 1] + crossed[k, 1].astype(f32)).astype(bf16)
+        else:
+            back[...] = mine[0, 0] + crossed[0, 0].astype(f32)
+            feed_own[...] = mine[0, 1] + crossed[0, 1].astype(f32)
+
+    def fetch(k):
+        arrive[k].wait_recv()
+        if k == 2:
+            pl.when(middle)(passed.start)
+        swaps[k] = net.start(xs.at[k, 0], xs.at[k, 1], core)
+
+    order = (0, 2, 3, 1)
+    for i, k in enumerate(order):
+        first(k)
+        if i:
+            finish(order[i - 1])
+        if i < 3:
+            fetch(order[i + 1])
+        second(k)
+
+    rows = xs.shape[0] * 2 * part
+
+    def term(source, grads, begin):
+        def step(m, carry):
+            here = pl.ds(pl.multiple_of(m * TILE, TILE), TILE)
+            left = source[:, :, here].reshape(rows, TILE)
+            value = dot_tile(left, grads[...].reshape(rows, hidden), 0, 0)
+            wv[here, begin : begin + hidden] = value.astype(bf16)
+            return carry
+
+        lax.fori_loop(0, width // TILE, step, 0)
+
+    flat = xs.reshape(xs.shape[0], 2 * part, width)
+    term(flat, gate_g, 0)
+    finish(order[3])
+    term(flat, up_g, hidden)
+    term(fg, inner, 2 * hidden)
+    store = pltpu.make_async_copy(wv, terms, local.at[1])
+    store.start()
+    for k in (1, 2, 3):
+        sums[k].wait_recv()
+    back[...] = back[...] + landed[0].astype(f32) + landed[1].astype(f32) + landed[2].astype(f32)
+    pl.when(middle)(direct.wait_send)
+    pl.when(middle)(passed.wait_send)
+    for copy in net.started:
+        copy.wait_send()
+    store.wait()
+
+
+def feed_forward(x, fg, w):
+    bf16, f32 = jnp.bfloat16, jnp.float32
+    part, width = x.shape
+    cols = w.shape[1]
+    hidden = cols // 3
+    blocks = fg.shape[0]
+    copies = 20
+    vmem, anywhere = pl.BlockSpec(memory_space=pltpu.VMEM), pl.BlockSpec(memory_space=pl.ANY)
+    return pl.pallas_call(
+        feed_kernel,
+        out_shape=[
+            jax.ShapeDtypeStruct((part, width), f32),
+            jax.ShapeDtypeStruct((part, width), f32),
+            jax.ShapeDtypeStruct((blocks - 1, part, width), bf16),
+            jax.ShapeDtypeStruct(w.shape, bf16),
+        ],
+        in_specs=[vmem, vmem, anywhere],
+        out_specs=[vmem, vmem, vmem, anywhere],
+        scratch_shapes=[
+            pltpu.VMEM((blocks, 2, part, width), bf16),
+            pltpu.VMEM(w.shape, bf16),
+            pltpu.VMEM((blocks, 2 * part, hidden), bf16),
+            pltpu.VMEM((blocks, 2 * part, hidden), bf16),
+            pltpu.VMEM((blocks, 2 * part, hidden), bf16),
+            pltpu.VMEM((blocks, 2, part, width), f32),
+            pltpu.VMEM((blocks, 2, part, width), bf16),
+            pltpu.VMEM((blocks, 2, part, width), bf16),
+            pltpu.VMEM((blocks - 1, part, width), bf16),
+            pltpu.VMEM((blocks - 1, part, width), bf16),
+            pltpu.SemaphoreType.DMA((copies,)),
+            pltpu.SemaphoreType.DMA((copies,)),
+            pltpu.SemaphoreType.DMA((2,)),
+        ],
+        compiler_params=pltpu.CompilerParams(collective_id=3, has_side_effects=True, vmem_limit_bytes=62 * 2**20),
+    )(x, fg, w)
+
+
 def swap(x, axis, k):
     return lax.ppermute(x, axis, [(i, i ^ k) for i in range(lax.axis_size(axis))])
 
@@ -484,8 +651,8 @@
 
 
 def grads_out_kernel(
-    ff, at, gate_out, up_out, down_out, query_out, key_out, value_out, output_out,
-    terms, corner_x, corner_y, side_x, side_y, landed, at_terms, at_in, at_total, at_landed, send, receive, local,
+    ff, at, fs, feed_out, gate_out, up_out, down_out, query_out, key_out, value_out, output_out,
+    terms, corner_x, corner_y, side_x, side_y, landed, feed_in, at_terms, at_in, at_total, at_landed, send, receive, local,
 ):
     f32, bf16 = jnp.float32, jnp.bfloat16
     z, c, t = (lax.axis_index(a) for a in (FSDP, CONTEXT, TENSOR))
@@ -503,6 +670,7 @@
     attn_load.start()
     attn_load.wait()
     attn_in = [net.start(at_terms.at[flip(z, k)], at_in.at[k - 1], (flip(z, k), c, t)) for k in (3, 2, 1)]
+    feed = [net.start(fs.at[k - 1], feed_in.at[k - 1], (flip(z, k), c, t)) for k in (3, 2, 1)]
     first = {}
     for k in order:
         zs = flip(z, k)
@@ -551,29 +719,32 @@
         zs = flip(z, k)
         columns = pl.ds(pl.multiple_of(zs * size, size), size)
         for i, out in enumerate((gate_out, up_out, down_out)):
-            out[:, columns] = landed[k, :, i * size : (i + 1) * size].astype(f32)
+            out[:, columns] = landed[k, :, i * size : (i + 1) * size]
     for copy in attn_out:
         copy.wait_recv()
     begin = 0
     for out in (query_out, key_out, value_out, output_out):
         size = out.shape[1] // 4
         for j in range(4):
-            out[:, j * size : (j + 1) * size] = at_landed[j, :, begin : begin + size].astype(f32)
+            out[:, j * size : (j + 1) * size] = at_landed[j, :, begin : begin + size]
         begin += size
+    for copy in feed:
+        copy.wait_recv()
+    feed_out[...] = feed_in[0].astype(f32) + feed_in[1].astype(f32) + feed_in[2].astype(f32)
     for copy in net.started:
         copy.wait_send()
 
 
-def grads_out(ff, at, sizes):
+def grads_out(ff, at, fs, sizes):
     bf16, f32 = jnp.bfloat16, jnp.float32
     rows, cols = ff.shape[2:]
     attn_cols = at.shape[3]
     copies = 32
     return pl.pallas_call(
         grads_out_kernel,
-        out_shape=[jax.ShapeDtypeStruct((rows, s), f32) for s in sizes],
-        in_specs=[pl.BlockSpec(memory_space=pl.ANY)] * 2,
-        out_specs=[pl.BlockSpec(memory_space=pltpu.VMEM)] * len(sizes),
+        out_shape=[jax.ShapeDtypeStruct(fs.shape[1:], f32)] + [jax.ShapeDtypeStruct((rows, s), bf16) for s in sizes],
+        in_specs=[pl.BlockSpec(memory_space=pl.ANY)] * 2 + [pl.BlockSpec(memory_space=pltpu.VMEM)],
+        out_specs=[pl.BlockSpec(memory_space=pltpu.VMEM)] * (1 + len(sizes)),
         scratch_shapes=[
             pltpu.VMEM((4, 4, rows, cols), bf16),
             pltpu.VMEM((4, rows // 2, cols), bf16),
@@ -581,6 +752,7 @@
             pltpu.VMEM((4, rows, cols), bf16),
             pltpu.VMEM((4, rows, cols), bf16),
             pltpu.VMEM((4, rows, cols), bf16),
+            pltpu.VMEM(fs.shape, bf16),
             pltpu.VMEM((4, 4, rows, attn_cols), bf16),
             pltpu.VMEM((3, 4, rows, attn_cols), bf16),
             pltpu.VMEM((4, rows, attn_cols), bf16),
@@ -590,7 +762,7 @@
             pltpu.SemaphoreType.DMA((5,)),
         ],
         compiler_params=pltpu.CompilerParams(collective_id=2, has_side_effects=True, vmem_limit_bytes=60 * 2**20),
-    )(ff, at)
+    )(ff, at, fs)
 
 
 def on_device_split(
@@ -642,8 +814,7 @@
     w_out = wa[..., qkv_cols:].reshape(width, q_cols)
     my_tokens = cut(tokens[0], t, part, 0)
     all_tokens = all_tokens.reshape(group_rows, width).astype(f32)
-    w_gate_up = wf[..., : 2 * ff_cols].reshape(width, 2 * ff_cols)
-    w_down = wf[..., 2 * ff_cols :].reshape(width, ff_cols)
+    w_feed = wf.reshape(width, 3 * ff_cols)
 
     my_valid = lax.dynamic_slice_in_dim(valid_rows, c * local_rows + t * part, part)
     cotangent = cut(out_grad[0], t, part, 0).astype(f32) * my_valid[:, None].astype(f32)
@@ -688,34 +859,15 @@
     inverse_two = lax.rsqrt(jnp.mean(hidden * hidden, axis=-1, keepdims=True) + norm_eps)
     unit_two = hidden * inverse_two
 
-    def scatter_block(partial, k):
-        mine = partial[:part] + swap(partial[part:].astype(bf16), TENSOR, 1).astype(f32)
-        return mine if k == 0 else swap(mine.astype(bf16), FSDP, k).astype(f32)
-
-    normed_blocks = [
-        jnp.concatenate([b, swap(b, TENSOR, 1)], axis=0) for b in fsdp_blocks((unit_two * gain_two).astype(bf16))
-    ]
-    inner_blocks, gate_blocks, up_blocks, back_parts, feed_parts = [], [], [], [], []
-    for k in range(nz):
-        gate_up = jnp.dot(normed_blocks[k], w_gate_up, preferred_element_type=f32)
-        gate_out, up_out = gate_up[:, :ff_cols], gate_up[:, ff_cols:]
-        inner_grad = jnp.dot(feed_grads[k], w_down, preferred_element_type=f32)
-        sig = jax.nn.sigmoid(gate_out)
-        inner_blocks.append((gate_out * sig * up_out).astype(bf16))
-        gate_blocks.append((inner_grad * up_out * sig * (1.0 + gate_out * (1.0 - sig))).astype(bf16))
-        up_blocks.append((inner_grad * gate_out * sig).astype(bf16))
-        both = jnp.concatenate([gate_blocks[k], up_blocks[k]], axis=1)
-        back_parts.append(scatter_block(dot_last(both, w_gate_up), k))
-        feed_parts.append(dot_last(inner_blocks[k], w_down))
-    normed_grad_two = sum(back_parts)
-    feed_out = sum(scatter_block(p, k) for k, p in enumerate(feed_parts))
-    output = (hidden + residual_mult * feed_out).astype(bf16)
+    normed_grad_two, feed_own, feed_send, ff_terms = feed_forward(
+        (unit_two * gain_two).astype(bf16), jnp.stack(feed_grads), w_feed
+    )
+    ff_terms = ff_terms.reshape(nz, nc, wrows, 3 * ff_cols)
 
     def both_cores(x):
         out = put(jnp.zeros((nt,) + x.shape, x.dtype), x, t)
         return put(out, swap(x, TENSOR, 1), 1 - t).reshape(1, local_rows, width)
 
-    output = both_cores(output)
     feed_gain_term = jnp.sum(normed_grad_two * unit_two, axis=0)
     hidden_grad = cotangent + norm_back(normed_grad_two, unit_two, gain_two, inverse_two)
 
@@ -728,16 +880,6 @@
         attn_grad = put(attn_grad, block, c ^ k, t)
         attn_grad = put(attn_grad, swap(block, TENSOR, 1), c ^ k, 1 - t)
     attn_grad = attn_grad.reshape(group_rows, width)[:filled]
-
-    normed_two = jnp.concatenate(normed_blocks, axis=0)
-    ff_terms = jnp.concatenate(
-        [
-            dot_first(normed_two, jnp.concatenate(gate_blocks, axis=0)).astype(bf16),
-            dot_first(normed_two, jnp.concatenate(up_blocks, axis=0)).astype(bf16),
-            dot_first(jnp.concatenate(feed_grads, axis=0), jnp.concatenate(inner_blocks, axis=0)).astype(bf16),
-        ],
-        axis=1,
-    ).reshape(nz, nc, wrows, 3 * ff_cols)
 
     out_term = dot_first(attn_grad, attended_f)
     mixed_grad = jnp.dot(attn_grad, w_out, preferred_element_type=f32).astype(bf16).reshape(filled, per_group, HEAD)
@@ -768,7 +910,9 @@
     terms = jnp.concatenate([qkv_term, out_term], axis=1).astype(bf16).reshape(nz, nc, wrows, -1)
     sizes = [w.shape[1] for w in (gate_weight, up_weight, down_weight)]
     sizes += [w.shape[1] for w in (query_weight, key_weight, value_weight, output_weight)]
-    grad_gate, grad_up, grad_down, *attn_terms = grads_out(ff_terms, terms, sizes)
+    feed_in, *weight_grads = grads_out(ff_terms, terms, feed_send, sizes)
+    grad_gate, grad_up, grad_down, *attn_terms = [g.astype(f32) for g in weight_grads]
+    output = both_cores((hidden + residual_mult * (feed_own + feed_in)).astype(bf16))
     return (output, input_grad, gain_terms[0], *attn_terms, gain_terms[1], grad_gate, grad_up, grad_down)
 
 

time: 839 us -> 743 us (0.89)
  Pallas kernels: 321 us -> 463 us
  waiting for transfers between devices: 168 us -> 91 us
  matrix products: 116 us -> 45.3 us
  local copies, waits for them, and re-layouts: 101 us -> 38.8 us
  starting transfers between devices: 45.2 us -> 28.5 us
  other arithmetic: 76.6 us -> 66.8 us
    pallas_call x1 -> x2, Pallas kernels: 137 us -> 279 us  [the longest x1 182 us: grads_out(): pl.pallas_call(grads_out_kernel, out_shape=[jax.ShapeDtypeStruct(fs.shape...]
    ppermute x48 -> x28, waiting for transfers between devices: 157 us -> 78.5 us  [swap(): lax.ppermute(x, axis, [(i, i ^ k) for i in range(lax.axis_size(axis))])]
    unnamed x196 -> x137, local copies, waits for them, and re-layouts: 45.3 us -> 17.1 us
    dot_general x5 -> x2, matrix products: 33.6 us -> 5.91 us  [dot_first(): lax.dot_general(left, right, (((0,), (0,)), ((), ())), preferred_element_...]
    dot_general x8 -> x0, matrix products: 25.7 us -> none  [the longest x4 12.9 us: on_device_split(): gate_up = jnp.dot(normed_blocks[k], w_gate_up, preferred_element_type=f32)]
    dot_general x10 -> x2, matrix products: 27.7 us -> 6.5 us  [dot_last(): lax.dot_general(left, right, (((1,), (1,)), ((), ())), preferred_element_...]
    concatenate x1 -> x0, other arithmetic: 21 us -> none  [on_device_split(): jnp.concatenate([dot_first(normed_two, jnp.concatenate(gate_blocks, axis=...]
    concatenate x3 -> x0, local copies, waits for them, and re-layouts: 18.6 us -> none  [the longest x1 16.9 us: on_device_split(): jnp.concatenate([dot_first(normed_two, jnp.concatenate(gate_blocks, axis=...]
  transfers between devices with their start and end apart: 52 -> 30, of which waited for: 15 -> 12; matrix products, arithmetic and copies ran while one was open for 26% -> 7% of each run, Pallas kernels for 16% -> 25%
where the time goes in v3:
time: 743 us; the launch traced here: 736 us
  Pallas kernels  463 us (62%)
  waiting for transfers between devices  91 us (12%)
  other arithmetic  66.8 us (9%)
  matrix products  45.3 us (6%)
  local copies, waits for them, and re-layouts  38.8 us (5%)
  starting transfers between devices  28.5 us (4%)
    pallas_call x1, Pallas kernels, weights_in(): pl.pallas_call(weights_in_kernel, out_shape=[jax.ShapeDtypeStruct(s, bf16...  185 us
    pallas_call x1, Pallas kernels, grads_out(): pl.pallas_call(grads_out_kernel, out_shape=[jax.ShapeDtypeStruct(fs.shape...  182 us
    pallas_call x1, Pallas kernels, feed_forward(): pl.pallas_call(feed_kernel, out_shape=[jax.ShapeDtypeStruct((part, width)...  96.4 us
    ppermute x28, waiting for transfers between devices, swap(): lax.ppermute(x, axis, [(i, i ^ k) for i in range(lax.axis_size(axis))])  78.5 us
    ppermute x28, starting transfers between devices, swap(): lax.ppermute(x, axis, [(i, i ^ k) for i in range(lax.axis_size(axis))])  25.7 us
    unnamed x137, local copies, waits for them, and re-layouts  17.1 us
  transfers between devices with their start and end apart: 30, of which 12 were waited for; matrix products, arithmetic and copies ran while one was open for 7% of the time, Pallas kernels for 25%

profile of v3, /device:TPU:0, one launch (start us, length us, event | category | flops | bytes accessed | tf_op | source)
XLA Modules:
  0.0 735.7 jit_solution(16425288523011835492)
XLA Ops:
  17.7 2.9 pad_maximum_fusion.1.wf
  20.7 184.5 %shard_map.203 = (bf16[4,4,128,640]{3,2,1,0:T(8,128)(2,1)S(1)}, bf16[4,4,128,3072]{3,2,1,0:T(8,128)(2,1)}, bf16[4,2,128,2048]{3,2,1,0:T(8,128)(2,1)}, bf16[4,4,16,128]{3,2,1,0:T(8,128)(2,1)S(1)}) custom-call(bf16[4,128,640]{2,1,0:T(8,128)(2,1)S(1)} %pad_maximum_fusion.4.wa, bf16[4,128,3072]{2,1,0:T(8,128)(2,1)} %pad_maximum_fusion.1.wf, ...), custom_call_target="tpu_custom_call" | custom-call | tf_op jit(solution)/shard_map/pallas_call | solution.py:436
  205.3 3.2 multiply_reduce_fusion
  209.9 2.8 fusion.83
  221.4 8.1 %fusion.84 = (f32[4,768]{1,0:T(4,128)S(1)}, f32[4,768,768]{1,2,0:T(8,128)}) fusion(pred[768,768]{0,1:T(8,128)(4,1)} %fusion.17, bf16[768,64,1]{0,1,2:T(8,128)(2,1)} %get-tuple-element.70, bf16[768,4,64]{0,2,1:T(8,128)(2,1)} %fusion.47), kind=kOutput, calls=%fused_computation.176 | convolution fusion | flops 311427840 | bytes 10530816 | tf_op jit(solution)/shard_map/sub | solution.py:838
  229.5 4.7 fusion.20
  235.2 4.6 fusion.85
  239.9 2.5 fusion.18
  245.0 2.0 fusion.39
  247.0 10.1 %collective-permute-start.7 = (bf16[128,2048]{1,0:T(8,128)(2,1)}, bf16[128,2048]{1,0:T(8,128)(2,1)}, u32[]{:S(2)}, u32[]{:S(2)}) collective-permute-start(bf16[128,2048]{1,0:T(8,128)(2,1)} %fusion.39), channel_id=1, source_target_pairs={{0,16},{8,24},{16,0},{24,8},{1,17},{9,25},{17,1},{25,9},{2,18},{10... | collective-permute-start | bytes 1572872 | tf_op jit(solution)/shard_map/ppermute | solution.py:618
  258.8 22.7 %collective-permute-done.7 = bf16[128,2048]{1,0:T(8,128)(2,1)} collective-permute-done((bf16[128,2048]{1,0:T(8,128)(2,1)}, bf16[128,2048]{1,0:T(8,128)(2,1)}, u32[]{:S(2)}, u32[]{:S(2)}) %collective-permute-start.7) | collective-permute-done | bytes 524320 | tf_op jit(solution)/shard_map/ppermute | solution.py:618
  284.7 12.6 %collective-permute-done.10 = bf16[128,2048]{1,0:T(8,128)(2,1)} collective-permute-done((bf16[128,2048]{1,0:T(8,128)(2,1)}, bf16[128,2048]{1,0:T(8,128)(2,1)}, u32[]{:S(2)}, u32[]{:S(2)}) %collective-permute-start.10) | collective-permute-done | bytes 524320 | tf_op jit(solution)/shard_map/ppermute | solution.py:640
  301.3 3.4 bitcast_add_fusion.1
  308.6 2.8 pad_maximum_fusion.fg
  311.4 8.4 %collective-permute-done.1 = bf16[128,2048]{1,0:T(8,128)(2,1)S(1)} collective-permute-done((bf16[128,2048]{1,0:T(8,128)(2,1)S(1)}, bf16[128,2048]{1,0:T(8,128)(2,1)S(1)}, u32[]{:S(2)}, u32[]{:S(2)}) %collective-permute-start.1) | collective-permute-done | bytes 524320 | tf_op jit(solution)/shard_map/ppermute | solution.py:618
  319.8 11.9 %collective-permute-done.2 = bf16[128,2048]{1,0:T(8,128)(2,1)S(1)} collective-permute-done((bf16[128,2048]{1,0:T(8,128)(2,1)S(1)}, bf16[128,2048]{1,0:T(8,128)(2,1)S(1)}, u32[]{:S(2)}, u32[]{:S(2)}) %collective-permute-start.2) | collective-permute-done | bytes 524320 | tf_op jit(solution)/shard_map/ppermute | solution.py:618
  334.8 96.4 %shard_map.204 = (f32[128,2048]{1,0:T(8,128)}, f32[128,2048]{1,0:T(8,128)}, bf16[3,128,2048]{2,1,0:T(8,128)(2,1)}, bf16[2048,3072]{1,0:T(8,128)(2,1)}) custom-call(bf16[128,2048]{1,0:T(8,128)(2,1)} %multiply_convert_fusion.6.x, bf16[4,256,2048]{2,1,0:T(8,128)(2,1)} %pad_maximum_fusion.fg, bf16[2048,3072]{1,0:T(8,128)(2,1)} %bitcast.239), custom_call_target="tpu_custom_call" | custom-call | tf_op jit(solution)/shard_map/pallas_call | solution.py:588
  431.3 2.6 multiply_reduce_fusion.2
  438.6 4.9 bitcast_multiply_fusion.1
  443.5 6.4 collective-permute-done.13
  449.9 10.9 %collective-permute-done.15 = bf16[128,2048]{1,0:T(8,128)(2,1)S(1)} collective-permute-done((bf16[128,2048]{1,0:T(8,128)(2,1)S(1)}, bf16[128,2048]{1,0:T(8,128)(2,1)S(1)}, u32[]{:S(2)}, u32[]{:S(2)}) %collective-permute-start.15) | collective-permute-done | bytes 524320 | tf_op jit(solution)/shard_map/ppermute | solution.py:618
  466.8 6.0 fusion.1
  472.7 10.0 %fusion.3 = bf16[4,768,768]{1,2,0:T(8,128)(2,1)} fusion(f32[768,768,4]{1,0,2:T(8,128)} %get-tuple-element.87, f32[4,768]{1,0:T(4,128)} %get-tuple-element.86, f32[4,768,768]{1,2,0:T(8,128)} %get-tuple-element.85, f32[4,768]{1,0:T(4,128)} %copy-done.45), kind=kLoop, calls=%fused_computation.5 | loop fusion | flops 11796480 | bytes 23617536 | tf_op jit(solution)/shard_map/convert_element_type | solution.py:888
  482.8 3.5 broadcast_multiply_fusion
  488.2 5.4 fusion.28
  503.9 3.0 fusion.12
  507.0 4.9 copy.73
  513.2 2.9 convolution_convert_fusion
  519.0 182.1 %shard_map.205 = (f32[128,2048]{1,0:T(8,128)}, bf16[128,4096]{1,0:T(8,128)(2,1)}, bf16[128,4096]{1,0:T(8,128)(2,1)}, bf16[128,4096]{1,0:T(8,128)(2,1)}, bf16[128...) custom-call(bf16[4,4,128,3072]{3,2,1,0:T(8,128)(2,1)} %bitcast.240, ...), custom_call_target="tpu_custom_call" | custom-call | tf_op jit(solution)/shard_map/pallas_call | solution.py:743
  701.3 3.4 bitcast_add_fusion
  716.7 3.2 collective-permute-done.21
  719.8 11.4 %collective-permute-done.22 = bf16[128,2048]{1,0:T(8,128)(2,1)S(1)} collective-permute-done((bf16[128,2048]{1,0:T(8,128)(2,1)S(1)}, bf16[128,2048]{1,0:T(8,128)(2,1)S(1)}, u32[]{:S(2)}, u32[]{:S(2)}) %collective-permute-start.22) | collective-permute-done | bytes 524320 | tf_op jit(solution)/shard_map/ppermute | solution.py:618
  (282 shorter events, 89.3 us)
Async XLA Ops:
  242.4 58.9 %collective-permute-start = (bf16[4,128,2048]{2,1,0:T(8,128)(2,1)S(1)}, bf16[4,128,2048]{2,1,0:T(8,128)(2,1)}, u32[]{:S(2)}, u32[]{:S(2)}) collective-permute-start(bf16[4,128,2048]{2,1,0:T(8,128)(2,1)S(1)} %fusion.18), channel_id=1, source_target_pairs={{0,1},{1,0},{2,3},{3,2},{4,5},{5,4},{6,7},{7,6},{8,9},{9,8},{10,11... | collective-permute-start | bytes 6291464 | tf_op jit(solution)/shard_map/ppermute | solution.py:618
  247.0 34.5 %collective-permute-start.7 = (bf16[128,2048]{1,0:T(8,128)(2,1)}, bf16[128,2048]{1,0:T(8,128)(2,1)}, u32[]{:S(2)}, u32[]{:S(2)}) collective-permute-start(bf16[128,2048]{1,0:T(8,128)(2,1)} %fusion.39), channel_id=1, source_target_pairs={{0,16},{8,24},{16,0},{24,8},{1,17},{9,25},{17,1},{25,9},{2,18},{10... | collective-permute-start | bytes 1572872 | tf_op jit(solution)/shard_map/ppermute | solution.py:618
  257.1 25.7 %collective-permute-start.5 = (bf16[128,2048]{1,0:T(8,128)(2,1)}, bf16[128,2048]{1,0:T(8,128)(2,1)}, u32[]{:S(2)}, u32[]{:S(2)}) collective-permute-start(bf16[128,2048]{1,0:T(8,128)(2,1)} %fusion.39), channel_id=1, source_target_pairs={{0,8},{8,0},{16,24},{24,16},{1,9},{9,1},{17,25},{25,17},{2,10},{10... | collective-permute-start | bytes 1572872 | tf_op jit(solution)/shard_map/ppermute | solution.py:618
  257.1 25.8 %collective-permute-start.4 = (bf16[128,2048]{1,0:T(8,128)(2,1)}, bf16[128,2048]{1,0:T(8,128)(2,1)}, u32[]{:S(2)}, u32[]{:S(2)}) collective-permute-start(bf16[128,2048]{1,0:T(8,128)(2,1)} %fusion.39), channel_id=1, source_target_pairs={{0,1},{1,0},{2,3},{3,2},{4,5},{5,4},{6,7},{7,6},{8,9},{9,8},{10,11... | collective-permute-start | bytes 1572872 | tf_op jit(solution)/shard_map/ppermute | solution.py:618
  257.3 27.3 %collective-permute-start.9 = (bf16[128,2048]{1,0:T(8,128)(2,1)}, bf16[128,2048]{1,0:T(8,128)(2,1)}, u32[]{:S(2)}, u32[]{:S(2)}) collective-permute-start(bf16[128,2048]{1,0:T(8,128)(2,1)} %fusion.39), channel_id=1, source_target_pairs={{8,16},{16,8},{9,17},{17,9},{10,18},{18,10},{11,19},{19,11},{12,20... | collective-permute-start | bytes 1572872 | tf_op jit(solution)/shard_map/ppermute | solution.py:640
  281.5 15.8 %collective-permute-start.10 = (bf16[128,2048]{1,0:T(8,128)(2,1)}, bf16[128,2048]{1,0:T(8,128)(2,1)}, u32[]{:S(2)}, u32[]{:S(2)}) collective-permute-start(bf16[128,2048]{1,0:T(8,128)(2,1)} %collective-permute-done.7), channel_id=1, source_target_pairs={{16,24},{8,0},{17,25},{9,1},{18,26},{10,2},{19,27},{11,3},{20,28},... | collective-permute-start | bytes 1572872 | tf_op jit(solution)/shard_map/ppermute | solution.py:640
  282.8 15.9 %collective-permute-start.8 = (bf16[128,2048]{1,0:T(8,128)(2,1)}, bf16[128,2048]{1,0:T(8,128)(2,1)}, u32[]{:S(2)}, u32[]{:S(2)}) collective-permute-start(bf16[128,2048]{1,0:T(8,128)(2,1)} %collective-permute-done.7), channel_id=1, source_target_pairs={{0,1},{1,0},{2,3},{3,2},{4,5},{5,4},{6,7},{7,6},{8,9},{9,8},{10,11... | collective-permute-start | bytes 1572872 | tf_op jit(solution)/shard_map/ppermute | solution.py:618
  282.9 17.1 %collective-permute-start.6 = (bf16[128,2048]{1,0:T(8,128)(2,1)}, bf16[128,2048]{1,0:T(8,128)(2,1)}, u32[]{:S(2)}, u32[]{:S(2)}) collective-permute-start(bf16[128,2048]{1,0:T(8,128)(2,1)} %collective-permute-done.5), channel_id=1, source_target_pairs={{0,1},{1,0},{2,3},{3,2},{4,5},{5,4},{6,7},{7,6},{8,9},{9,8},{10,11... | collective-permute-start | bytes 1572872 | tf_op jit(solution)/shard_map/ppermute | solution.py:618
  298.6 10.0 %collective-permute-start.11 = (bf16[128,2048]{1,0:T(8,128)(2,1)S(1)}, bf16[128,2048]{1,0:T(8,128)(2,1)S(1)}, u32[]{:S(2)}, u32[]{:S(2)}) collective-permute-start(bf16[128,2048]{1,0:T(8,128)(2,1)S(1)} %add.181), channel_id=1, source_target_pairs={{0,1},{1,0},{2,3},{3,2},{4,5},{5,4},{6,7},{7,6},{8,9},{9,8},{10,11... | collective-permute-start | bytes 1572872 | tf_op jit(solution)/shard_map/ppermute | solution.py:618
  304.9 14.9 %collective-permute-start.1 = (bf16[128,2048]{1,0:T(8,128)(2,1)S(1)}, bf16[128,2048]{1,0:T(8,128)(2,1)S(1)}, u32[]{:S(2)}, u32[]{:S(2)}) collective-permute-start(bf16[128,2048]{1,0:T(8,128)(2,1)S(1)} %get-tuple-element.59), channel_id=1, source_target_pairs={{0,2},{2,0},{4,6},{6,4},{1,3},{3,1},{5,7},{7,5},{8,10},{10,8},{12,... | collective-permute-start | bytes 1572872 | tf_op jit(solution)/shard_map/ppermute | solution.py:618
  306.5 25.3 %collective-permute-start.2 = (bf16[128,2048]{1,0:T(8,128)(2,1)S(1)}, bf16[128,2048]{1,0:T(8,128)(2,1)S(1)}, u32[]{:S(2)}, u32[]{:S(2)}) collective-permute-start(bf16[128,2048]{1,0:T(8,128)(2,1)S(1)} %get-tuple-element.61), channel_id=1, source_target_pairs={{0,4},{2,6},{4,0},{6,2},{1,5},{3,7},{5,1},{7,3},{8,12},{10,14},{12... | collective-permute-start | bytes 1572872 | tf_op jit(solution)/shard_map/ppermute | solution.py:618
  307.1 24.7 %collective-permute-start.3 = (bf16[128,2048]{1,0:T(8,128)(2,1)S(1)}, bf16[128,2048]{1,0:T(8,128)(2,1)S(1)}, u32[]{:S(2)}, u32[]{:S(2)}) collective-permute-start(bf16[128,2048]{1,0:T(8,128)(2,1)S(1)} %get-tuple-element.60), channel_id=1, source_target_pairs={{0,6},{2,4},{4,2},{6,0},{1,7},{3,5},{5,3},{7,1},{8,14},{10,12},{12... | collective-permute-start | bytes 1572872 | tf_op jit(solution)/shard_map/ppermute | solution.py:618
  332.8 98.4 %copy-start.48 = (f32[128]{0:T(128)}, f32[128]{0:T(128)S(1)}, u32[]{:S(2)}) copy-start(f32[128]{0:T(128)S(1)} %add_rsqrt_fusion.2) | copy-start | bytes 1540
  435.0 26.4 %collective-permute-start.12 = (bf16[128,2048]{1,0:T(8,128)(2,1)S(1)}, bf16[128,2048]{1,0:T(8,128)(2,1)S(1)}, u32[]{:S(2)}, u32[]{:S(2)}) collective-permute-start(bf16[128,2048]{1,0:T(8,128)(2,1)S(1)} %get-tuple-element.52), channel_id=1, source_target_pairs={{0,1},{1,0},{2,3},{3,2},{4,5},{5,4},{6,7},{7,6},{8,9},{9,8},{10,11... | collective-permute-start | bytes 1572872 | tf_op jit(solution)/shard_map/ppermute | solution.py:618
  435.1 14.9 %collective-permute-start.13 = (bf16[128,2048]{1,0:T(8,128)(2,1)S(1)}, bf16[128,2048]{1,0:T(8,128)(2,1)S(1)}, u32[]{:S(2)}, u32[]{:S(2)}) collective-permute-start(bf16[128,2048]{1,0:T(8,128)(2,1)S(1)} %get-tuple-element.52), channel_id=1, source_target_pairs={{0,2},{2,0},{4,6},{6,4},{1,3},{3,1},{5,7},{7,5},{8,10},{10,8},{12,... | collective-permute-start | bytes 1572872 | tf_op jit(solution)/shard_map/ppermute | solution.py:618
  435.6 25.2 %collective-permute-start.15 = (bf16[128,2048]{1,0:T(8,128)(2,1)S(1)}, bf16[128,2048]{1,0:T(8,128)(2,1)S(1)}, u32[]{:S(2)}, u32[]{:S(2)}) collective-permute-start(bf16[128,2048]{1,0:T(8,128)(2,1)S(1)} %get-tuple-element.52), channel_id=1, source_target_pairs={{0,4},{2,6},{4,0},{6,2},{1,5},{3,7},{5,1},{7,3},{8,12},{10,14},{12... | collective-permute-start | bytes 1572872 | tf_op jit(solution)/shard_map/ppermute | solution.py:618
  437.0 23.8 %collective-permute-start.17 = (bf16[128,2048]{1,0:T(8,128)(2,1)S(1)}, bf16[128,2048]{1,0:T(8,128)(2,1)S(1)}, u32[]{:S(2)}, u32[]{:S(2)}) collective-permute-start(bf16[128,2048]{1,0:T(8,128)(2,1)S(1)} %get-tuple-element.52), channel_id=1, source_target_pairs={{0,6},{2,4},{4,2},{6,0},{1,7},{3,5},{5,3},{7,1},{8,14},{10,12},{12... | collective-permute-start | bytes 1572872 | tf_op jit(solution)/shard_map/ppermute | solution.py:618
  438.6 28.1 %slice-start.3 = ((s8[9437184]{0:T(1024)(128)(4,1)}), s8[4194304]{0:T(1024)(128)(4,1)S(1)}, s32[]{:S(2)}) async-start(s8[9437184]{0:T(1024)(128)(4,1)} %bitcast.241), calls=%async_computation.3 | async-start | bytes 8388608
  449.9 11.6 %collective-permute-start.14 = (bf16[128,2048]{1,0:T(8,128)(2,1)S(1)}, bf16[128,2048]{1,0:T(8,128)(2,1)S(1)}, u32[]{:S(2)}, u32[]{:S(2)}) collective-permute-start(bf16[128,2048]{1,0:T(8,128)(2,1)S(1)} %collective-permute-done.13), channel_id=1, source_target_pairs={{0,1},{1,0},{2,3},{3,2},{4,5},{5,4},{6,7},{7,6},{8,9},{9,8},{10,11... | collective-permute-start | bytes 1572872 | tf_op jit(solution)/shard_map/ppermute | solution.py:618
  460.9 1.9 collective-permute-start.16
  460.9 2.7 collective-permute-start.18
  497.0 4.8 collective-permute-start.25
  500.3 200.9 %collective-permute-start.20 = (bf16[4,128,2048]{2,1,0:T(8,128)(2,1)}, bf16[4,128,2048]{2,1,0:T(8,128)(2,1)}, u32[]{:S(2)}, u32[]{:S(2)}) collective-permute-start(bf16[4,128,2048]{2,1,0:T(8,128)(2,1)} %fusion.19), channel_id=1, source_target_pairs={{0,1},{1,0},{2,3},{3,2},{4,5},{5,4},{6,7},{7,6},{8,9},{9,8},{10,11... | collective-permute-start | bytes 6291464 | tf_op jit(solution)/shard_map/ppermute | solution.py:618
  502.4 9.4 %collective-permute-start.26 = (f32[2,2048]{1,0:T(2,128)}, f32[2,2048]{1,0:T(2,128)}, u32[]{:S(2)}, u32[]{:S(2)}) collective-permute-start(f32[2,2048]{1,0:T(2,128)} %fusion.77), channel_id=1, source_target_pairs={{0,2},{2,0},{4,6},{6,4},{1,3},{3,1},{5,7},{7,5},{8,10},{10,8},{12,... | collective-permute-start | bytes 49160 | tf_op jit(solution)/shard_map/ppermute | solution.py:618
  512.8 3.8 collective-permute-start.27
  516.6 184.6 %collective-permute-start.28 = (f32[2,2048]{1,0:T(2,128)S(1)}, f32[2,2048]{1,0:T(2,128)S(1)}, u32[]{:S(2)}, u32[]{:S(2)}) collective-permute-start(f32[2,2048]{1,0:T(2,128)S(1)} %add.193), channel_id=1, source_target_pairs={{0,8},{8,0},{16,24},{24,16},{1,9},{9,1},{17,25},{25,17},{2,10},{10... | collective-permute-start | bytes 49160 | tf_op jit(solution)/shard_map/ppermute | solution.py:618
  701.2 15.5 %collective-permute-start.29 = (f32[2,2048]{1,0:T(2,128)S(1)}, f32[2,2048]{1,0:T(2,128)S(1)}, u32[]{:S(2)}, u32[]{:S(2)}) collective-permute-start(f32[2,2048]{1,0:T(2,128)S(1)} %add.194), channel_id=1, source_target_pairs={{0,16},{8,24},{16,0},{24,8},{1,17},{9,25},{17,1},{25,9},{2,18},{10... | collective-permute-start | bytes 49160 | tf_op jit(solution)/shard_map/ppermute | solution.py:618
  705.0 14.9 %collective-permute-start.21 = (bf16[128,2048]{1,0:T(8,128)(2,1)S(1)}, bf16[128,2048]{1,0:T(8,128)(2,1)S(1)}, u32[]{:S(2)}, u32[]{:S(2)}) collective-permute-start(bf16[128,2048]{1,0:T(8,128)(2,1)S(1)} %get-tuple-element.56), channel_id=1, source_target_pairs={{0,2},{2,0},{4,6},{6,4},{1,3},{3,1},{5,7},{7,5},{8,10},{10,8},{12,... | collective-permute-start | bytes 1572872 | tf_op jit(solution)/shard_map/ppermute | solution.py:618
  706.5 24.8 %collective-permute-start.22 = (bf16[128,2048]{1,0:T(8,128)(2,1)S(1)}, bf16[128,2048]{1,0:T(8,128)(2,1)S(1)}, u32[]{:S(2)}, u32[]{:S(2)}) collective-permute-start(bf16[128,2048]{1,0:T(8,128)(2,1)S(1)} %get-tuple-element.58), channel_id=1, source_target_pairs={{0,4},{2,6},{4,0},{6,2},{1,5},{3,7},{5,1},{7,3},{8,12},{10,14},{12... | collective-permute-start | bytes 1572872 | tf_op jit(solution)/shard_map/ppermute | solution.py:618
  707.1 24.2 %collective-permute-start.23 = (bf16[128,2048]{1,0:T(8,128)(2,1)S(1)}, bf16[128,2048]{1,0:T(8,128)(2,1)S(1)}, u32[]{:S(2)}, u32[]{:S(2)}) collective-permute-start(bf16[128,2048]{1,0:T(8,128)(2,1)S(1)} %get-tuple-element.57), channel_id=1, source_target_pairs={{0,6},{2,4},{4,2},{6,0},{1,7},{3,5},{5,3},{7,1},{8,14},{10,12},{12... | collective-permute-start | bytes 1572872 | tf_op jit(solution)/shard_map/ppermute | solution.py:618
  708.9 24.1 %collective-permute-start.19 = (bf16[128,2048]{1,0:T(8,128)(2,1)S(1)}, bf16[128,2048]{1,0:T(8,128)(2,1)S(1)}, u32[]{:S(2)}, u32[]{:S(2)}) collective-permute-start(bf16[128,2048]{1,0:T(8,128)(2,1)S(1)} %get-tuple-element.50), channel_id=1, source_target_pairs={{0,1},{1,0},{2,3},{3,2},{4,5},{5,4},{6,7},{7,6},{8,9},{9,8},{10,11... | collective-permute-start | bytes 1572872 | tf_op jit(solution)/shard_map/ppermute | solution.py:618
  732.5 2.0 collective-permute-start.24
  (63 other events, 303.9 us)

commit v4 on v3

--- a/solution.py
+++ b/solution.py
@@ -339,12 +339,43 @@
     pl.semaphore_wait(barrier, len(partners))
 
 
-def weights_in_kernel(wa, wf, xt, gain, wa_all, wf_all, x_all, gain_all, send, receive, local):
+def dot_tile(left, right, left_axis, right_axis):
+    return lax.dot_general(left, right, (((left_axis,), (right_axis,)), ((), ())), preferred_element_type=jnp.float32)
+
+
+TILE = 256
+
+
+def turn_lanes(x, low):
+    return jnp.where(low, pltpu.roll(x, x.shape[1] - HEAD // 2, 1), pltpu.roll(x, HEAD // 2, 1))
+
+
+def low_lanes(shape, width):
+    return lax.rem(lax.broadcasted_iota(jnp.int32, shape, 1), 2 * width) < width
+
+
+def split_pair(x):
+    low = low_lanes(x.shape, HEAD)
+    a, b = jnp.where(low, x, 0.0), jnp.where(low, 0.0, x)
+    return a, pltpu.roll(a, HEAD, 1), pltpu.roll(b, HEAD, 1), b
+
+
+def attention_kernel(
+    wa, wf, xt, gain, fgx, cos, sin, seg_col, seg_row,
+    wa_out, wf_all, normed_out, q, kv, logs, attended, hidden_out, normed_two, fg_all, gains,
+    wa_all, x_all, gain_all, normed, pairs, sums, mine, cross, crossed, totals, landed, send, receive, local,
+):
+    f32, bf16 = jnp.float32, jnp.bfloat16
     z, c, t = (lax.axis_index(a) for a in (FSDP, CONTEXT, TENSOR))
     peers = [(flip(z, i), flip(c, j), t) for i in range(4) for j in range(4) if i or j]
     core = (z, c, 1 - t)
     greet(peers + [core])
     net = Copies(send, receive)
+    middle = (z == 1) | (z == 2)
+    nt, part, width = xt.shape
+    rows = nt * part
+    q_cols = q.shape[1]
+    qkv_cols = q_cols + 2 * HEAD
     ends = []
     own = []
     for i, (source, target) in enumerate(
@@ -353,50 +384,53 @@
             (xt, x_all.at[c]),
             (wf.at[z], wf_all.at[z, c]),
             (gain, gain_all.at[z, c]),
+            (fgx, fg_all.at[0, 0]),
         )
     ):
         own.append(pltpu.make_async_copy(source, target, local.at[i]))
         own[-1].start()
 
+    def spread(source, slot, forward):
+        one = net.start(source, slot(1), (flip(z, 1), c, t))
+        two = net.start(source, slot(2), (flip(z, 2), c, t))
+        three = net.index()
+        direct = net.make(three, source, slot(3), (3 - z, c, t))
+        pl.when(middle)(direct.start)
+        passed = pltpu.make_async_remote_copy(
+            src_ref=forward[0],
+            dst_ref=forward[1],
+            send_sem=send.at[net.index()],
+            recv_sem=receive.at[three],
+            device_id=(flip(z, 1), c, t),
+            device_id_type=pl.DeviceIdType.MESH,
+        )
+        return one, two, direct, passed
+
     attn_in = [net.start(wa.at[flip(c, k)], wa_all.at[z, c], (z, flip(c, k), t)) for k in (1, 2, 3)]
     tokens_in = [net.start(xt.at[t], x_all.at[c, t], (z, flip(c, k), t)) for k in (1, 2, 3)]
+    ff_in = {1: net.start(wf.at[flip(z, 1)], wf_all.at[z, c], (flip(z, 1), c, t))}
     for device in peers:
         ends.append(net.start(gain, gain_all.at[z, c], device))
     own[2].wait()
-    forward = []
-    middle = (z == 1) | (z == 2)
+    ff_out = {0: [net.start(wf_all.at[z, c], wf_all.at[z, c], (z, flip(c, k), t)) for k in (1, 2)]}
+    weights = []
     for j in range(4):
         if j:
             attn_in[j - 1].wait_recv()
         else:
             own[0].wait()
         piece = wa_all.at[z, flip(c, j)]
-        ends.append(net.start(piece, piece, (flip(z, 1), c, t)))
-        two = net.start(piece, piece, (flip(z, 2), c, t))
-        three = net.index()
-        direct = net.make(three, piece, piece, (3 - z, c, t))
-        pl.when(middle)(direct.start)
         passed_piece = wa_all.at[flip(z, 2), flip(c, j)]
-        passed = pltpu.make_async_remote_copy(
-            src_ref=passed_piece,
-            dst_ref=passed_piece,
-            send_sem=send.at[net.index()],
-            recv_sem=receive.at[three],
-            device_id=(flip(z, 1), c, t),
-            device_id_type=pl.DeviceIdType.MESH,
-        )
-        forward.append((two, direct, passed))
-    ff_in = {k: net.start(wf.at[flip(z, k)], wf_all.at[z, c], (flip(z, k), c, t)) for k in (3, 2)}
-    ff_out = {0: [net.start(wf_all.at[z, c], wf_all.at[z, c], (z, flip(c, k), t)) for k in (1, 2)]}
-    swaps = []
+        weights.append(spread(piece, lambda k, piece=piece: piece, (passed_piece, passed_piece)))
+    for k in (3, 2):
+        ff_in[k] = net.start(wf.at[flip(z, k)], wf_all.at[z, c], (flip(z, k), c, t))
+    feed = spread(fgx, lambda k: fg_all.at[k, 0], (fg_all.at[2, 0], fg_all.at[3, 0]))
+    swaps = [net.start(fgx, fg_all.at[0, 1], core)]
+    token_swaps = []
     for k, copy in zip((1, 2, 3), tokens_in):
         copy.wait_recv()
         piece = x_all.at[flip(c, k), t]
-        swaps.append(net.start(piece, piece, core))
-    for two, direct, passed in forward:
-        two.wait_recv()
-        pl.when(middle)(passed.start)
-    ff_in[1] = net.start(wf.at[flip(z, 1)], wf_all.at[z, c], (flip(z, 1), c, t))
+        token_swaps.append(net.start(piece, piece, core))
     halves = []
 
     def corner(k):
@@ -409,49 +443,187 @@
         piece = wf_all.at[zs, flip(c, 1), pl.ds(64, 64)]
         halves.append(net.start(piece, piece, (z, flip(c, 2), t)))
 
-    last = 0
-    for k in (3, 2, 1):
+    def onward(k):
         ff_in[k].wait_recv()
         piece = wf_all.at[flip(z, k), c]
         ff_out[k] = [net.start(piece, piece, (z, flip(c, j), t)) for j in (1, 2)]
-        corner(last)
-        last = k
-    corner(last)
-    for copy in halves + swaps + ends:
+
+    own[1].wait()
+    own[3].wait()
+    for copy in token_swaps + ends:
         copy.wait_recv()
-    for _, direct, passed in forward:
+    for i in range(2):
+        gains[i : i + 1, :] = jnp.concatenate(
+            [gain_all[a, b, i : i + 1, :].astype(f32) for a in range(4) for b in range(4)], axis=1
+        )
+
+    def norm_rows(i, carry):
+        x = x_all[i].reshape(rows, width).astype(f32)
+        inverse = lax.rsqrt(jnp.mean(x * x, axis=-1, keepdims=True) + norm_eps)
+        normed[i] = (x * inverse * gains[0:1, :]).astype(bf16)
+        return carry
+
+    lax.fori_loop(0, 4, norm_rows, 0)
+    save = [pltpu.make_async_copy(normed, normed_out, local.at[5])]
+    save[0].start()
+    onward(1)
+    corner(0)
+    for one, two, direct, passed in weights:
+        two.wait_recv()
+        pl.when(middle)(passed.start)
+    for one, two, direct, passed in weights:
+        one.wait_recv()
         direct.wait_recv()
+    save.append(pltpu.make_async_copy(wa_all, wa_out, local.at[6]))
+    save[1].start()
+
+    def project(i, carry):
+        here = pl.ds(pl.multiple_of(i * rows, rows), rows)
+        w = wa_all[...].reshape(width, wa_all.shape[3])
+        qkv = dot_tile(normed[i], w[:, :qkv_cols], 1, 0)
+        cos_b, sin_b = cos[here, :], sin[here, :]
+        quarter = low_lanes(cos_b.shape, HEAD // 2)
+        half = low_lanes(cos_b.shape, HEAD)
+        for p in range(q_cols // 128):
+            block = qkv[:, p * 128 : (p + 1) * 128]
+            q[here, p * 128 : (p + 1) * 128] = (block * cos_b + turn_lanes(block, quarter) * sin_b).astype(bf16)
+        block = qkv[:, q_cols:]
+        block = jnp.where(half, block * cos_b + turn_lanes(block, quarter) * sin_b, block)
+        kv[here, :] = block.astype(bf16)
+        for j, piece in enumerate(split_pair(block)):
+            pairs[j, here, :] = piece.astype(bf16)
+        return carry
+
+    lax.fori_loop(0, 4, project, 0)
+    corner(1)
+
+    def attend(i):
+        count = (i + 1) * rows
+        here = pl.ds(i * rows, rows)
+        keep = (seg_col[here, :] == seg_row[:, :count]) & (
+            lax.broadcasted_iota(jnp.int32, (rows, count), 0) + i * rows
+            >= lax.broadcasted_iota(jnp.int32, (rows, count), 1)
+        )
+        lane = lax.broadcasted_iota(jnp.int32, (rows, 128), 1)
+        log_sums = jnp.zeros((rows, 128), f32)
+        for p in range(q_cols // 128):
+            out = jnp.zeros((rows, 128), f32)
+            for e in range(2):
+                scores = dot_tile(q[here, p * 128 : (p + 1) * 128], pairs[e, :count, :], 1, 1)
+                scores = jnp.where(keep, scores * attention_mult, -1e30)
+                highest = jnp.max(scores, axis=-1, keepdims=True)
+                weight = jnp.exp(scores - highest)
+                total = jnp.sum(weight, axis=-1, keepdims=True)
+                out = out + dot_tile((weight / total).astype(bf16), pairs[2 + e, :count, :], 1, 0)
+                log_sums = jnp.where(lane == 2 * p + e, highest + jnp.log(total), log_sums)
+            attended[here, p * 128 : (p + 1) * 128] = out.astype(bf16)
+        logs[here, :] = log_sums
+
+    attend(0)
+    attend(1)
+    onward(3)
+    attend(2)
+    last = pl.ds(3 * rows, rows)
+    both = (pairs[2, last, :] + pairs[3, last, :]).astype(bf16)
+    for p in range(q_cols // 128):
+        attended[last, p * 128 : (p + 1) * 128] = both
+    corner(3)
+
+    crosses, outs = {}, {}
+    for k in (3, 1, 2, 0):
+        mine_rows = pl.ds(pl.multiple_of(flip(c, k) * rows, rows), rows)
+
+        def out_tile(n, carry, mine_rows=mine_rows):
+            here = pl.ds(pl.multiple_of(n * 128, 128), 128)
+            w = wa_all[lax.div(n, 4), lax.rem(n, 4), :, qkv_cols:]
+            sums[:, here] = dot_tile(attended[mine_rows, :], w, 1, 1)
+            return carry
+
+        lax.fori_loop(0, width // 128, out_tile, 0)
+        mine[k] = sums[pl.ds(pl.multiple_of(t * part, part), part), :]
+        cross[k] = sums[pl.ds(pl.multiple_of((1 - t) * part, part), part), :].astype(bf16)
+        crosses[k] = net.start(cross.at[k], crossed.at[k], core)
+    for k in (3, 1, 2):
+        crosses[k].wait_recv()
+        totals[k - 1] = (mine[k] + crossed[k].astype(f32)).astype(bf16)
+        outs[k] = net.start(totals.at[k - 1], landed.at[k - 1], (z, flip(c, k), t))
+    onward(2)
+    one, two, direct, passed = feed
+    two.wait_recv()
+    pl.when(middle)(passed.start)
+    swaps.append(net.start(fg_all.at[2, 0], fg_all.at[2, 1], core))
+    one.wait_recv()
+    swaps.append(net.start(fg_all.at[1, 0], fg_all.at[1, 1], core))
+    crosses[0].wait_recv()
+    total = mine[0] + crossed[0].astype(f32)
+    for k in (1, 2, 3):
+        outs[k].wait_recv()
+        total = total + landed[k - 1].astype(f32)
+    hidden = xt[t].astype(f32) + residual_mult * total
+    hidden_out[...] = hidden
+    inverse = lax.rsqrt(jnp.mean(hidden * hidden, axis=-1, keepdims=True) + norm_eps)
+    normed_two[...] = (hidden * inverse * gains[1:2, :]).astype(bf16)
+    direct.wait_recv()
+    swaps.append(net.start(fg_all.at[3, 0], fg_all.at[3, 1], core))
+    corner(2)
+    for copy in halves + swaps:
+        copy.wait_recv()
+    for _, _, direct, passed in weights + [feed]:
         pl.when(middle)(direct.wait_send)
         pl.when(middle)(passed.wait_send)
     for copy in net.started:
         copy.wait_send()
-    own[1].wait()
-    own[3].wait()
-
-
-def weights_in(wa, wf, xt, gain):
-    bf16 = jnp.bfloat16
-    shapes = ((4, 4) + wa.shape[1:], (4, 4) + wf.shape[1:], (4,) + xt.shape, (4, 4) + gain.shape)
-    copies = 128
+    own[4].wait()
+    for copy in save:
+        copy.wait()
+
+
+def attention_forward(wa, wf, xt, gain, fgx, cos, sin, seg_col, seg_row):
+    bf16, f32 = jnp.bfloat16, jnp.float32
+    nt, part, width = xt.shape
+    rows = nt * part
+    total = 4 * rows
+    wa_cols = wa.shape[2]
+    q_cols = (wa_cols - 2 * HEAD) // 2
+    filled = seg_col.shape[0]
+    copies = 96
+    vmem, anywhere = pl.BlockSpec(memory_space=pltpu.VMEM), pl.BlockSpec(memory_space=pl.ANY)
+    outs = (
+        ((4, 4) + wa.shape[1:], bf16, anywhere),
+        ((4, 4) + wf.shape[1:], bf16, anywhere),
+        ((4, rows, width), bf16, anywhere),
+        ((total, q_cols), bf16, vmem),
+        ((total, 2 * HEAD), bf16, vmem),
+        ((filled, 128), f32, vmem),
+        ((total, q_cols), bf16, vmem),
+        ((part, width), f32, vmem),
+        ((part, width), bf16, vmem),
+        ((4, nt, part, width), bf16, anywhere),
+        ((2, width), f32, vmem),
+    )
     return pl.pallas_call(
-        weights_in_kernel,
-        out_shape=[jax.ShapeDtypeStruct(s, bf16) for s in shapes],
-        in_specs=[pl.BlockSpec(memory_space=pltpu.VMEM)] * 4,
-        out_specs=[pl.BlockSpec(memory_space=pl.ANY)] * 4,
+        attention_kernel,
+        out_shape=[jax.ShapeDtypeStruct(shape, dtype) for shape, dtype, _ in outs],
+        in_specs=[vmem] * 9,
+        out_specs=[spec for _, _, spec in outs],
         scratch_shapes=[
+            pltpu.VMEM((4, 4) + wa.shape[1:], bf16),
+            pltpu.VMEM((4, nt, part, width), bf16),
+            pltpu.VMEM((4, 4) + gain.shape, bf16),
+            pltpu.VMEM((4, rows, width), bf16),
+            pltpu.VMEM((4, total, 2 * HEAD), bf16),
+            pltpu.VMEM((rows, width), f32),
+            pltpu.VMEM((4, part, width), f32),
+            pltpu.VMEM((4, part, width), bf16),
+            pltpu.VMEM((4, part, width), bf16),
+            pltpu.VMEM((3, part, width), bf16),
+            pltpu.VMEM((3, part, width), bf16),
             pltpu.SemaphoreType.DMA((copies,)),
             pltpu.SemaphoreType.DMA((copies,)),
-            pltpu.SemaphoreType.DMA((4,)),
+            pltpu.SemaphoreType.DMA((7,)),
         ],
-        compiler_params=pltpu.CompilerParams(collective_id=1, has_side_effects=True, vmem_limit_bytes=48 * 2**20),
-    )(wa, wf, xt, gain)
-
-
-def dot_tile(left, right, left_axis, right_axis):
-    return lax.dot_general(left, right, (((left_axis,), (right_axis,)), ((), ())), preferred_element_type=jnp.float32)
-
-
-TILE = 256
+        compiler_params=pltpu.CompilerParams(collective_id=1, has_side_effects=True, vmem_limit_bytes=60 * 2**20),
+    )(wa, wf, xt, gain, fgx, cos, sin, seg_col, seg_row)
 
 
 def feed_kernel(
@@ -618,10 +790,6 @@
     return lax.ppermute(x, axis, [(i, i ^ k) for i in range(lax.axis_size(axis))])
 
 
-def after(x, *others):
-    return lax.optimization_barrier((x, *others))[0]
-
-
 def put(buffer, block, *index):
     lead = len(index)
     block = block.reshape((1,) * lead + buffer.shape[lead:])
@@ -632,22 +800,6 @@
 
 def cut(x, index, size, axis):
     return lax.dynamic_slice_in_dim(x, index * size, size, axis)
-
-
-def fsdp_blocks(x):
-    one = swap(x, FSDP, 1)
-    two = swap(x, FSDP, 2)
-    three = lax.ppermute(x, FSDP, [(1, 2), (2, 1)]) + lax.ppermute(two, FSDP, [(2, 3), (1, 0)])
-    return [x, one, two, three]
-
-
-def context_blocks(x, axis):
-    one = swap(x, CONTEXT, 1)
-    two = swap(x, CONTEXT, 2)
-    half = x.shape[axis] // 2
-    low = swap(lax.slice_in_dim(two, 0, half, axis=axis), CONTEXT, 1)
-    high = swap(lax.slice_in_dim(one, half, 2 * half, axis=axis), CONTEXT, 2)
-    return one, two, low, high
 
 
 def grads_out_kernel(
@@ -807,41 +959,26 @@
         axis=2,
     )
     gain = jnp.pad(jnp.stack([attention_gain, feed_gain]).astype(bf16), ((0, 14), (0, 0)))
-    wa, wf, all_tokens, gains = weights_in(wa, wf, tokens[0].reshape(nt, part, width), gain)
-    gains = gains[:, :, :2].transpose(2, 0, 1, 3).reshape(2, width).astype(f32)
+    my_valid = lax.dynamic_slice_in_dim(valid_rows, c * local_rows + t * part, part)
+    cotangent = cut(out_grad[0], t, part, 0).astype(f32) * my_valid[:, None].astype(f32)
+    feed_grad = (residual_mult * cotangent).astype(bf16)
+    sign = jnp.where(jnp.arange(HEAD) < HEAD // 2, -1.0, 1.0).astype(f32)
+    wide_cos = jnp.concatenate([cos_table, cos_table], axis=1)
+    wide_sin = jnp.concatenate([sine_table * sign, sine_table * sign], axis=1)
+    wa, wf, normed_one, queries, pair, logs, attended, hidden, normed_two, feed_grads, gains = attention_forward(
+        wa, wf, tokens[0].reshape(nt, part, width), gain, feed_grad, wide_cos, wide_sin,
+        segment[:filled, None], segment[None, :filled],
+    )
     gain_one, gain_two = gains[0], gains[1]
     w_qkv = wa[..., :qkv_cols].reshape(width, qkv_cols)
     w_out = wa[..., qkv_cols:].reshape(width, q_cols)
-    my_tokens = cut(tokens[0], t, part, 0)
-    all_tokens = all_tokens.reshape(group_rows, width).astype(f32)
     w_feed = wf.reshape(width, 3 * ff_cols)
-
-    my_valid = lax.dynamic_slice_in_dim(valid_rows, c * local_rows + t * part, part)
-    cotangent = cut(out_grad[0], t, part, 0).astype(f32) * my_valid[:, None].astype(f32)
-    feed_grads = fsdp_blocks((residual_mult * cotangent).astype(bf16))
-    feed_grads = [jnp.concatenate([b, swap(b, TENSOR, 1)], axis=0) for b in feed_grads]
-
-    inverse_all = lax.rsqrt(jnp.mean(all_tokens * all_tokens, axis=-1, keepdims=True) + norm_eps)
-    unit_all = all_tokens * inverse_all
-    normed_one = (unit_all * gain_one).astype(bf16)
-    qkv = jnp.dot(normed_one, w_qkv, preferred_element_type=f32)
-    queries = rotate(qkv[:, :q_cols].reshape(group_rows, per_group, HEAD), cos_table, sine_table).astype(bf16)
-    keys = rotate(qkv[:, q_cols : q_cols + kv_cols].reshape(group_rows, 1, HEAD), cos_table, sine_table)
-    keys = keys.astype(bf16)[:, 0]
-    values = qkv[:, q_cols + kv_cols :].astype(bf16)
+    normed_one = normed_one.reshape(group_rows, width)
+    q_f = queries[:filled].reshape(filled, per_group, HEAD)
+    k_f, v_f = pair[:filled, :HEAD], pair[:filled, HEAD:]
+    attended_f = attended[:filled]
     slot_ids = jnp.arange(filled, dtype=jnp.int32)
     allowed = (segment[:filled, None] == segment[None, :filled]) & (slot_ids[:, None] >= slot_ids[None, :])
-    q_f, k_f, v_f = queries[:filled], keys[:filled], values[:filled]
-    scores = jnp.einsum("tgd,sd->gts", q_f, k_f, preferred_element_type=f32)
-    scores = jnp.where(allowed[None], scores * attention_mult, -1e30)
-    highest = jnp.max(scores, axis=-1, keepdims=True)
-    weight = jnp.exp(scores - highest)
-    totals = jnp.sum(weight, axis=-1, keepdims=True)
-    probabilities = weight / totals
-    prob_low = probabilities.astype(bf16)
-    mixed = jnp.einsum("gts,sd->tgd", prob_low, v_f, preferred_element_type=f32).astype(bf16)
-    attended_f = mixed.reshape(filled, q_cols)
-    attended = jnp.concatenate([attended_f, jnp.tile(values[filled:], (1, per_group))], axis=0)
 
     def scatter_context(partial):
         partial = partial.reshape(nc, nt, part, width)
@@ -853,14 +990,12 @@
             total = total + swap(cut(mine, c ^ k, 1, 0)[0].astype(bf16), CONTEXT, k).astype(f32)
         return total
 
-    attn_out = scatter_context(dot_last(attended, w_out))
-    my_inputs = my_tokens.astype(f32)
-    hidden = my_inputs + residual_mult * attn_out
+    my_inputs = cut(tokens[0], t, part, 0).astype(f32)
     inverse_two = lax.rsqrt(jnp.mean(hidden * hidden, axis=-1, keepdims=True) + norm_eps)
     unit_two = hidden * inverse_two
 
     normed_grad_two, feed_own, feed_send, ff_terms = feed_forward(
-        (unit_two * gain_two).astype(bf16), jnp.stack(feed_grads), w_feed
+        normed_two, feed_grads.reshape(nz, local_rows, width), w_feed
     )
     ff_terms = ff_terms.reshape(nz, nc, wrows, 3 * ff_cols)
 
@@ -883,6 +1018,10 @@
 
     out_term = dot_first(attn_grad, attended_f)
     mixed_grad = jnp.dot(attn_grad, w_out, preferred_element_type=f32).astype(bf16).reshape(filled, per_group, HEAD)
+    scores = jnp.einsum("tgd,sd->gts", q_f, k_f, preferred_element_type=f32)
+    scores = jnp.where(allowed[None], scores * attention_mult, -1e30)
+    probabilities = jnp.exp(scores - logs[:, :per_group].T[:, :, None])
+    prob_low = probabilities.astype(bf16)
     prob_grad = jnp.einsum("tgd,sd->gts", mixed_grad, v_f, preferred_element_type=f32)
     row_dot = jnp.sum(probabilities * prob_grad, axis=-1, keepdims=True)
     score_grad = (attention_mult * probabilities * (prob_grad - row_dot)).astype(bf16)
@@ -894,11 +1033,11 @@
     key_grad = rotate_back(key_grad[:, None], cos_f, sine_f)[:, 0].astype(bf16)
     qkv_grad = jnp.concatenate([query_grad, key_grad, value_grad], axis=1)
     normed_part = dot_last(qkv_grad, w_qkv)
-    attn_gain_term = jnp.sum(normed_part * unit_all[:filled], axis=0)
     normed_part = jnp.pad(normed_part, ((0, group_rows - filled), (0, 0)))
     normed_grad_one = scatter_context(normed_part)
     inverse_one = lax.rsqrt(jnp.mean(my_inputs * my_inputs, axis=-1, keepdims=True) + norm_eps)
     unit_one = my_inputs * inverse_one
+    attn_gain_term = jnp.sum(normed_grad_one * unit_one, axis=0)
     input_grad = both_cores((hidden_grad + norm_back(normed_grad_one, unit_one, gain_one, inverse_one)).astype(bf16))
 
     gain_terms = jnp.stack([attn_gain_term, feed_gain_term])

time: 743 us -> 682 us (0.918)
  waiting for transfers between devices: 91 us -> 45.1 us
  local copies, waits for them, and re-layouts: 38.8 us -> 65 us
  matrix products: 45.3 us -> 21.7 us
  other arithmetic: 66.8 us -> 46 us
  Pallas kernels: 463 us -> 482 us
  starting transfers between devices: 28.5 us -> 10.7 us
    ppermute x28 -> x18, waiting for transfers between devices: 78.5 us -> 45.1 us  [swap(): lax.ppermute(x, axis, [(i, i ^ k) for i in range(lax.axis_size(axis))])]
    ppermute x28 -> x18, starting transfers between devices: 25.7 us -> 10.7 us  [swap(): lax.ppermute(x, axis, [(i, i ^ k) for i in range(lax.axis_size(axis))])]
    ppermute x2 -> x0, waiting for transfers between devices: 12.6 us -> none  [the longest x1 12.6 us: fsdp_blocks(): lax.ppermute(two, FSDP, [(2, 3), (1, 0)])]
    pallas_call x1, Pallas kernels: 185 us -> 196 us  [attention_forward(): pl.pallas_call(attention_kernel, out_shape=[jax.ShapeDtypeStruct(shape, d...]
    dynamic_update_slice x9, local copies, waits for them, and re-layouts: 0.45 us -> 10.3 us  [put(): return lax.dynamic_update_slice(buffer, block, start)]
    sub x1 -> x0, matrix products: 8.1 us -> none  [on_device_split(): weight = jnp.exp(scores - highest)]
    unnamed x137 -> x79, local copies, waits for them, and re-layouts: 17.1 us -> 17.7 us
  transfers between devices with their start and end apart: 30 -> 18, of which waited for: 12 -> 9; matrix products, arithmetic and copies ran while one was open for 7% -> 7% of each run, Pallas kernels for 25% -> 27%
where the time goes in v4:
time: 682 us; the launch traced here: 672 us
  Pallas kernels  482 us (71%)
  local copies, waits for them, and re-layouts  65 us (10%)
  other arithmetic  46 us (7%)
  waiting for transfers between devices  45.1 us (7%)
  matrix products  21.7 us (3%)
  starting transfers between devices  10.7 us (2%)
    pallas_call x1, Pallas kernels, attention_forward(): pl.pallas_call(attention_kernel, out_shape=[jax.ShapeDtypeStruct(shape, d...  196 us
    pallas_call x1, Pallas kernels, grads_out(): pl.pallas_call(grads_out_kernel, out_shape=[jax.ShapeDtypeStruct(fs.shape...  183 us
    pallas_call x1, Pallas kernels, feed_forward(): pl.pallas_call(feed_kernel, out_shape=[jax.ShapeDtypeStruct((part, width)...  103 us
    ppermute x18, waiting for transfers between devices, swap(): lax.ppermute(x, axis, [(i, i ^ k) for i in range(lax.axis_size(axis))])  45.1 us
    unnamed x79, local copies, waits for them, and re-layouts  17.7 us
  transfers between devices with their start and end apart: 18, of which 9 were waited for; matrix products, arithmetic and copies ran while one was open for 7% of the time, Pallas kernels for 27%

profile of v4, /device:TPU:0, one launch (start us, length us, event | category | flops | bytes accessed | tf_op | source)
XLA Modules:
  0.0 671.8 jit_solution(10716367071873770532)
XLA Ops:
  20.4 3.6 fusion.37
  29.9 196.1 %shard_map.203 = (bf16[4,4,128,640]{3,2,1,0:T(8,128)(2,1)}, bf16[4,4,128,3072]{3,2,1,0:T(8,128)(2,1)}, bf16[4,256,2048]{2,1,0:T(8,128)(2,1)}, bf16[1024,256]{1,0...) custom-call(bf16[4,128,640]{2,1,0:T(8,128)(2,1)} %pad_maximum_fusion, ...), custom_call_target="tpu_custom_call" | custom-call | tf_op jit(solution)/shard_map/pallas_call | solution.py:604
  228.9 102.7 %shard_map.204 = (f32[128,2048]{1,0:T(8,128)}, f32[128,2048]{1,0:T(8,128)}, bf16[3,128,2048]{2,1,0:T(8,128)(2,1)}, bf16[2048,3072]{1,0:T(8,128)(2,1)}) custom-call(bf16[128,2048]{1,0:T(8,128)(2,1)} %get-tuple-element.35.x, bf16[4,256,2048]{2,1,0:T(8,128)(2,1)} %bitcast.205, bf16[2048,3072]{1,0:T(8,128)(2,1)} %bitcast.196), custom_call_target="tpu_custom_call" | custom-call | tf_op jit(solution)/shard_map/pallas_call | solution.py:760
  333.3 2.5 broadcast_in_dim.37
  341.5 2.3 slice.79
  343.7 2.8 slice.87
  349.2 2.5 collective-permute-done.3
  353.3 10.8 %collective-permute-done.5 = bf16[128,2048]{1,0:T(8,128)(2,1)} collective-permute-done((bf16[128,2048]{1,0:T(8,128)(2,1)}, bf16[128,2048]{1,0:T(8,128)(2,1)}, u32[]{:S(2)}, u32[]{:S(2)}) %collective-permute-start.5) | collective-permute-done | bytes 524320 | tf_op jit(solution)/shard_map/ppermute | solution.py:790
  364.1 1.9 bitcast_dynamic-update-slice_fusion.10
  366.0 1.9 bitcast_dynamic-update-slice_fusion.9
  368.7 1.9 bitcast_dynamic-update-slice_fusion.7
  371.5 2.0 bitcast_dynamic-update-slice_fusion.5
  374.4 2.3 slice.91
  379.3 2.6 fusion.17
  382.0 5.7 fusion
  388.5 7.9 %fusion.2 = bf16[4,768,768]{1,2,0:T(8,128)(2,1)S(1)} fusion(f32[768,768,4]{1,0,2:T(8,128)} %get-tuple-element.90, f32[768,768,4]{1,0,2:T(8,128)} %copy-done, f32[4,768]{1,0:T(4,128)S(1)} %get-tuple-element.89, f32[4,768]{1,0:T(4,128)S(1)} %copy.89, pred[768,768]{0,1:T(8,128)(4,1)S(1)} %fusion.9), kind=kLoop, calls=%fused_computation.4 | loop fusion | flops 16515072 | bytes 24207360 | tf_op jit(solution)/shard_map/convert_element_type | solution.py:1027
  396.4 2.1 copy-done.2
  400.1 3.4 broadcast_multiply_fusion
  406.1 3.3 fusion.51
  410.6 3.2 copy-done.1
  416.0 4.1 slice.70
  420.1 4.7 copy.86
  425.0 4.7 copy.101
  429.8 3.6 bitcast_add_fusion
  438.2 1.9 convolution_convert_fusion
  440.1 8.3 %collective-permute-done.9 = bf16[128,2048]{1,0:T(8,128)(2,1)S(1)} collective-permute-done((bf16[128,2048]{1,0:T(8,128)(2,1)S(1)}, bf16[128,2048]{1,0:T(8,128)(2,1)S(1)}, u32[]{:S(2)}, u32[]{:S(2)}) %collective-permute-start.9) | collective-permute-done | bytes 524320 | tf_op jit(solution)/shard_map/ppermute | solution.py:790
  448.4 10.4 %collective-permute-done.11 = bf16[128,2048]{1,0:T(8,128)(2,1)S(1)} collective-permute-done((bf16[128,2048]{1,0:T(8,128)(2,1)S(1)}, bf16[128,2048]{1,0:T(8,128)(2,1)S(1)}, u32[]{:S(2)}, u32[]{:S(2)}) %collective-permute-start.11) | collective-permute-done | bytes 524320 | tf_op jit(solution)/shard_map/ppermute | solution.py:790
  463.5 182.9 %shard_map.205 = (f32[128,2048]{1,0:T(8,128)}, bf16[128,4096]{1,0:T(8,128)(2,1)}, bf16[128,4096]{1,0:T(8,128)(2,1)}, bf16[128,4096]{1,0:T(8,128)(2,1)}, bf16[128...) custom-call(bf16[4,4,128,3072]{3,2,1,0:T(8,128)(2,1)} %bitcast.195, ...), custom_call_target="tpu_custom_call" | custom-call | tf_op jit(solution)/shard_map/pallas_call | solution.py:895
  648.2 1.9 bitcast_dynamic-update-slice_fusion.3
  658.3 3.2 collective-permute-done.15
  662.2 3.1 collective-permute-done.16
  666.2 3.8 collective-permute-done.17
  (185 shorter events, 75.9 us)
Async XLA Ops:
  0.6 10.6 %copy-start.14 = (f32[128,4096]{1,0:T(8,128)S(1)}, f32[128,4096]{1,0:T(8,128)}, u32[]{:S(2)}) copy-start(f32[128,4096]{1,0:T(8,128)} %param.21) | copy-start | bytes 6291460
  18.1 9.1 %copy-start.9 = (bf16[128,4,1024]{2,0,1:T(8,128)(2,1)S(1)}, bf16[128,4,1024]{2,0,1:T(8,128)(2,1)}, u32[]{:S(2)}) copy-start(bf16[128,4,1024]{2,0,1:T(8,128)(2,1)} %copy.84) | copy-start | bytes 3145732
  18.1 8.1 %copy-start.20 = (bf16[1,256,2048]{2,1,0:T(8,128)(2,1)S(1)}, bf16[1,256,2048]{2,1,0:T(8,128)(2,1)}, u32[]{:S(2)}) copy-start(bf16[1,256,2048]{2,1,0:T(8,128)(2,1)} %param.13) | copy-start | bytes 3145732
  228.9 102.7 %copy-start.3 = (f32[128,2048]{1,0:T(8,128)S(1)}, f32[128,2048]{1,0:T(8,128)}, u32[]{:S(2)}) copy-start(f32[128,2048]{1,0:T(8,128)} %get-tuple-element.34) | copy-start | bytes 3145732
  333.3 7.8 %copy-start.28 = (f32[768,128]{1,0:T(8,128)S(1)}, f32[768,128]{1,0:T(8,128)}, u32[]{:S(2)}) copy-start(f32[768,128]{1,0:T(8,128)} %get-tuple-element.43) | copy-start | bytes 1179652
  337.5 14.2 %collective-permute-start.3 = (bf16[128,2048]{1,0:T(8,128)(2,1)}, bf16[128,2048]{1,0:T(8,128)(2,1)}, u32[]{:S(2)}, u32[]{:S(2)}) collective-permute-start(bf16[128,2048]{1,0:T(8,128)(2,1)} %get-tuple-element.69), channel_id=1, source_target_pairs={{0,4},{2,6},{4,0},{6,2},{1,5},{3,7},{5,1},{7,3},{8,12},{10,14},{12... | collective-permute-start | bytes 1572872 | tf_op jit(solution)/shard_map/ppermute | solution.py:790
  338.2 15.1 %collective-permute-start.1 = (bf16[128,2048]{1,0:T(8,128)(2,1)}, bf16[128,2048]{1,0:T(8,128)(2,1)}, u32[]{:S(2)}, u32[]{:S(2)}) collective-permute-start(bf16[128,2048]{1,0:T(8,128)(2,1)} %get-tuple-element.69), channel_id=1, source_target_pairs={{0,2},{2,0},{4,6},{6,4},{1,3},{3,1},{5,7},{7,5},{8,10},{10,8},{12,... | collective-permute-start | bytes 1572872 | tf_op jit(solution)/shard_map/ppermute | solution.py:790
  339.6 24.5 %collective-permute-start = (bf16[128,2048]{1,0:T(8,128)(2,1)}, bf16[128,2048]{1,0:T(8,128)(2,1)}, u32[]{:S(2)}, u32[]{:S(2)}) collective-permute-start(bf16[128,2048]{1,0:T(8,128)(2,1)} %get-tuple-element.69), channel_id=1, source_target_pairs={{0,1},{1,0},{2,3},{3,2},{4,5},{5,4},{6,7},{7,6},{8,9},{9,8},{10,11... | collective-permute-start | bytes 1572872 | tf_op jit(solution)/shard_map/ppermute | solution.py:790
  339.6 24.5 %collective-permute-start.5 = (bf16[128,2048]{1,0:T(8,128)(2,1)}, bf16[128,2048]{1,0:T(8,128)(2,1)}, u32[]{:S(2)}, u32[]{:S(2)}) collective-permute-start(bf16[128,2048]{1,0:T(8,128)(2,1)} %get-tuple-element.69), channel_id=1, source_target_pairs={{0,6},{2,4},{4,2},{6,0},{1,7},{3,5},{5,3},{7,1},{8,14},{10,12},{12... | collective-permute-start | bytes 1572872 | tf_op jit(solution)/shard_map/ppermute | solution.py:790
  341.0 6.8 %copy-start.16 = (bf16[1024,128]{1,0:T(8,128)(2,1)S(1)}, bf16[1024,128]{1,0:T(8,128)(2,1)}, u32[]{:S(2)}) copy-start(bf16[1024,128]{1,0:T(8,128)(2,1)} %get-tuple-element.41) | copy-start | bytes 786436
  349.2 32.7 %copy-start = (f32[768,768,4]{1,0,2:T(8,128)}, f32[768,768,4]{1,0,2:T(8,128)S(1)}, u32[]{:S(2)}) copy-start(f32[768,768,4]{1,0,2:T(8,128)S(1)} %fusion.45) | copy-start | bytes 28311556
  351.7 18.9 %collective-permute-start.4 = (bf16[128,2048]{1,0:T(8,128)(2,1)}, bf16[128,2048]{1,0:T(8,128)(2,1)S(1)}, u32[]{:S(2)}, u32[]{:S(2)}) collective-permute-start(bf16[128,2048]{1,0:T(8,128)(2,1)} %collective-permute-done.3), channel_id=1, source_target_pairs={{0,1},{1,0},{2,3},{3,2},{4,5},{5,4},{6,7},{7,6},{8,9},{9,8},{10,11... | collective-permute-start | bytes 1572872 | tf_op jit(solution)/shard_map/ppermute | solution.py:790
  353.3 14.6 %collective-permute-start.2 = (bf16[128,2048]{1,0:T(8,128)(2,1)}, bf16[128,2048]{1,0:T(8,128)(2,1)S(1)}, u32[]{:S(2)}, u32[]{:S(2)}) collective-permute-start(bf16[128,2048]{1,0:T(8,128)(2,1)} %collective-permute-done.1), channel_id=1, source_target_pairs={{0,1},{1,0},{2,3},{3,2},{4,5},{5,4},{6,7},{7,6},{8,9},{9,8},{10,11... | collective-permute-start | bytes 1572872 | tf_op jit(solution)/shard_map/ppermute | solution.py:790
  364.1 9.4 %collective-permute-start.6 = (bf16[128,2048]{1,0:T(8,128)(2,1)}, bf16[128,2048]{1,0:T(8,128)(2,1)S(1)}, u32[]{:S(2)}, u32[]{:S(2)}) collective-permute-start(bf16[128,2048]{1,0:T(8,128)(2,1)} %collective-permute-done.5), channel_id=1, source_target_pairs={{0,1},{1,0},{2,3},{3,2},{4,5},{5,4},{6,7},{7,6},{8,9},{9,8},{10,11... | collective-permute-start | bytes 1572872 | tf_op jit(solution)/shard_map/ppermute | solution.py:790
  371.5 6.8 %copy-start.22 = (bf16[4,4,128,256]{3,2,1,0:T(8,128)(2,1)S(1)}, bf16[4,4,128,256]{3,2,1,0:T(8,128)(2,1)}, u32[]{:S(2)}) copy-start(bf16[4,4,128,256]{3,2,1,0:T(8,128)(2,1)} %slice.79) | copy-start | bytes 3145732
  415.5 14.3 %collective-permute-start.8 = (bf16[4,128,2048]{2,1,0:T(8,128)(2,1)}, bf16[4,128,2048]{2,1,0:T(8,128)(2,1)}, u32[]{:S(2)}, u32[]{:S(2)}) collective-permute-start(bf16[4,128,2048]{2,1,0:T(8,128)(2,1)} %fusion.10), channel_id=1, source_target_pairs={{0,1},{1,0},{2,3},{3,2},{4,5},{5,4},{6,7},{7,6},{8,9},{9,8},{10,11... | collective-permute-start | bytes 6291464 | tf_op jit(solution)/shard_map/ppermute | solution.py:790
  429.8 7.4 %copy-start.13 = (bf16[2048,768]{1,0:T(8,128)(2,1)S(1)}, bf16[2048,768]{1,0:T(8,128)(2,1)}, u32[]{:S(2)}) copy-start(bf16[2048,768]{1,0:T(8,128)(2,1)} %copy.101) | copy-start | bytes 9437188
  429.8 7.4 %copy-start.35 = (bf16[1024,256]{1,0:T(8,128)(2,1)S(1)}, bf16[1024,256]{1,0:T(8,128)(2,1)}, u32[]{:S(2)}) copy-start(bf16[1024,256]{1,0:T(8,128)(2,1)} %get-tuple-element.47) | copy-start | bytes 1572868
  433.6 14.9 %collective-permute-start.9 = (bf16[128,2048]{1,0:T(8,128)(2,1)S(1)}, bf16[128,2048]{1,0:T(8,128)(2,1)S(1)}, u32[]{:S(2)}, u32[]{:S(2)}) collective-permute-start(bf16[128,2048]{1,0:T(8,128)(2,1)S(1)} %get-tuple-element.71), channel_id=1, source_target_pairs={{0,2},{2,0},{4,6},{6,4},{1,3},{3,1},{5,7},{7,5},{8,10},{10,8},{12,... | collective-permute-start | bytes 1572872 | tf_op jit(solution)/shard_map/ppermute | solution.py:790
  434.3 24.6 %collective-permute-start.11 = (bf16[128,2048]{1,0:T(8,128)(2,1)S(1)}, bf16[128,2048]{1,0:T(8,128)(2,1)S(1)}, u32[]{:S(2)}, u32[]{:S(2)}) collective-permute-start(bf16[128,2048]{1,0:T(8,128)(2,1)S(1)} %get-tuple-element.72), channel_id=1, source_target_pairs={{0,6},{2,4},{4,2},{6,0},{1,7},{3,5},{5,3},{7,1},{8,14},{10,12},{12... | collective-permute-start | bytes 1572872 | tf_op jit(solution)/shard_map/ppermute | solution.py:790
  435.7 24.5 %collective-permute-start.10 = (bf16[128,2048]{1,0:T(8,128)(2,1)S(1)}, bf16[128,2048]{1,0:T(8,128)(2,1)S(1)}, u32[]{:S(2)}, u32[]{:S(2)}) collective-permute-start(bf16[128,2048]{1,0:T(8,128)(2,1)S(1)} %get-tuple-element.73), channel_id=1, source_target_pairs={{0,4},{2,6},{4,0},{6,2},{1,5},{3,7},{5,1},{7,3},{8,12},{10,14},{12... | collective-permute-start | bytes 1572872 | tf_op jit(solution)/shard_map/ppermute | solution.py:790
  438.2 22.1 %copy-start.31 = (f32[1,2048]{1,0:T(1,128)S(1)}, f32[1,2048]{1,0:T(1,128)}, u32[]{:S(2)}) copy-start(f32[1,2048]{1,0:T(1,128)} %get-tuple-element.85) | copy-start | bytes 24580
  461.7 184.8 %collective-permute-start.13 = (f32[2,2048]{1,0:T(2,128)S(1)}, f32[2,2048]{1,0:T(2,128)S(1)}, u32[]{:S(2)}, u32[]{:S(2)}) collective-permute-start(f32[2,2048]{1,0:T(2,128)S(1)} %pad_maximum_fusion.9), channel_id=1, source_target_pairs={{0,1},{1,0},{2,3},{3,2},{4,5},{5,4},{6,7},{7,6},{8,9},{9,8},{10,11... | collective-permute-start | bytes 49160 | tf_op jit(solution)/shard_map/ppermute | solution.py:790
  646.5 6.6 copy-start.19
  646.5 11.1 %collective-permute-start.14 = (f32[2,2048]{1,0:T(2,128)S(1)}, f32[2,2048]{1,0:T(2,128)S(1)}, u32[]{:S(2)}, u32[]{:S(2)}) collective-permute-start(f32[2,2048]{1,0:T(2,128)S(1)} %fusion.62), channel_id=1, source_target_pairs={{0,2},{2,0},{4,6},{6,4},{1,3},{3,1},{5,7},{7,5},{8,10},{10,8},{12,... | collective-permute-start | bytes 49160 | tf_op jit(solution)/shard_map/ppermute | solution.py:790
  653.1 13.1 %collective-permute-start.7 = (bf16[128,2048]{1,0:T(8,128)(2,1)S(1)}, bf16[128,2048]{1,0:T(8,128)(2,1)S(1)}, u32[]{:S(2)}, u32[]{:S(2)}) collective-permute-start(bf16[128,2048]{1,0:T(8,128)(2,1)S(1)} %get-tuple-element.67), channel_id=1, source_target_pairs={{0,1},{1,0},{2,3},{3,2},{4,5},{5,4},{6,7},{7,6},{8,9},{9,8},{10,11... | collective-permute-start | bytes 1572872 | tf_op jit(solution)/shard_map/ppermute | solution.py:790
  654.6 7.1 %copy-start.6 = (f32[128,2048]{1,0:T(8,128)S(1)}, f32[128,2048]{1,0:T(8,128)}, u32[]{:S(2)}) copy-start(f32[128,2048]{1,0:T(8,128)} %get-tuple-element.70) | copy-start | bytes 3145732
  654.6 7.1 %copy-start.8 = (f32[128,2048]{1,0:T(8,128)S(1)}, f32[128,2048]{1,0:T(8,128)}, u32[]{:S(2)}) copy-start(f32[128,2048]{1,0:T(8,128)} %get-tuple-element.65) | copy-start | bytes 3145732
  657.7 3.8 collective-permute-start.15
  661.5 3.8 collective-permute-start.16
  662.1 8.4 %collective-permute-start.12 = (bf16[128,2048]{1,0:T(8,128)(2,1)S(1)}, bf16[128,2048]{1,0:T(8,128)(2,1)S(1)}, u32[]{:S(2)}, u32[]{:S(2)}) collective-permute-start(bf16[128,2048]{1,0:T(8,128)(2,1)S(1)} %get-tuple-element.64), channel_id=1, source_target_pairs={{0,1},{1,0},{2,3},{3,2},{4,5},{5,4},{6,7},{7,6},{8,9},{9,8},{10,11... | collective-permute-start | bytes 1572872 | tf_op jit(solution)/shard_map/ppermute | solution.py:790
  665.3 4.7 collective-permute-start.17
  (22 other events, 80.4 us)

commit v5 on v4

--- a/solution.py
+++ b/solution.py
@@ -802,26 +802,36 @@
     return lax.dynamic_slice_in_dim(x, index * size, size, axis)
 
 
-def grads_out_kernel(
-    ff, at, fs, feed_out, gate_out, up_out, down_out, query_out, key_out, value_out, output_out,
-    terms, corner_x, corner_y, side_x, side_y, landed, feed_in, at_terms, at_in, at_total, at_landed, send, receive, local,
+def backward_kernel(
+    ff, fs, al, wa_in, normed_in, q, kv, logs, attended, cos, sin, seg_col, seg_row,
+    feed_in, back_own, back_in, ff_out, at_out,
+    terms, corner_x, corner_y, side_x, side_y, at_terms, at_in, at_total, wa, normed, ag, pairs, mixed, acc, dqkv,
+    sums, mine, cross, crossed, totals, send, receive, local,
 ):
     f32, bf16 = jnp.float32, jnp.bfloat16
     z, c, t = (lax.axis_index(a) for a in (FSDP, CONTEXT, TENSOR))
-    greet([(flip(z, k), c, t) for k in (1, 2, 3)] + [(z, flip(c, k), t) for k in (1, 2, 3)])
+    core = (z, c, 1 - t)
+    greet([(flip(z, k), c, t) for k in (1, 2, 3)] + [(z, flip(c, k), t) for k in (1, 2, 3)] + [core])
     net = Copies(send, receive)
-    rows = ff.shape[2]
-    half = rows // 2
+    wrows = ff.shape[2]
+    half = wrows // 2
+    part, width = al.shape
+    rows = 2 * part
+    q_cols = q.shape[1]
+    qkv_cols = q_cols + 2 * HEAD
+    blocks = normed.shape[0]
     order = (3, 2, 1, 0)
     loads = {}
     for k in order:
         zs = flip(z, k)
         loads[k] = pltpu.make_async_copy(ff.at[zs], terms.at[zs], local.at[k])
         loads[k].start()
-    attn_load = pltpu.make_async_copy(at, at_terms, local.at[4])
-    attn_load.start()
-    attn_load.wait()
-    attn_in = [net.start(at_terms.at[flip(z, k)], at_in.at[k - 1], (flip(z, k), c, t)) for k in (3, 2, 1)]
+    wa_load = pltpu.make_async_copy(wa_in, wa, local.at[4])
+    wa_load.start()
+    normed_load = pltpu.make_async_copy(normed_in.at[pl.ds(0, blocks)], normed, local.at[5])
+    normed_load.start()
+    ag_in = [net.start(al, ag.at[c, t], (z, flip(c, k), t)) for k in (3, 1, 2)]
+    swaps = [net.start(al, ag.at[c, t], core)]
     feed = [net.start(fs.at[k - 1], feed_in.at[k - 1], (flip(z, k), c, t)) for k in (3, 2, 1)]
     first = {}
     for k in order:
@@ -831,8 +841,18 @@
             net.start(terms.at[zs, flip(c, 3), pl.ds(0, half)], corner_x.at[k], (z, flip(c, 1), t)),
             net.start(terms.at[zs, flip(c, 3), pl.ds(half, half)], corner_y.at[k], (z, flip(c, 2), t)),
         )
-    second = {}
-    for k in order:
+    ag[c, t] = al[...]
+    for j, piece in enumerate(split_pair(kv[...].astype(f32))):
+        pairs[j] = piece.astype(bf16)
+    acc[...] = jnp.zeros_like(acc)
+    dqkv[pl.ds(blocks * rows, rows), :] = jnp.zeros((rows, qkv_cols), bf16)
+    for k, copy in zip((3, 1, 2), ag_in):
+        copy.wait_recv()
+        piece = ag.at[flip(c, k), t]
+        swaps.append(net.start(piece, piece, core))
+    second, third = {}, {}
+
+    def sides(k):
         zs = flip(z, k)
         for copy in first[k]:
             copy.wait_recv()
@@ -844,6 +864,117 @@
             net.start(terms.at[zs, yb], side_y.at[k], (z, yb, t)),
             net.start(terms.at[zs, xb], side_x.at[k], (z, xb, t)),
         )
+
+    def owners(k):
+        zs = flip(z, k)
+        for copy in second[k]:
+            copy.wait_recv()
+        total = terms[zs, c].astype(f32) + side_x[k].astype(f32) + side_y[k].astype(f32)
+        terms[zs, c] = total.astype(bf16)
+        if k:
+            third[k] = net.start(terms.at[zs, c], ff_out.at[z], (zs, c, t))
+        else:
+            third[0] = pltpu.make_async_copy(terms.at[z, c], ff_out.at[z], local.at[6])
+            third[0].start()
+
+    for copy in swaps:
+        copy.wait_recv()
+    wa_load.wait()
+    normed_load.wait()
+
+    def mix(i, carry):
+        w = wa[...].reshape(width, wa.shape[3])[:, qkv_cols:]
+        here = pl.ds(pl.multiple_of(i * rows, rows), rows)
+        mixed[here, :] = dot_tile(ag[i].reshape(rows, width), w, 1, 0).astype(bf16)
+        return carry
+
+    lax.fori_loop(0, blocks, mix, 0)
+    sides(3)
+
+    def out_term(m, carry):
+        here = pl.ds(pl.multiple_of(m * wrows, wrows), wrows)
+        left = ag[0:blocks, :, :, here].reshape(blocks * rows, wrows)
+        value = dot_tile(left, attended[0 : blocks * rows, :], 0, 0)
+        at_terms[lax.div(m, 4), lax.rem(m, 4), :, qkv_cols:] = value.astype(bf16)
+        return carry
+
+    lax.fori_loop(0, width // wrows, out_term, 0)
+    sides(2)
+
+    def attend(i):
+        count = (i + 1) * rows
+        here = pl.ds(i * rows, rows)
+        keep = (seg_col[here, :] == seg_row[:, :count]) & (
+            lax.broadcasted_iota(jnp.int32, (rows, count), 0) + i * rows
+            >= lax.broadcasted_iota(jnp.int32, (rows, count), 1)
+        )
+        log_sums = logs[here, :]
+        lane = lax.broadcasted_iota(jnp.int32, (rows, 128), 1)
+        cos_b, sin_b = cos[here, :], sin[here, :]
+        quarter = low_lanes(cos_b.shape, HEAD // 2)
+        for p in range(q_cols // 128):
+            block = slice(p * 128, (p + 1) * 128)
+            grad = jnp.zeros((rows, 128), f32)
+            for e in range(2):
+                scores = dot_tile(q[here, block], pairs[e, :count, :], 1, 1)
+                scores = jnp.where(keep, scores * attention_mult, -1e30)
+                log = jnp.sum(jnp.where(lane == 2 * p + e, log_sums, 0.0), axis=-1, keepdims=True)
+                prob = jnp.exp(scores - log)
+                prob_grad = dot_tile(mixed[here, block], pairs[2 + e, :count, :], 1, 1)
+                row_dot = jnp.sum(prob * prob_grad, axis=-1, keepdims=True)
+                score_grad = (attention_mult * prob * (prob_grad - row_dot)).astype(bf16)
+                grad = grad + dot_tile(score_grad, pairs[e, :count, :], 1, 0)
+                acc[e, :count, :] += dot_tile(score_grad, q[here, block], 0, 0)
+                acc[2 + e, :count, :] += dot_tile(prob.astype(bf16), mixed[here, block], 0, 0)
+            dqkv[here, block] = (grad * cos_b + turn_lanes(grad * sin_b, quarter)).astype(bf16)
+
+    attend(0)
+    sides(1)
+    attend(1)
+    sides(0)
+    attend(2)
+    owners(3)
+    filled = blocks * rows
+    low = low_lanes((filled, 128), HEAD)
+    key_grad = jnp.where(low, acc[0], 0.0) + pltpu.roll(jnp.where(low, 0.0, acc[1]), HEAD, 1)
+    value_grad = jnp.where(low, 0.0, acc[3]) + pltpu.roll(jnp.where(low, acc[2], 0.0), HEAD, 1)
+    turned = turn_lanes(key_grad * sin[0:filled, :], low_lanes((filled, 128), HEAD // 2))
+    key_grad = key_grad * cos[0:filled, :] + turned
+    dqkv[0:filled, q_cols:] = jnp.where(low, key_grad, value_grad).astype(bf16)
+
+    crosses, outs = {}, {}
+    for k in (3, 1, 2, 0):
+        mine_rows = pl.ds(pl.multiple_of(flip(c, k) * rows, rows), rows)
+
+        def back_tile(n, carry, mine_rows=mine_rows):
+            here = pl.ds(pl.multiple_of(n * 128, 128), 128)
+            w = wa[lax.div(n, 4), lax.rem(n, 4), :, :qkv_cols]
+            sums[:, here] = dot_tile(dqkv[mine_rows, :], w, 1, 1)
+            return carry
+
+        lax.fori_loop(0, width // 128, back_tile, 0)
+        mine[k] = sums[pl.ds(pl.multiple_of(t * part, part), part), :]
+        cross[k] = sums[pl.ds(pl.multiple_of((1 - t) * part, part), part), :].astype(bf16)
+        crosses[k] = net.start(cross.at[k], crossed.at[k], core)
+    owners(2)
+    for k in (3, 1, 2):
+        crosses[k].wait_recv()
+        totals[k - 1] = (mine[k] + crossed[k].astype(f32)).astype(bf16)
+        outs[k] = net.start(totals.at[k - 1], back_in.at[k - 1], (z, flip(c, k), t))
+    crosses[0].wait_recv()
+    back_own[...] = mine[0] + crossed[0].astype(f32)
+
+    def qkv_term(m, carry):
+        here = pl.ds(pl.multiple_of(m * wrows, wrows), wrows)
+        left = normed[:, :, here].reshape(filled, wrows)
+        value = dot_tile(left, dqkv[0:filled, :], 0, 0)
+        at_terms[lax.div(m, 4), lax.rem(m, 4), :, :qkv_cols] = value.astype(bf16)
+        return carry
+
+    lax.fori_loop(0, width // wrows, qkv_term, 0)
+    attn_in = [net.start(at_terms.at[flip(z, k)], at_in.at[k - 1], (flip(z, k), c, t)) for k in (3, 2, 1)]
+    owners(1)
+    owners(0)
     for copy in attn_in:
         copy.wait_recv()
     for j in range(4):
@@ -851,70 +982,66 @@
         for i in range(3):
             total = total + at_in[i, j].astype(f32)
         at_total[j] = total.astype(bf16)
-    attn_out = [net.start(at_total.at[flip(c, k)], at_landed.at[c], (z, flip(c, k), t)) for k in (1, 2, 3)]
-    at_landed[c] = at_total[c]
-    third = {}
-    for k in order:
-        zs = flip(z, k)
-        for copy in second[k]:
-            copy.wait_recv()
-        total = terms[zs, c].astype(f32) + side_x[k].astype(f32) + side_y[k].astype(f32)
-        if k:
-            terms[zs, c] = total.astype(bf16)
-            third[k] = net.start(terms.at[zs, c], landed.at[k], (zs, c, t))
-        else:
-            landed[0] = total.astype(bf16)
-    size = gate_out.shape[1] // 4
-    for k in (0, 3, 2, 1):
-        if k:
-            third[k].wait_recv()
-        zs = flip(z, k)
-        columns = pl.ds(pl.multiple_of(zs * size, size), size)
-        for i, out in enumerate((gate_out, up_out, down_out)):
-            out[:, columns] = landed[k, :, i * size : (i + 1) * size]
-    for copy in attn_out:
+    attn_out = [net.start(at_total.at[flip(c, k)], at_out.at[c], (z, flip(c, k), t)) for k in (1, 2, 3)]
+    keep_own = pltpu.make_async_copy(at_total.at[c], at_out.at[c], local.at[7])
+    keep_own.start()
+    for copy in feed + attn_out + [outs[k] for k in (1, 2, 3)] + [third[k] for k in (1, 2, 3)]:
         copy.wait_recv()
-    begin = 0
-    for out in (query_out, key_out, value_out, output_out):
-        size = out.shape[1] // 4
-        for j in range(4):
-            out[:, j * size : (j + 1) * size] = at_landed[j, :, begin : begin + size]
-        begin += size
-    for copy in feed:
-        copy.wait_recv()
-    feed_out[...] = feed_in[0].astype(f32) + feed_in[1].astype(f32) + feed_in[2].astype(f32)
     for copy in net.started:
         copy.wait_send()
-
-
-def grads_out(ff, at, fs, sizes):
+    third[0].wait()
+    keep_own.wait()
+
+
+def backward(ff, fs, al, wa, normed, q, kv, logs, attended, cos, sin, seg_col, seg_row):
     bf16, f32 = jnp.bfloat16, jnp.float32
-    rows, cols = ff.shape[2:]
-    attn_cols = at.shape[3]
-    copies = 32
+    wrows, cols = ff.shape[2:]
+    attn_cols = wa.shape[3]
+    part, width = al.shape
+    total = q.shape[0]
+    filled = seg_col.shape[0]
+    rows = 2 * part
+    blocks = filled // rows
+    copies = 48
+    vmem, anywhere = pl.BlockSpec(memory_space=pltpu.VMEM), pl.BlockSpec(memory_space=pl.ANY)
     return pl.pallas_call(
-        grads_out_kernel,
-        out_shape=[jax.ShapeDtypeStruct(fs.shape[1:], f32)] + [jax.ShapeDtypeStruct((rows, s), bf16) for s in sizes],
-        in_specs=[pl.BlockSpec(memory_space=pl.ANY)] * 2 + [pl.BlockSpec(memory_space=pltpu.VMEM)],
-        out_specs=[pl.BlockSpec(memory_space=pltpu.VMEM)] * (1 + len(sizes)),
+        backward_kernel,
+        out_shape=[
+            jax.ShapeDtypeStruct(fs.shape, bf16),
+            jax.ShapeDtypeStruct(al.shape, f32),
+            jax.ShapeDtypeStruct(fs.shape, bf16),
+            jax.ShapeDtypeStruct((4, wrows, cols), bf16),
+            jax.ShapeDtypeStruct((4, wrows, attn_cols), bf16),
+        ],
+        in_specs=[anywhere, vmem, vmem, anywhere, anywhere] + [vmem] * 8,
+        out_specs=[anywhere, vmem, anywhere, anywhere, anywhere],
         scratch_shapes=[
-            pltpu.VMEM((4, 4, rows, cols), bf16),
-            pltpu.VMEM((4, rows // 2, cols), bf16),
-            pltpu.VMEM((4, rows // 2, cols), bf16),
-            pltpu.VMEM((4, rows, cols), bf16),
-            pltpu.VMEM((4, rows, cols), bf16),
-            pltpu.VMEM((4, rows, cols), bf16),
-            pltpu.VMEM(fs.shape, bf16),
-            pltpu.VMEM((4, 4, rows, attn_cols), bf16),
-            pltpu.VMEM((3, 4, rows, attn_cols), bf16),
-            pltpu.VMEM((4, rows, attn_cols), bf16),
-            pltpu.VMEM((4, rows, attn_cols), bf16),
+            pltpu.VMEM((4, 4, wrows, cols), bf16),
+            pltpu.VMEM((4, wrows // 2, cols), bf16),
+            pltpu.VMEM((4, wrows // 2, cols), bf16),
+            pltpu.VMEM((4, wrows, cols), bf16),
+            pltpu.VMEM((4, wrows, cols), bf16),
+            pltpu.VMEM((4, 4, wrows, attn_cols), bf16),
+            pltpu.VMEM((3, 4, wrows, attn_cols), bf16),
+            pltpu.VMEM((4, wrows, attn_cols), bf16),
+            pltpu.VMEM(wa.shape, bf16),
+            pltpu.VMEM((blocks, rows, width), bf16),
+            pltpu.VMEM((4, 2, part, width), bf16),
+            pltpu.VMEM((4, total, 2 * HEAD), bf16),
+            pltpu.VMEM((filled, q.shape[1]), bf16),
+            pltpu.VMEM((4, filled, 2 * HEAD), f32),
+            pltpu.VMEM((total, q.shape[1] + 2 * HEAD), bf16),
+            pltpu.VMEM((rows, width), f32),
+            pltpu.VMEM((4, part, width), f32),
+            pltpu.VMEM((4, part, width), bf16),
+            pltpu.VMEM((4, part, width), bf16),
+            pltpu.VMEM((3, part, width), bf16),
             pltpu.SemaphoreType.DMA((copies,)),
             pltpu.SemaphoreType.DMA((copies,)),
-            pltpu.SemaphoreType.DMA((5,)),
+            pltpu.SemaphoreType.DMA((8,)),
         ],
-        compiler_params=pltpu.CompilerParams(collective_id=2, has_side_effects=True, vmem_limit_bytes=60 * 2**20),
-    )(ff, at, fs)
+        compiler_params=pltpu.CompilerParams(collective_id=2, has_side_effects=True, vmem_limit_bytes=63 * 2**20),
+    )(ff, fs, al, wa, normed, q, kv, logs, attended, cos, sin, seg_col, seg_row)
 
 
 def on_device_split(
@@ -970,26 +1097,7 @@
         segment[:filled, None], segment[None, :filled],
     )
     gain_one, gain_two = gains[0], gains[1]
-    w_qkv = wa[..., :qkv_cols].reshape(width, qkv_cols)
-    w_out = wa[..., qkv_cols:].reshape(width, q_cols)
     w_feed = wf.reshape(width, 3 * ff_cols)
-    normed_one = normed_one.reshape(group_rows, width)
-    q_f = queries[:filled].reshape(filled, per_group, HEAD)
-    k_f, v_f = pair[:filled, :HEAD], pair[:filled, HEAD:]
-    attended_f = attended[:filled]
-    slot_ids = jnp.arange(filled, dtype=jnp.int32)
-    allowed = (segment[:filled, None] == segment[None, :filled]) & (slot_ids[:, None] >= slot_ids[None, :])
-
-    def scatter_context(partial):
-        partial = partial.reshape(nc, nt, part, width)
-        mine = cut(partial, t, 1, 1)[:, 0]
-        other = cut(partial, 1 - t, 1, 1)[:, 0].astype(bf16)
-        mine = mine + swap(other, TENSOR, 1).astype(f32)
-        total = cut(mine, c, 1, 0)[0]
-        for k in range(1, nc):
-            total = total + swap(cut(mine, c ^ k, 1, 0)[0].astype(bf16), CONTEXT, k).astype(f32)
-        return total
-
     my_inputs = cut(tokens[0], t, part, 0).astype(f32)
     inverse_two = lax.rsqrt(jnp.mean(hidden * hidden, axis=-1, keepdims=True) + norm_eps)
     unit_two = hidden * inverse_two
@@ -1007,34 +1115,12 @@
     hidden_grad = cotangent + norm_back(normed_grad_two, unit_two, gain_two, inverse_two)
 
     attn_low = (residual_mult * hidden_grad).astype(bf16)
-    attn_grad = jnp.zeros((nc, nt, part, width), bf16)
-    attn_grad = put(attn_grad, attn_low, c, t)
-    attn_grad = put(attn_grad, swap(attn_low, TENSOR, 1), c, 1 - t)
-    for k in range(1, nc):
-        block = swap(attn_low, CONTEXT, k)
-        attn_grad = put(attn_grad, block, c ^ k, t)
-        attn_grad = put(attn_grad, swap(block, TENSOR, 1), c ^ k, 1 - t)
-    attn_grad = attn_grad.reshape(group_rows, width)[:filled]
-
-    out_term = dot_first(attn_grad, attended_f)
-    mixed_grad = jnp.dot(attn_grad, w_out, preferred_element_type=f32).astype(bf16).reshape(filled, per_group, HEAD)
-    scores = jnp.einsum("tgd,sd->gts", q_f, k_f, preferred_element_type=f32)
-    scores = jnp.where(allowed[None], scores * attention_mult, -1e30)
-    probabilities = jnp.exp(scores - logs[:, :per_group].T[:, :, None])
-    prob_low = probabilities.astype(bf16)
-    prob_grad = jnp.einsum("tgd,sd->gts", mixed_grad, v_f, preferred_element_type=f32)
-    row_dot = jnp.sum(probabilities * prob_grad, axis=-1, keepdims=True)
-    score_grad = (attention_mult * probabilities * (prob_grad - row_dot)).astype(bf16)
-    query_grad = jnp.einsum("gts,sd->tgd", score_grad, k_f, preferred_element_type=f32)
-    key_grad = jnp.einsum("gts,tgd->sd", score_grad, q_f, preferred_element_type=f32)
-    value_grad = jnp.einsum("gts,tgd->sd", prob_low, mixed_grad, preferred_element_type=f32).astype(bf16)
-    cos_f, sine_f = cos_table[:filled], sine_table[:filled]
-    query_grad = rotate_back(query_grad, cos_f, sine_f).reshape(filled, q_cols).astype(bf16)
-    key_grad = rotate_back(key_grad[:, None], cos_f, sine_f)[:, 0].astype(bf16)
-    qkv_grad = jnp.concatenate([query_grad, key_grad, value_grad], axis=1)
-    normed_part = dot_last(qkv_grad, w_qkv)
-    normed_part = jnp.pad(normed_part, ((0, group_rows - filled), (0, 0)))
-    normed_grad_one = scatter_context(normed_part)
+    feed_in, back_own, back_in, ff_grads, attn_grads = backward(
+        ff_terms, feed_send, attn_low, wa, normed_one, queries, pair, logs, attended, wide_cos, wide_sin,
+        segment[:filled, None], segment[None, :filled],
+    )
+    output = both_cores((hidden + residual_mult * (feed_own + jnp.sum(feed_in.astype(f32), axis=0))).astype(bf16))
+    normed_grad_one = back_own + jnp.sum(back_in.astype(f32), axis=0)
     inverse_one = lax.rsqrt(jnp.mean(my_inputs * my_inputs, axis=-1, keepdims=True) + norm_eps)
     unit_one = my_inputs * inverse_one
     attn_gain_term = jnp.sum(normed_grad_one * unit_one, axis=0)
@@ -1045,13 +1131,12 @@
         gain_terms = gain_terms + swap(gain_terms, axis, k)
     gain_terms = cut(gain_terms, z * nc + c, wrows, 1)
 
-    qkv_term = dot_first(normed_one[:filled], qkv_grad)
-    terms = jnp.concatenate([qkv_term, out_term], axis=1).astype(bf16).reshape(nz, nc, wrows, -1)
-    sizes = [w.shape[1] for w in (gate_weight, up_weight, down_weight)]
-    sizes += [w.shape[1] for w in (query_weight, key_weight, value_weight, output_weight)]
-    feed_in, *weight_grads = grads_out(ff_terms, terms, feed_send, sizes)
-    grad_gate, grad_up, grad_down, *attn_terms = [g.astype(f32) for g in weight_grads]
-    output = both_cores((hidden + residual_mult * (feed_own + feed_in)).astype(bf16))
+    def columns(x, begin, size):
+        return x[:, :, begin : begin + size].transpose(1, 0, 2).reshape(wrows, -1).astype(f32)
+
+    grad_gate, grad_up, grad_down = (columns(ff_grads, i * ff_cols, ff_cols) for i in range(3))
+    begins = (0, q_cols, q_cols + kv_cols, qkv_cols)
+    attn_terms = [columns(attn_grads, i, n) for i, n in zip(begins, (q_cols, kv_cols, kv_cols, q_cols))]
     return (output, input_grad, gain_terms[0], *attn_terms, gain_terms[1], grad_gate, grad_up, grad_down)
 
 

time: 682 us -> 593 us (0.87)
  waiting for transfers between devices: 45.1 us -> 3.76 us
  Pallas kernels: 482 us -> 514 us
  local copies, waits for them, and re-layouts: 65 us -> 36.4 us
  matrix products: 21.7 us -> 0 us
  other arithmetic: 46 us -> 24.5 us
    ppermute x18 -> x7, waiting for transfers between devices: 45.1 us -> 3.76 us  [swap(): lax.ppermute(x, axis, [(i, i ^ k) for i in range(lax.axis_size(axis))])]
    pallas_call x1, Pallas kernels: 183 us -> 215 us  [backward(): pl.pallas_call(backward_kernel, out_shape=[jax.ShapeDtypeStruct(fs.shape,...]
    dot_general x9 -> x0, matrix products: 21.7 us -> none  [the longest x1 5.69 us: on_device_split(): jnp.einsum('tgd,sd->gts', mixed_grad, v_f, preferred_element_type=f32)]
    slice x8 -> x0, local copies, waits for them, and re-layouts: 12.9 us -> none  [the longest x1 4.06 us: on_device_split(): qkv_term = dot_first(normed_one[:filled], qkv_grad)]
    convert_element_type x10 -> x4, other arithmetic: 17.6 us -> 5.36 us  [the longest x3 3.79 us: columns(): x[:, :, begin:begin + size].transpose(1, 0, 2).reshape(wrows, -1)]
    dot_general x2 -> x0, local copies, waits for them, and re-layouts: 9.5 us -> none  [dot_first(): lax.dot_general(left, right, (((0,), (0,)), ((), ())), preferred_element_...]
    dynamic_update_slice x9 -> x2, local copies, waits for them, and re-layouts: 10.3 us -> 2.96 us  [put(): return lax.dynamic_update_slice(buffer, block, start)]
    unnamed x79 -> x56, local copies, waits for them, and re-layouts: 17.7 us -> 20.2 us
  transfers between devices with their start and end apart: 18 -> 7, of which waited for: 9 -> 2; matrix products, arithmetic and copies ran while one was open for 7% -> 5% of each run, Pallas kernels for 27% -> 0%
where the time goes in v5:
time: 593 us; the launch traced here: 585 us
  Pallas kernels  514 us (87%)
  local copies, waits for them, and re-layouts  36.4 us (6%)
  other arithmetic  24.5 us (4%)
    pallas_call x1, Pallas kernels, backward(): pl.pallas_call(backward_kernel, out_shape=[jax.ShapeDtypeStruct(fs.shape,...  215 us
    pallas_call x1, Pallas kernels, attention_forward(): pl.pallas_call(attention_kernel, out_shape=[jax.ShapeDtypeStruct(shape, d...  196 us
    pallas_call x1, Pallas kernels, feed_forward(): pl.pallas_call(feed_kernel, out_shape=[jax.ShapeDtypeStruct((part, width)...  103 us
    unnamed x56, local copies, waits for them, and re-layouts  20.2 us
  transfers between devices with their start and end apart: 7, of which 2 were waited for; matrix products, arithmetic and copies ran while one was open for 5% of the time, Pallas kernels for 0%

profile of v5, /device:TPU:0, one launch (start us, length us, event | category | flops | bytes accessed | tf_op | source)
XLA Modules:
  0.0 585.1 jit_solution(3266406256576629328)
XLA Ops:
  3.8 1.8 copy.63
  6.2 1.8 copy.65
  8.5 1.8 copy.61
  10.4 1.3 copy.62
  11.7 1.2 copy.53
  13.1 1.2 copy.59
  15.3 2.0 sine_multiply_fusion
  17.3 1.3 pad_maximum_fusion.3
  19.3 1.8 pad_maximum_fusion.wf
  21.9 1.0 fusion.9
  24.0 196.3 %shard_map.203 = (bf16[4,4,128,640]{3,2,1,0:T(8,128)(2,1)}, bf16[4,4,128,3072]{3,2,1,0:T(8,128)(2,1)}, bf16[4,256,2048]{2,1,0:T(8,128)(2,1)}, bf16[1024,256]{1,0...) custom-call(bf16[4,128,640]{2,1,0:T(8,128)(2,1)} %pad_maximum_fusion, ...), custom_call_target="tpu_custom_call" | custom-call | tf_op jit(solution)/shard_map/pallas_call | solution.py:604
  220.3 1.4 multiply_reduce_fusion.2
  222.5 102.6 %shard_map.204 = (f32[128,2048]{1,0:T(8,128)}, f32[128,2048]{1,0:T(8,128)}, bf16[3,128,2048]{2,1,0:T(8,128)(2,1)}, bf16[2048,3072]{1,0:T(8,128)(2,1)}) custom-call(bf16[128,2048]{1,0:T(8,128)(2,1)} %get-tuple-element.32.x, bf16[4,256,2048]{2,1,0:T(8,128)(2,1)} %bitcast.94, bf16[2048,3072]{1,0:T(8,128)(2,1)} %bitcast.83), custom_call_target="tpu_custom_call" | custom-call | tf_op jit(solution)/shard_map/pallas_call | solution.py:760
  325.2 1.7 multiply_reduce_fusion
  327.0 1.6 multiply_convert_fusion
  328.6 215.3 %shard_map.205 = (bf16[3,128,2048]{2,1,0:T(8,128)(2,1)}, f32[128,2048]{1,0:T(8,128)}, bf16[3,128,2048]{2,1,0:T(8,128)(2,1)}, bf16[4,128,3072]{2,1,0:T(8,128)(2,1)}, bf16[4,128,640]{2,1,0:T(8,128)(2,1)}) custom-call(bf16[4,4,128,3072]{3,2,1,0:T(8,128)(2,1)} %bitcast.82, bf16[3,128,2048]{2,1,0:T(8,128)(2,1)} %get-tuple-element.37.fs, ...), custom_call_target="tpu_custom_call" | custom-call | tf_op jit(solution)/shard_map/pallas_call | solution.py:1007
  544.0 1.9 convert_reduce_fusion
  546.5 1.1 broadcast.75.clone.1
  547.6 2.7 bitcast_dynamic-update-slice_fusion.1
  551.1 1.5 collective-permute-start.3
  552.7 1.0 bitcast_dynamic-update-slice_fusion.3
  554.9 1.6 collective-permute-start.4
  556.5 2.9 convert_bitcast_fusion
  559.7 3.6 collective-permute-done.5
  564.9 1.9 copy.73
  566.8 1.8 copy.80
  568.6 1.9 copy.74
  570.5 1.8 copy.81
  572.3 1.9 copy.75
  574.2 1.8 copy.82
  580.7 1.9 bitcast_dynamic-update-slice_fusion
  582.6 1.1 bitcast_dynamic-update-slice_fusion.2
  (101 shorter events, 18.7 us)
Async XLA Ops:
  10.4 4.1 copy-start.17
  10.4 4.3 copy-start.18
  15.1 3.6 copy-start.19
  15.1 3.6 copy-start.20
  15.1 4.2 copy-start.5
  19.3 1.8 copy-start.2
  19.3 2.7 copy-start.14
  222.5 102.6 %copy-start = (f32[128,2048]{1,0:T(8,128)S(1)}, f32[128,2048]{1,0:T(8,128)}, u32[]{:S(2)}) copy-start(f32[128,2048]{1,0:T(8,128)} %get-tuple-element.31) | copy-start | bytes 3145732
  325.2 1.8 copy-start.6
  325.2 1.8 copy-start.15
  543.9 2.0 copy-start.3
  543.9 2.0 copy-start.4
  546.4 4.6 collective-permute-start.2
  547.6 3.2 copy-start.8
  550.3 2.5 copy-start.1
  550.3 2.5 copy-start.9
  550.3 30.5 %collective-permute-start.1 = (bf16[128,2048]{1,0:T(8,128)(2,1)}, bf16[128,2048]{1,0:T(8,128)(2,1)}, u32[]{:S(2)}, u32[]{:S(2)}) collective-permute-start(bf16[128,2048]{1,0:T(8,128)(2,1)} %get-tuple-element.80), channel_id=1, source_target_pairs={{0,1},{1,0},{2,3},{3,2},{4,5},{5,4},{6,7},{7,6},{8,9},{9,8},{10,11... | collective-permute-start | bytes 1572872 | tf_op jit(solution)/shard_map/ppermute | solution.py:790
  551.1 3.8 collective-permute-start.3
  552.7 3.8 copy-start.7
  553.8 1.0 copy-start.11
  554.7 27.9 %collective-permute-start = (bf16[128,2048]{1,0:T(8,128)(2,1)}, bf16[128,2048]{1,0:T(8,128)(2,1)}, u32[]{:S(2)}, u32[]{:S(2)}) collective-permute-start(bf16[128,2048]{1,0:T(8,128)(2,1)} %get-tuple-element.82), channel_id=1, source_target_pairs={{0,1},{1,0},{2,3},{3,2},{4,5},{5,4},{6,7},{7,6},{8,9},{9,8},{10,11... | collective-permute-start | bytes 1572872 | tf_op jit(solution)/shard_map/ppermute | solution.py:790
  554.9 4.5 collective-permute-start.4
  556.5 3.0 copy-start.16
  559.5 3.8 collective-permute-start.5
  563.3 16.9 %collective-permute-start.6 = (f32[2,2048]{1,0:T(2,128)S(1)}, f32[2,2048]{1,0:T(2,128)S(1)}, u32[]{:S(2)}, u32[]{:S(2)}) collective-permute-start(f32[2,2048]{1,0:T(2,128)S(1)} %add.92), channel_id=1, source_target_pairs={{0,16},{8,24},{16,0},{24,8},{1,17},{9,25},{17,1},{25,9},{2,18},{10... | collective-permute-start | bytes 49160 | tf_op jit(solution)/shard_map/ppermute | solution.py:790
  576.0 2.4 copy-start.10
  577.2 5.4 copy-start.12
  583.7 1.0 copy-start.13

commit v6 on v5

--- a/solution.py
+++ b/solution.py
@@ -375,6 +375,11 @@
     nt, part, width = xt.shape
     rows = nt * part
     q_cols = q.shape[1]
+    hidden = wf_all.shape[4]
+
+    def columns(owner):
+        return pl.ds(pl.multiple_of(owner * hidden, hidden), hidden)
+
     qkv_cols = q_cols + 2 * HEAD
     ends = []
     own = []
@@ -382,7 +387,7 @@
         (
             (wa.at[c], wa_all.at[z, c]),
             (xt, x_all.at[c]),
-            (wf.at[z], wf_all.at[z, c]),
+            (wf.at[:, :, columns(z)], wf_all.at[:, z, c]),
             (gain, gain_all.at[z, c]),
             (fgx, fg_all.at[0, 0]),
         )
@@ -408,11 +413,23 @@
 
     attn_in = [net.start(wa.at[flip(c, k)], wa_all.at[z, c], (z, flip(c, k), t)) for k in (1, 2, 3)]
     tokens_in = [net.start(xt.at[t], x_all.at[c, t], (z, flip(c, k), t)) for k in (1, 2, 3)]
-    ff_in = {1: net.start(wf.at[flip(z, 1)], wf_all.at[z, c], (flip(z, 1), c, t))}
+    parts = {k: (0, 1, 2) if k == 2 else (slice(None),) for k in range(4)}
+
+    def weights_to(k):
+        there = columns(flip(z, k))
+        return [net.start(wf.at[m, :, there], wf_all.at[m, z, c], (flip(z, k), c, t)) for m in parts[k]]
+
+    ff_in = {1: weights_to(1)}
     for device in peers:
         ends.append(net.start(gain, gain_all.at[z, c], device))
     own[2].wait()
-    ff_out = {0: [net.start(wf_all.at[z, c], wf_all.at[z, c], (z, flip(c, k), t)) for k in (1, 2)]}
+    ff_out = {}
+
+    def pass_on(k, m):
+        piece = wf_all.at[m, flip(z, k), c]
+        ff_out.setdefault(k, []).append([net.start(piece, piece, (z, flip(c, j), t)) for j in (1, 2)])
+
+    pass_on(0, slice(None))
     weights = []
     for j in range(4):
         if j:
@@ -423,7 +440,7 @@
         passed_piece = wa_all.at[flip(z, 2), flip(c, j)]
         weights.append(spread(piece, lambda k, piece=piece: piece, (passed_piece, passed_piece)))
     for k in (3, 2):
-        ff_in[k] = net.start(wf.at[flip(z, k)], wf_all.at[z, c], (flip(z, k), c, t))
+        ff_in[k] = weights_to(k)
     feed = spread(fgx, lambda k: fg_all.at[k, 0], (fg_all.at[2, 0], fg_all.at[3, 0]))
     swaps = [net.start(fgx, fg_all.at[0, 1], core)]
     token_swaps = []
@@ -435,18 +452,18 @@
 
     def corner(k):
         zs = flip(z, k)
-        one, two = ff_out[k]
-        two.wait_recv()
-        piece = wf_all.at[zs, flip(c, 2), pl.ds(0, 64)]
-        halves.append(net.start(piece, piece, (z, flip(c, 1), t)))
-        one.wait_recv()
-        piece = wf_all.at[zs, flip(c, 1), pl.ds(64, 64)]
-        halves.append(net.start(piece, piece, (z, flip(c, 2), t)))
+        for m, (one, two) in zip(parts[k], ff_out[k]):
+            two.wait_recv()
+            piece = wf_all.at[m, zs, flip(c, 2), pl.ds(0, 64)]
+            halves.append(net.start(piece, piece, (z, flip(c, 1), t)))
+            one.wait_recv()
+            piece = wf_all.at[m, zs, flip(c, 1), pl.ds(64, 64)]
+            halves.append(net.start(piece, piece, (z, flip(c, 2), t)))
 
     def onward(k):
-        ff_in[k].wait_recv()
-        piece = wf_all.at[flip(z, k), c]
-        ff_out[k] = [net.start(piece, piece, (z, flip(c, j), t)) for j in (1, 2)]
+        for m, copy in zip(parts[k], ff_in[k]):
+            copy.wait_recv()
+            pass_on(k, m)
 
     own[1].wait()
     own[3].wait()
@@ -586,11 +603,11 @@
     wa_cols = wa.shape[2]
     q_cols = (wa_cols - 2 * HEAD) // 2
     filled = seg_col.shape[0]
-    copies = 96
+    copies = 112
     vmem, anywhere = pl.BlockSpec(memory_space=pltpu.VMEM), pl.BlockSpec(memory_space=pl.ANY)
     outs = (
         ((4, 4) + wa.shape[1:], bf16, anywhere),
-        ((4, 4) + wf.shape[1:], bf16, anywhere),
+        ((3, 4, 4, wf.shape[1], wf.shape[2] // 4), bf16, anywhere),
         ((4, rows, width), bf16, anywhere),
         ((total, q_cols), bf16, vmem),
         ((total, 2 * HEAD), bf16, vmem),
@@ -636,7 +653,7 @@
     greet([(flip(z, k), c, t) for k in (1, 2, 3)] + [core])
     net = Copies(send, receive)
     part, width = x.shape
-    hidden = wv.shape[1] // 3
+    hidden = wv.shape[2]
     load = pltpu.make_async_copy(w, wv, local.at[0])
     load.start()
     middle = (z == 1) | (z == 2)
@@ -665,9 +682,9 @@
 
         def step(n, carry):
             at = pl.multiple_of(n * TILE, TILE)
-            g = dot_tile(rows, wv[:, pl.ds(at, TILE)], 1, 0)
-            u = dot_tile(rows, wv[:, pl.ds(hidden + at, TILE)], 1, 0)
-            d = dot_tile(grads, wv[:, pl.ds(2 * hidden + at, TILE)], 1, 0)
+            g = dot_tile(rows, wv[0, :, pl.ds(at, TILE)], 1, 0)
+            u = dot_tile(rows, wv[1, :, pl.ds(at, TILE)], 1, 0)
+            d = dot_tile(grads, wv[2, :, pl.ds(at, TILE)], 1, 0)
             sig = jax.nn.sigmoid(g)
             here = pl.ds(at, TILE)
             inner[k, :, here] = (g * sig * u).astype(bf16)
@@ -682,8 +699,8 @@
     def second(k):
         def step(n, carry):
             here = pl.ds(pl.multiple_of(n * TILE, TILE), TILE)
-            b = dot_tile(gate_g[k], wv[here, 0:hidden], 1, 1) + dot_tile(up_g[k], wv[here, hidden : 2 * hidden], 1, 1)
-            f = dot_tile(inner[k], wv[here, 2 * hidden :], 1, 1)
+            b = dot_tile(gate_g[k], wv[0, here, :], 1, 1) + dot_tile(up_g[k], wv[1, here, :], 1, 1)
+            f = dot_tile(inner[k], wv[2, here, :], 1, 1)
             mine[k, 0, :, here] = b[:part]
             mine[k, 1, :, here] = f[:part]
             cross[k, 0, :, here] = b[part:].astype(bf16)
@@ -722,12 +739,12 @@
 
     rows = xs.shape[0] * 2 * part
 
-    def term(source, grads, begin):
+    def term(source, grads, i):
         def step(m, carry):
             here = pl.ds(pl.multiple_of(m * TILE, TILE), TILE)
             left = source[:, :, here].reshape(rows, TILE)
             value = dot_tile(left, grads[...].reshape(rows, hidden), 0, 0)
-            wv[here, begin : begin + hidden] = value.astype(bf16)
+            wv[i, here, :] = value.astype(bf16)
             return carry
 
         lax.fori_loop(0, width // TILE, step, 0)
@@ -735,8 +752,8 @@
     flat = xs.reshape(xs.shape[0], 2 * part, width)
     term(flat, gate_g, 0)
     finish(order[3])
-    term(flat, up_g, hidden)
-    term(fg, inner, 2 * hidden)
+    term(flat, up_g, 1)
+    term(fg, inner, 2)
     store = pltpu.make_async_copy(wv, terms, local.at[1])
     store.start()
     for k in (1, 2, 3):
@@ -752,8 +769,7 @@
 def feed_forward(x, fg, w):
     bf16, f32 = jnp.bfloat16, jnp.float32
     part, width = x.shape
-    cols = w.shape[1]
-    hidden = cols // 3
+    hidden = w.shape[2]
     blocks = fg.shape[0]
     copies = 20
     vmem, anywhere = pl.BlockSpec(memory_space=pltpu.VMEM), pl.BlockSpec(memory_space=pl.ANY)
@@ -790,21 +806,13 @@
     return lax.ppermute(x, axis, [(i, i ^ k) for i in range(lax.axis_size(axis))])
 
 
-def put(buffer, block, *index):
-    lead = len(index)
-    block = block.reshape((1,) * lead + buffer.shape[lead:])
-    zero = jnp.int32(0)
-    start = tuple(jnp.asarray(i, jnp.int32) for i in index) + (zero,) * (buffer.ndim - lead)
-    return lax.dynamic_update_slice(buffer, block, start)
-
-
 def cut(x, index, size, axis):
     return lax.dynamic_slice_in_dim(x, index * size, size, axis)
 
 
 def backward_kernel(
     ff, fs, al, wa_in, normed_in, q, kv, logs, attended, cos, sin, seg_col, seg_row,
-    feed_in, back_own, back_in, ff_out, at_out,
+    feed_in, back_own, back_in, ff_out, query_out, kv_out, output_out,
     terms, corner_x, corner_y, side_x, side_y, at_terms, at_in, at_total, wa, normed, ag, pairs, mixed, acc, dqkv,
     sums, mine, cross, crossed, totals, send, receive, local,
 ):
@@ -813,7 +821,7 @@
     core = (z, c, 1 - t)
     greet([(flip(z, k), c, t) for k in (1, 2, 3)] + [(z, flip(c, k), t) for k in (1, 2, 3)] + [core])
     net = Copies(send, receive)
-    wrows = ff.shape[2]
+    wrows, hidden = ff.shape[3:]
     half = wrows // 2
     part, width = al.shape
     rows = 2 * part
@@ -824,23 +832,27 @@
     loads = {}
     for k in order:
         zs = flip(z, k)
-        loads[k] = pltpu.make_async_copy(ff.at[zs], terms.at[zs], local.at[k])
+        loads[k] = pltpu.make_async_copy(ff.at[:, zs], terms.at[:, zs], local.at[k])
         loads[k].start()
     wa_load = pltpu.make_async_copy(wa_in, wa, local.at[4])
     wa_load.start()
     normed_load = pltpu.make_async_copy(normed_in.at[pl.ds(0, blocks)], normed, local.at[5])
     normed_load.start()
+    first = {}
+
+    def corners(k):
+        zs = flip(z, k)
+        loads[k].wait()
+        first[k] = (
+            net.start(terms.at[:, zs, flip(c, 3), pl.ds(0, half)], corner_x.at[k], (z, flip(c, 1), t)),
+            net.start(terms.at[:, zs, flip(c, 3), pl.ds(half, half)], corner_y.at[k], (z, flip(c, 2), t)),
+        )
+
+    corners(3)
     ag_in = [net.start(al, ag.at[c, t], (z, flip(c, k), t)) for k in (3, 1, 2)]
     swaps = [net.start(al, ag.at[c, t], core)]
     feed = [net.start(fs.at[k - 1], feed_in.at[k - 1], (flip(z, k), c, t)) for k in (3, 2, 1)]
-    first = {}
-    for k in order:
-        zs = flip(z, k)
-        loads[k].wait()
-        first[k] = (
-            net.start(terms.at[zs, flip(c, 3), pl.ds(0, half)], corner_x.at[k], (z, flip(c, 1), t)),
-            net.start(terms.at[zs, flip(c, 3), pl.ds(half, half)], corner_y.at[k], (z, flip(c, 2), t)),
-        )
+    corners(2)
     ag[c, t] = al[...]
     for j, piece in enumerate(split_pair(kv[...].astype(f32))):
         pairs[j] = piece.astype(bf16)
@@ -858,23 +870,26 @@
             copy.wait_recv()
         low, high = pl.ds(0, half), pl.ds(half, half)
         xb, yb = flip(c, 1), flip(c, 2)
-        terms[zs, yb, low] = (terms[zs, yb, low].astype(f32) + corner_x[k].astype(f32)).astype(bf16)
-        terms[zs, xb, high] = (terms[zs, xb, high].astype(f32) + corner_y[k].astype(f32)).astype(bf16)
+        for m in range(3):
+            terms[m, zs, yb, low] = (terms[m, zs, yb, low].astype(f32) + corner_x[k, m].astype(f32)).astype(bf16)
+            terms[m, zs, xb, high] = (terms[m, zs, xb, high].astype(f32) + corner_y[k, m].astype(f32)).astype(bf16)
         second[k] = (
-            net.start(terms.at[zs, yb], side_y.at[k], (z, yb, t)),
-            net.start(terms.at[zs, xb], side_x.at[k], (z, xb, t)),
+            net.start(terms.at[:, zs, yb], side_y.at[k], (z, yb, t)),
+            net.start(terms.at[:, zs, xb], side_x.at[k], (z, xb, t)),
         )
 
     def owners(k):
         zs = flip(z, k)
         for copy in second[k]:
             copy.wait_recv()
-        total = terms[zs, c].astype(f32) + side_x[k].astype(f32) + side_y[k].astype(f32)
-        terms[zs, c] = total.astype(bf16)
+        for m in range(3):
+            total = terms[m, zs, c].astype(f32) + side_x[k, m].astype(f32) + side_y[k, m].astype(f32)
+            terms[m, zs, c] = total.astype(bf16)
+        columns = ff_out.at[:, :, pl.ds(pl.multiple_of(z * hidden, hidden), hidden)]
         if k:
-            third[k] = net.start(terms.at[zs, c], ff_out.at[z], (zs, c, t))
+            third[k] = net.start(terms.at[:, zs, c], columns, (zs, c, t))
         else:
-            third[0] = pltpu.make_async_copy(terms.at[z, c], ff_out.at[z], local.at[6])
+            third[0] = pltpu.make_async_copy(terms.at[:, z, c], columns, local.at[6])
             third[0].start()
 
     for copy in swaps:
@@ -890,6 +905,7 @@
 
     lax.fori_loop(0, blocks, mix, 0)
     sides(3)
+    corners(1)
 
     def out_term(m, carry):
         here = pl.ds(pl.multiple_of(m * wrows, wrows), wrows)
@@ -899,7 +915,18 @@
         return carry
 
     lax.fori_loop(0, width // wrows, out_term, 0)
+
+    def terms_to(columns):
+        return [
+            net.start(
+                at_terms.at[flip(z, k), :, :, columns], at_in.at[k - 1, :, :, columns], (flip(z, k), c, t)
+            )
+            for k in (3, 2, 1)
+        ]
+
+    attn_in = terms_to(pl.ds(qkv_cols, q_cols))
     sides(2)
+    corners(0)
 
     def attend(i):
         count = (i + 1) * rows
@@ -929,11 +956,12 @@
             dqkv[here, block] = (grad * cos_b + turn_lanes(grad * sin_b, quarter)).astype(bf16)
 
     attend(0)
+    attend(1)
+    owners(3)
     sides(1)
-    attend(1)
+    attend(2)
     sides(0)
-    attend(2)
-    owners(3)
+    owners(2)
     filled = blocks * rows
     low = low_lanes((filled, 128), HEAD)
     key_grad = jnp.where(low, acc[0], 0.0) + pltpu.roll(jnp.where(low, 0.0, acc[1]), HEAD, 1)
@@ -956,7 +984,6 @@
         mine[k] = sums[pl.ds(pl.multiple_of(t * part, part), part), :]
         cross[k] = sums[pl.ds(pl.multiple_of((1 - t) * part, part), part), :].astype(bf16)
         crosses[k] = net.start(cross.at[k], crossed.at[k], core)
-    owners(2)
     for k in (3, 1, 2):
         crosses[k].wait_recv()
         totals[k - 1] = (mine[k] + crossed[k].astype(f32)).astype(bf16)
@@ -972,7 +999,7 @@
         return carry
 
     lax.fori_loop(0, width // wrows, qkv_term, 0)
-    attn_in = [net.start(at_terms.at[flip(z, k)], at_in.at[k - 1], (flip(z, k), c, t)) for k in (3, 2, 1)]
+    attn_in += terms_to(pl.ds(0, qkv_cols))
     owners(1)
     owners(0)
     for copy in attn_in:
@@ -982,27 +1009,37 @@
         for i in range(3):
             total = total + at_in[i, j].astype(f32)
         at_total[j] = total.astype(bf16)
-    attn_out = [net.start(at_total.at[flip(c, k)], at_out.at[c], (z, flip(c, k), t)) for k in (1, 2, 3)]
-    keep_own = pltpu.make_async_copy(at_total.at[c], at_out.at[c], local.at[7])
-    keep_own.start()
+    here = pl.ds(pl.multiple_of(c * q_cols, q_cols), q_cols)
+    attn_out, keep_own = [], []
+    for i, (columns, target) in enumerate(
+        (
+            (pl.ds(0, q_cols), query_out.at[:, here]),
+            (pl.ds(q_cols, 2 * HEAD), kv_out.at[c]),
+            (pl.ds(qkv_cols, q_cols), output_out.at[:, here]),
+        )
+    ):
+        attn_out += [net.start(at_total.at[flip(c, k), :, columns], target, (z, flip(c, k), t)) for k in (1, 2, 3)]
+        keep_own.append(pltpu.make_async_copy(at_total.at[c, :, columns], target, local.at[7 + i]))
+        keep_own[-1].start()
     for copy in feed + attn_out + [outs[k] for k in (1, 2, 3)] + [third[k] for k in (1, 2, 3)]:
         copy.wait_recv()
     for copy in net.started:
         copy.wait_send()
     third[0].wait()
-    keep_own.wait()
+    for copy in keep_own:
+        copy.wait()
 
 
 def backward(ff, fs, al, wa, normed, q, kv, logs, attended, cos, sin, seg_col, seg_row):
     bf16, f32 = jnp.bfloat16, jnp.float32
-    wrows, cols = ff.shape[2:]
+    wrows, hidden = ff.shape[3:]
     attn_cols = wa.shape[3]
     part, width = al.shape
     total = q.shape[0]
     filled = seg_col.shape[0]
     rows = 2 * part
     blocks = filled // rows
-    copies = 48
+    copies = 64
     vmem, anywhere = pl.BlockSpec(memory_space=pltpu.VMEM), pl.BlockSpec(memory_space=pl.ANY)
     return pl.pallas_call(
         backward_kernel,
@@ -1010,17 +1047,19 @@
             jax.ShapeDtypeStruct(fs.shape, bf16),
             jax.ShapeDtypeStruct(al.shape, f32),
             jax.ShapeDtypeStruct(fs.shape, bf16),
-            jax.ShapeDtypeStruct((4, wrows, cols), bf16),
-            jax.ShapeDtypeStruct((4, wrows, attn_cols), bf16),
+            jax.ShapeDtypeStruct((3, wrows, 4 * hidden), bf16),
+            jax.ShapeDtypeStruct((wrows, 4 * q.shape[1]), bf16),
+            jax.ShapeDtypeStruct((4, wrows, 2 * HEAD), bf16),
+            jax.ShapeDtypeStruct((wrows, 4 * q.shape[1]), bf16),
         ],
         in_specs=[anywhere, vmem, vmem, anywhere, anywhere] + [vmem] * 8,
-        out_specs=[anywhere, vmem, anywhere, anywhere, anywhere],
+        out_specs=[anywhere, vmem] + [anywhere] * 5,
         scratch_shapes=[
-            pltpu.VMEM((4, 4, wrows, cols), bf16),
-            pltpu.VMEM((4, wrows // 2, cols), bf16),
-            pltpu.VMEM((4, wrows // 2, cols), bf16),
-            pltpu.VMEM((4, wrows, cols), bf16),
-            pltpu.VMEM((4, wrows, cols), bf16),
+            pltpu.VMEM(ff.shape, bf16),
+            pltpu.VMEM((4, 3, wrows // 2, hidden), bf16),
+            pltpu.VMEM((4, 3, wrows // 2, hidden), bf16),
+            pltpu.VMEM((4, 3, wrows, hidden), bf16),
+            pltpu.VMEM((4, 3, wrows, hidden), bf16),
             pltpu.VMEM((4, 4, wrows, attn_cols), bf16),
             pltpu.VMEM((3, 4, wrows, attn_cols), bf16),
             pltpu.VMEM((4, wrows, attn_cols), bf16),
@@ -1038,7 +1077,7 @@
             pltpu.VMEM((3, part, width), bf16),
             pltpu.SemaphoreType.DMA((copies,)),
             pltpu.SemaphoreType.DMA((copies,)),
-            pltpu.SemaphoreType.DMA((8,)),
+            pltpu.SemaphoreType.DMA((10,)),
         ],
         compiler_params=pltpu.CompilerParams(collective_id=2, has_side_effects=True, vmem_limit_bytes=63 * 2**20),
     )(ff, fs, al, wa, normed, q, kv, logs, attended, cos, sin, seg_col, seg_row)
@@ -1081,10 +1120,7 @@
         ],
         axis=2,
     )
-    wf = jnp.concatenate(
-        [w.astype(bf16).reshape(wrows, nz, ff_cols).transpose(1, 0, 2) for w in (gate_weight, up_weight, down_weight)],
-        axis=2,
-    )
+    wf = jnp.stack([w.astype(bf16) for w in (gate_weight, up_weight, down_weight)])
     gain = jnp.pad(jnp.stack([attention_gain, feed_gain]).astype(bf16), ((0, 14), (0, 0)))
     my_valid = lax.dynamic_slice_in_dim(valid_rows, c * local_rows + t * part, part)
     cotangent = cut(out_grad[0], t, part, 0).astype(f32) * my_valid[:, None].astype(f32)
@@ -1097,7 +1133,7 @@
         segment[:filled, None], segment[None, :filled],
     )
     gain_one, gain_two = gains[0], gains[1]
-    w_feed = wf.reshape(width, 3 * ff_cols)
+    w_feed = wf.reshape(3, width, ff_cols)
     my_inputs = cut(tokens[0], t, part, 0).astype(f32)
     inverse_two = lax.rsqrt(jnp.mean(hidden * hidden, axis=-1, keepdims=True) + norm_eps)
     unit_two = hidden * inverse_two
@@ -1105,17 +1141,18 @@
     normed_grad_two, feed_own, feed_send, ff_terms = feed_forward(
         normed_two, feed_grads.reshape(nz, local_rows, width), w_feed
     )
-    ff_terms = ff_terms.reshape(nz, nc, wrows, 3 * ff_cols)
+    ff_terms = ff_terms.reshape(3, nz, nc, wrows, ff_cols)
 
     def both_cores(x):
-        out = put(jnp.zeros((nt,) + x.shape, x.dtype), x, t)
-        return put(out, swap(x, TENSOR, 1), 1 - t).reshape(1, local_rows, width)
+        other = swap(x, TENSOR, 1)
+        first, last = jnp.where(t == 0, x, other), jnp.where(t == 0, other, x)
+        return jnp.concatenate([first, last], axis=0)[None]
 
     feed_gain_term = jnp.sum(normed_grad_two * unit_two, axis=0)
     hidden_grad = cotangent + norm_back(normed_grad_two, unit_two, gain_two, inverse_two)
 
     attn_low = (residual_mult * hidden_grad).astype(bf16)
-    feed_in, back_own, back_in, ff_grads, attn_grads = backward(
+    feed_in, back_own, back_in, ff_grads, grad_query, kv_grads, grad_output = backward(
         ff_terms, feed_send, attn_low, wa, normed_one, queries, pair, logs, attended, wide_cos, wide_sin,
         segment[:filled, None], segment[None, :filled],
     )
@@ -1127,16 +1164,15 @@
     input_grad = both_cores((hidden_grad + norm_back(normed_grad_one, unit_one, gain_one, inverse_one)).astype(bf16))
 
     gain_terms = jnp.stack([attn_gain_term, feed_gain_term])
-    for axis, k in ((TENSOR, 1), (CONTEXT, 1), (CONTEXT, 2), (FSDP, 1), (FSDP, 2)):
-        gain_terms = gain_terms + swap(gain_terms, axis, k)
+    for axis in (TENSOR, CONTEXT, FSDP):
+        gain_terms = gain_terms + sum(swap(gain_terms, axis, k) for k in range(1, lax.axis_size(axis)))
     gain_terms = cut(gain_terms, z * nc + c, wrows, 1)
 
-    def columns(x, begin, size):
-        return x[:, :, begin : begin + size].transpose(1, 0, 2).reshape(wrows, -1).astype(f32)
-
-    grad_gate, grad_up, grad_down = (columns(ff_grads, i * ff_cols, ff_cols) for i in range(3))
-    begins = (0, q_cols, q_cols + kv_cols, qkv_cols)
-    attn_terms = [columns(attn_grads, i, n) for i, n in zip(begins, (q_cols, kv_cols, kv_cols, q_cols))]
+    grad_gate, grad_up, grad_down = (ff_grads[i].astype(f32) for i in range(3))
+    grad_key, grad_value = (
+        kv_grads[:, :, i : i + HEAD].transpose(1, 0, 2).reshape(wrows, -1).astype(f32) for i in (0, HEAD)
+    )
+    attn_terms = (grad_query.astype(f32), grad_key, grad_value, grad_output.astype(f32))
     return (output, input_grad, gain_terms[0], *attn_terms, gain_terms[1], grad_gate, grad_up, grad_down)
 
 

time: 593 us -> 544 us (0.917)
  Pallas kernels: 514 us -> 485 us
  local copies, waits for them, and re-layouts: 36.4 us -> 11.7 us
    pallas_call x1, Pallas kernels: 215 us -> 188 us  [backward(): pl.pallas_call(backward_kernel, out_shape=[jax.ShapeDtypeStruct(fs.shape,...]
    unnamed x56 -> x50, local copies, waits for them, and re-layouts: 20.2 us -> 6.73 us
    convert_element_type x7 -> x2, local copies, waits for them, and re-layouts: 6.31 us -> 0.22 us  [on_device_split(): kv_grads[:, :, i:i + HEAD].transpose(1, 0, 2).reshape(wrows, -1).astype(f32)]
  transfers between devices with their start and end apart: 7 -> 9, of which waited for: 2 -> 2; matrix products, arithmetic and copies ran while one was open for 5% -> 2% of each run, Pallas kernels for 0% -> 0%
where the time goes in v6:
time: 544 us; the launch traced here: 535 us
  Pallas kernels  485 us (89%)
  other arithmetic  27.5 us (5%)
  local copies, waits for them, and re-layouts  11.7 us (2%)
  starting transfers between devices  8.52 us (2%)
    pallas_call x1, Pallas kernels, attention_forward(): pl.pallas_call(attention_kernel, out_shape=[jax.ShapeDtypeStruct(shape, d...  195 us
    pallas_call x1, Pallas kernels, backward(): pl.pallas_call(backward_kernel, out_shape=[jax.ShapeDtypeStruct(fs.shape,...  188 us
    pallas_call x1, Pallas kernels, feed_forward(): pl.pallas_call(feed_kernel, out_shape=[jax.ShapeDtypeStruct((part, width)...  102 us
  transfers between devices with their start and end apart: 9, of which 2 were waited for; matrix products, arithmetic and copies ran while one was open for 2% of the time, Pallas kernels for 0%

profile of v6, /device:TPU:0, one launch (start us, length us, event | category | flops | bytes accessed | tf_op | source)
XLA Modules:
  0.0 534.6 jit_solution(4969925384745307188)
XLA Ops:
  1.2 1.1 reduce-window.4
  3.6 0.9 broadcast_in_dim.27.seg_col
  4.5 1.0 copy.39
  5.7 1.0 copy.41
  6.7 0.8 copy.42
  7.5 1.2 copy.37
  9.1 0.9 copy.44
  11.4 1.0 broadcast_multiply_fusion
  12.4 2.0 sine_multiply_fusion
  14.5 1.3 pad_maximum_fusion.3
  16.1 2.0 pad_maximum_fusion.wf
  18.1 1.0 pad_maximum_fusion.1.wa
  19.1 1.0 fusion.9
  20.1 195.3 %shard_map.203 = (bf16[4,4,128,640]{3,2,1,0:T(8,128)(2,1)}, bf16[3,4,4,128,1024]{4,3,2,1,0:T(8,128)(2,1)}, bf16[4,256,2048]{2,1,0:T(8,128)(2,1)}, bf16[1024,256]...) custom-call(bf16[4,128,640]{2,1,0:T(8,128)(2,1)} %pad_maximum_fusion, ...), custom_call_target="tpu_custom_call" | custom-call | tf_op jit(solution)/shard_map/pallas_call | solution.py:621
  215.5 1.4 multiply_reduce_fusion.2
  216.9 0.8 fusion.24
  217.7 101.8 %shard_map.204 = (f32[128,2048]{1,0:T(8,128)}, f32[128,2048]{1,0:T(8,128)}, bf16[3,128,2048]{2,1,0:T(8,128)(2,1)}, bf16[3,2048,1024]{2,1,0:T(8,128)(2,1)}) custom-call(bf16[128,2048]{1,0:T(8,128)(2,1)} %get-tuple-element.34.x, bf16[4,256,2048]{2,1,0:T(8,128)(2,1)} %bitcast.72, bf16[3,2048,1024]{2,1,0:T(8,128)(2,1)} %bitcast.70), custom_call_target="tpu_custom_call" | custom-call | tf_op jit(solution)/shard_map/pallas_call | solution.py:776
  319.5 1.7 multiply_reduce_fusion
  321.4 1.6 multiply_convert_fusion
  322.9 187.8 %shard_map.205 = (bf16[3,128,2048]{2,1,0:T(8,128)(2,1)}, f32[128,2048]{1,0:T(8,128)}, bf16[3,128,2048]{2,1,0:T(8,128)(2,1)}, bf16[3,128,4096]{2,1,0:T(8,128)(2,1...) custom-call(bf16[3,4,4,128,1024]{4,3,2,1,0:T(8,128)(2,1)} %bitcast.69, ...), custom_call_target="tpu_custom_call" | custom-call | tf_op jit(solution)/shard_map/pallas_call | solution.py:1044
  510.7 2.0 convert_reduce_fusion.1
  513.0 1.0 copy-done.11
  516.5 1.5 collective-permute-start.5
  518.0 1.4 collective-permute-start.4
  520.0 2.9 bitcast_convert_fusion
  523.2 2.0 collective-permute-start.8
  525.2 2.5 collective-permute-start.6
  527.8 0.8 convert_element_type.130
  528.7 0.8 convert_element_type.137
  529.6 0.8 copy.50
  531.9 1.1 maximum_bitcast_fusion
  533.0 1.1 maximum_bitcast_fusion.1
  (92 shorter events, 9.5 us)
Async XLA Ops:
  0.6 8.2 %copy-start.17 = (f32[128,1024]{1,0:T(8,128)S(1)}, f32[128,1024]{1,0:T(8,128)}, u32[]{:S(2)}) copy-start(f32[128,1024]{1,0:T(8,128)} %param.19) | copy-start | bytes 1572868
  0.7 9.3 %copy-start.10 = (f32[128,4096]{1,0:T(8,128)S(1)}, f32[128,4096]{1,0:T(8,128)}, u32[]{:S(2)}) copy-start(f32[128,4096]{1,0:T(8,128)} %param.21) | copy-start | bytes 6291460
  8.9 1.2 copy-start.21
  11.4 4.4 copy-start.8
  11.4 4.4 copy-start.9
  16.1 2.0 copy-start.13
  16.1 2.0 copy-start.18
  16.1 3.0 copy-start.2
  16.1 3.0 copy-start.14
  217.7 101.8 %copy-start = (f32[128,2048]{1,0:T(8,128)S(1)}, f32[128,2048]{1,0:T(8,128)}, u32[]{:S(2)}) copy-start(f32[128,2048]{1,0:T(8,128)} %get-tuple-element.33) | copy-start | bytes 3145732
  319.5 1.8 copy-start.6
  319.5 1.8 copy-start.15
  510.7 2.0 copy-start.1
  510.7 2.0 copy-start.12
  512.7 1.4 copy-start.11
  512.9 1.5 copy-start.3
  512.9 1.8 copy-start.4
  513.0 18.9 %collective-permute-start = (bf16[128,2048]{1,0:T(8,128)(2,1)S(1)}, bf16[128,2048]{1,0:T(8,128)(2,1)S(1)}, u32[]{:S(2)}, u32[]{:S(2)}) collective-permute-start(bf16[128,2048]{1,0:T(8,128)(2,1)S(1)} %add_convert_fusion), channel_id=1, source_target_pairs={{0,1},{1,0},{2,3},{3,2},{4,5},{5,4},{6,7},{7,6},{8,9},{9,8},{10,11... | collective-permute-start | bytes 1572872 | tf_op jit(solution)/shard_map/ppermute | solution.py:806
  514.1 1.4 copy-start.5
  515.2 1.2 collective-permute-start.2
  515.5 4.6 copy-start.7
  515.9 17.1 %collective-permute-start.1 = (bf16[128,2048]{1,0:T(8,128)(2,1)S(1)}, bf16[128,2048]{1,0:T(8,128)(2,1)S(1)}, u32[]{:S(2)}, u32[]{:S(2)}) collective-permute-start(bf16[128,2048]{1,0:T(8,128)(2,1)S(1)} %fusion.7), channel_id=1, source_target_pairs={{0,1},{1,0},{2,3},{3,2},{4,5},{5,4},{6,7},{7,6},{8,9},{9,8},{10,11... | collective-permute-start | bytes 1572872 | tf_op jit(solution)/shard_map/ppermute | solution.py:806
  516.5 6.5 %collective-permute-start.5 = (f32[2,2048]{1,0:T(2,128)S(1)}, f32[2,2048]{1,0:T(2,128)S(1)}, u32[]{:S(2)}, u32[]{:S(2)}) collective-permute-start(f32[2,2048]{1,0:T(2,128)S(1)} %fusion.22), channel_id=1, source_target_pairs={{0,6},{2,4},{4,2},{6,0},{1,7},{3,5},{5,3},{7,1},{8,14},{10,12},{12... | collective-permute-start | bytes 49160 | tf_op jit(solution)/shard_map/ppermute | solution.py:806
  518.0 4.9 collective-permute-start.4
  519.5 3.7 collective-permute-start.3
  520.0 7.7 %copy-start.16 = (bf16[4,128,128]{2,1,0:T(8,128)(2,1)S(1)}, bf16[4,128,128]{2,1,0:T(8,128)(2,1)}, u32[]{:S(2)}) copy-start(bf16[4,128,128]{2,1,0:T(8,128)(2,1)} %get-tuple-element.52) | copy-start | bytes 393220
  520.0 7.8 %copy-start.20 = (bf16[128,1024]{1,0:T(8,128)(2,1)S(1)}, bf16[128,1024]{1,0:T(8,128)(2,1)}, u32[]{:S(2)}) copy-start(bf16[128,1024]{1,0:T(8,128)(2,1)} %get-tuple-element.51) | copy-start | bytes 786436
  520.0 8.6 %copy-start.19 = (bf16[128,1024]{1,0:T(8,128)(2,1)S(1)}, bf16[128,1024]{1,0:T(8,128)(2,1)}, u32[]{:S(2)}) copy-start(bf16[128,1024]{1,0:T(8,128)(2,1)} %get-tuple-element.53) | copy-start | bytes 786436
  523.2 8.0 %collective-permute-start.8 = (f32[2,2048]{1,0:T(2,128)S(1)}, f32[2,2048]{1,0:T(2,128)S(1)}, u32[]{:S(2)}, u32[]{:S(2)}) collective-permute-start(f32[2,2048]{1,0:T(2,128)S(1)} %add_add_fusion), channel_id=1, source_target_pairs={{0,24},{8,16},{16,8},{24,0},{1,25},{9,17},{17,9},{25,1},{2,26},{10... | collective-permute-start | bytes 49160 | tf_op jit(solution)/shard_map/ppermute | solution.py:806
  525.2 6.0 %collective-permute-start.7 = (f32[2,2048]{1,0:T(2,128)S(1)}, f32[2,2048]{1,0:T(2,128)S(1)}, u32[]{:S(2)}, u32[]{:S(2)}) collective-permute-start(f32[2,2048]{1,0:T(2,128)S(1)} %add_add_fusion), channel_id=1, source_target_pairs={{0,16},{8,24},{16,0},{24,8},{1,17},{9,25},{17,1},{25,9},{2,18},{10... | collective-permute-start | bytes 49160 | tf_op jit(solution)/shard_map/ppermute | solution.py:806
  525.2 6.0 %collective-permute-start.6 = (f32[2,2048]{1,0:T(2,128)S(1)}, f32[2,2048]{1,0:T(2,128)S(1)}, u32[]{:S(2)}, u32[]{:S(2)}) collective-permute-start(f32[2,2048]{1,0:T(2,128)S(1)} %add_add_fusion), channel_id=1, source_target_pairs={{0,8},{8,0},{16,24},{24,16},{1,9},{9,1},{17,25},{25,17},{2,10},{10... | collective-permute-start | bytes 49160 | tf_op jit(solution)/shard_map/ppermute | solution.py:806

commit v7 on v6

--- a/solution.py
+++ b/solution.py
@@ -411,6 +411,40 @@
         )
         return one, two, direct, passed
 
+    class Chain:
+        def __init__(self, source, block):
+            self.one = net.start(source, block(0, 1), (flip(z, 1), c, t))
+            two, three = net.index(), net.index()
+            self.direct = net.make(three, source, block(0, 3), (3 - z, c, t))
+            self.near = net.make(two, block(1, 1), block(1, 2), (3 - z, c, t))
+            self.over = self.hop(two, block(3, 3), block(3, 2))
+            self.far = self.hop(three, block(2, 2), block(2, 3))
+            pl.when(middle)(self.direct.start)
+
+        def hop(self, receives, source, target):
+            return pltpu.make_async_remote_copy(
+                src_ref=source,
+                dst_ref=target,
+                send_sem=send.at[net.index()],
+                recv_sem=receive.at[receives],
+                device_id=(flip(z, 1), c, t),
+                device_id_type=pl.DeviceIdType.MESH,
+            )
+
+        def pass_near(self):
+            self.one.wait_recv()
+            pl.when(middle)(self.near.start)
+
+        def pass_far(self):
+            self.direct.wait_recv()
+            pl.when(middle)(self.over.start)
+            self.near.wait_recv()
+            pl.when(middle)(self.far.start)
+
+        def end(self):
+            for copy in (self.direct, self.near, self.over, self.far):
+                pl.when(middle)(copy.wait_send)
+
     attn_in = [net.start(wa.at[flip(c, k)], wa_all.at[z, c], (z, flip(c, k), t)) for k in (1, 2, 3)]
     tokens_in = [net.start(xt.at[t], x_all.at[c, t], (z, flip(c, k), t)) for k in (1, 2, 3)]
     parts = {k: (0, 1, 2) if k == 2 else (slice(None),) for k in range(4)}
@@ -441,7 +475,7 @@
         weights.append(spread(piece, lambda k, piece=piece: piece, (passed_piece, passed_piece)))
     for k in (3, 2):
         ff_in[k] = weights_to(k)
-    feed = spread(fgx, lambda k: fg_all.at[k, 0], (fg_all.at[2, 0], fg_all.at[3, 0]))
+    feed = Chain(fgx, lambda _, j: fg_all.at[j, 0])
     swaps = [net.start(fgx, fg_all.at[0, 1], core)]
     token_swaps = []
     for k, copy in zip((1, 2, 3), tokens_in):
@@ -513,6 +547,7 @@
 
     lax.fori_loop(0, 4, project, 0)
     corner(1)
+    feed.pass_near()
 
     def attend(i):
         count = (i + 1) * rows
@@ -565,11 +600,6 @@
         totals[k - 1] = (mine[k] + crossed[k].astype(f32)).astype(bf16)
         outs[k] = net.start(totals.at[k - 1], landed.at[k - 1], (z, flip(c, k), t))
     onward(2)
-    one, two, direct, passed = feed
-    two.wait_recv()
-    pl.when(middle)(passed.start)
-    swaps.append(net.start(fg_all.at[2, 0], fg_all.at[2, 1], core))
-    one.wait_recv()
     swaps.append(net.start(fg_all.at[1, 0], fg_all.at[1, 1], core))
     crosses[0].wait_recv()
     total = mine[0] + crossed[0].astype(f32)
@@ -580,12 +610,14 @@
     hidden_out[...] = hidden
     inverse = lax.rsqrt(jnp.mean(hidden * hidden, axis=-1, keepdims=True) + norm_eps)
     normed_two[...] = (hidden * inverse * gains[1:2, :]).astype(bf16)
-    direct.wait_recv()
-    swaps.append(net.start(fg_all.at[3, 0], fg_all.at[3, 1], core))
+    feed.pass_far()
+    for k in (2, 3):
+        swaps.append(net.start(fg_all.at[k, 0], fg_all.at[k, 1], core))
     corner(2)
     for copy in halves + swaps:
         copy.wait_recv()
-    for _, _, direct, passed in weights + [feed]:
+    feed.end()
+    for _, _, direct, passed in weights:
         pl.when(middle)(direct.wait_send)
         pl.when(middle)(passed.wait_send)
     for copy in net.started:
@@ -814,7 +846,7 @@
     ff, fs, al, wa_in, normed_in, q, kv, logs, attended, cos, sin, seg_col, seg_row,
     feed_in, back_own, back_in, ff_out, query_out, kv_out, output_out,
     terms, corner_x, corner_y, side_x, side_y, at_terms, at_in, at_total, wa, normed, ag, pairs, mixed, acc, dqkv,
-    sums, mine, cross, crossed, totals, send, receive, local,
+    sums, mine, cross, crossed, totals, held_feed, held_terms, send, receive, local,
 ):
     f32, bf16 = jnp.float32, jnp.bfloat16
     z, c, t = (lax.axis_index(a) for a in (FSDP, CONTEXT, TENSOR))
@@ -851,7 +883,57 @@
     corners(3)
     ag_in = [net.start(al, ag.at[c, t], (z, flip(c, k), t)) for k in (3, 1, 2)]
     swaps = [net.start(al, ag.at[c, t], core)]
-    feed = [net.start(fs.at[k - 1], feed_in.at[k - 1], (flip(z, k), c, t)) for k in (3, 2, 1)]
+    middle = (z == 1) | (z == 2)
+    chains = []
+
+    class Sums:
+        def __init__(self, mine, held, landed):
+            self.mine, self.held, self.landed = mine, held, landed
+            neighbour = (flip(z, 1), c, t)
+            self.ends = [net.make(net.index(), mine(k), held(k), neighbour) for k in (3, 2)]
+            for copy in self.ends:
+                pl.when(jnp.logical_not(middle))(copy.start)
+            self.one = net.start(mine(1), landed(0), neighbour)
+            two, spare = net.index(), net.index()
+            self.out = [net.make(two, held(2), landed(1), (3 - z, c, t))]
+            self.out.append(
+                pltpu.make_async_remote_copy(
+                    src_ref=held(3),
+                    dst_ref=landed(1),
+                    send_sem=send.at[spare],
+                    recv_sem=receive.at[two],
+                    device_id=(flip(z, 2), c, t),
+                    device_id_type=pl.DeviceIdType.MESH,
+                )
+            )
+            chains.append(self)
+
+        def add(self, k, own):
+            held, mine = self.held(k), self.mine(own)
+            for i in range(held.shape[0]) if len(held.shape) == 3 else (slice(None),):
+                held[i] = (held[i].astype(f32) + mine[i].astype(f32)).astype(bf16)
+
+        def hand_on(self):
+            @pl.when(middle)
+            def _():
+                for copy in self.ends:
+                    copy.wait_recv()
+                self.add(3, 2)
+                self.out[1].start()
+                self.add(2, 3)
+                self.out[0].start()
+
+        def wait_in(self):
+            self.one.wait_recv()
+            self.out[0].wait_recv()
+
+        def wait_out(self):
+            for copy in self.ends:
+                pl.when(jnp.logical_not(middle))(copy.wait_send)
+            for copy in self.out:
+                pl.when(middle)(copy.wait_send)
+
+    feed = Sums(lambda k: fs.at[k - 1], lambda k: held_feed.at[k - 2], lambda i: feed_in.at[i])
     corners(2)
     ag[c, t] = al[...]
     for j, piece in enumerate(split_pair(kv[...].astype(f32))):
@@ -917,14 +999,14 @@
     lax.fori_loop(0, width // wrows, out_term, 0)
 
     def terms_to(columns):
-        return [
-            net.start(
-                at_terms.at[flip(z, k), :, :, columns], at_in.at[k - 1, :, :, columns], (flip(z, k), c, t)
-            )
-            for k in (3, 2, 1)
-        ]
-
-    attn_in = terms_to(pl.ds(qkv_cols, q_cols))
+        return Sums(
+            lambda k: at_terms.at[flip(z, k), :, :, columns],
+            lambda k: held_terms.at[k - 2, :, :, columns],
+            lambda i: at_in.at[i, :, :, columns],
+        )
+
+    output_sums = terms_to(pl.ds(qkv_cols, q_cols))
+    feed.hand_on()
     sides(2)
     corners(0)
 
@@ -956,6 +1038,7 @@
             dqkv[here, block] = (grad * cos_b + turn_lanes(grad * sin_b, quarter)).astype(bf16)
 
     attend(0)
+    output_sums.hand_on()
     attend(1)
     owners(3)
     sides(1)
@@ -999,14 +1082,15 @@
         return carry
 
     lax.fori_loop(0, width // wrows, qkv_term, 0)
-    attn_in += terms_to(pl.ds(0, qkv_cols))
+    qkv_sums = terms_to(pl.ds(0, qkv_cols))
     owners(1)
     owners(0)
-    for copy in attn_in:
-        copy.wait_recv()
+    qkv_sums.hand_on()
+    output_sums.wait_in()
+    qkv_sums.wait_in()
     for j in range(4):
         total = at_terms[z, j].astype(f32)
-        for i in range(3):
+        for i in range(2):
             total = total + at_in[i, j].astype(f32)
         at_total[j] = total.astype(bf16)
     here = pl.ds(pl.multiple_of(c * q_cols, q_cols), q_cols)
@@ -1021,7 +1105,10 @@
         attn_out += [net.start(at_total.at[flip(c, k), :, columns], target, (z, flip(c, k), t)) for k in (1, 2, 3)]
         keep_own.append(pltpu.make_async_copy(at_total.at[c, :, columns], target, local.at[7 + i]))
         keep_own[-1].start()
-    for copy in feed + attn_out + [outs[k] for k in (1, 2, 3)] + [third[k] for k in (1, 2, 3)]:
+    feed.wait_in()
+    for chain in chains:
+        chain.wait_out()
+    for copy in attn_out + [outs[k] for k in (1, 2, 3)] + [third[k] for k in (1, 2, 3)]:
         copy.wait_recv()
     for copy in net.started:
         copy.wait_send()
@@ -1044,7 +1131,7 @@
     return pl.pallas_call(
         backward_kernel,
         out_shape=[
-            jax.ShapeDtypeStruct(fs.shape, bf16),
+            jax.ShapeDtypeStruct((2,) + al.shape, bf16),
             jax.ShapeDtypeStruct(al.shape, f32),
             jax.ShapeDtypeStruct(fs.shape, bf16),
             jax.ShapeDtypeStruct((3, wrows, 4 * hidden), bf16),
@@ -1061,7 +1148,7 @@
             pltpu.VMEM((4, 3, wrows, hidden), bf16),
             pltpu.VMEM((4, 3, wrows, hidden), bf16),
             pltpu.VMEM((4, 4, wrows, attn_cols), bf16),
-            pltpu.VMEM((3, 4, wrows, attn_cols), bf16),
+            pltpu.VMEM((2, 4, wrows, attn_cols), bf16),
             pltpu.VMEM((4, wrows, attn_cols), bf16),
             pltpu.VMEM(wa.shape, bf16),
             pltpu.VMEM((blocks, rows, width), bf16),
@@ -1075,6 +1162,8 @@
             pltpu.VMEM((4, part, width), bf16),
             pltpu.VMEM((4, part, width), bf16),
             pltpu.VMEM((3, part, width), bf16),
+            pltpu.VMEM((2, part, width), bf16),
+            pltpu.VMEM((2, 4, wrows, attn_cols), bf16),
             pltpu.SemaphoreType.DMA((copies,)),
             pltpu.SemaphoreType.DMA((copies,)),
             pltpu.SemaphoreType.DMA((10,)),

time: 544 us -> 524 us (0.963)
  Pallas kernels: 485 us -> 464 us
    pallas_call x1, Pallas kernels: 188 us -> 173 us  [backward(): pl.pallas_call(backward_kernel, out_shape=[jax.ShapeDtypeStruct((2,) + al...]
    pallas_call x1, Pallas kernels: 102 us -> 93.9 us  [feed_forward(): pl.pallas_call(feed_kernel, out_shape=[jax.ShapeDtypeStruct((part, width)...]
  transfers between devices with their start and end apart: 9 -> 9, of which waited for: 2 -> 3; matrix products, arithmetic and copies ran while one was open for 2% -> 2% of each run, Pallas kernels for 0% -> 0%
where the time goes in v7:
time: 524 us; the launch traced here: 515 us
  Pallas kernels  464 us (89%)
  other arithmetic  27.2 us (5%)
  local copies, waits for them, and re-layouts  11.7 us (2%)
  starting transfers between devices  9.65 us (2%)
    pallas_call x1, Pallas kernels, attention_forward(): pl.pallas_call(attention_kernel, out_shape=[jax.ShapeDtypeStruct(shape, d...  197 us
    pallas_call x1, Pallas kernels, backward(): pl.pallas_call(backward_kernel, out_shape=[jax.ShapeDtypeStruct((2,) + al...  173 us
    pallas_call x1, Pallas kernels, feed_forward(): pl.pallas_call(feed_kernel, out_shape=[jax.ShapeDtypeStruct((part, width)...  93.9 us
  transfers between devices with their start and end apart: 9, of which 3 were waited for; matrix products, arithmetic and copies ran while one was open for 2% of the time, Pallas kernels for 0%

profile of v7, /device:TPU:0, one launch (start us, length us, event | category | flops | bytes accessed | tf_op | source)
XLA Modules:
  0.0 514.9 jit_solution(14896862494826547576)
XLA Ops:
  1.2 1.1 reduce-window.4
  3.6 0.9 broadcast_in_dim.27.seg_col
  4.5 1.0 copy.39
  5.7 1.0 copy.41
  6.7 0.8 copy.42
  7.5 1.2 copy.37
  9.1 0.9 copy.44
  11.4 1.0 broadcast_multiply_fusion
  12.4 2.0 sine_multiply_fusion
  14.5 1.3 pad_maximum_fusion.3
  16.1 2.0 pad_maximum_fusion.wf
  18.1 1.0 pad_maximum_fusion.1.wa
  19.1 1.0 fusion.9
  20.1 196.6 %shard_map.203 = (bf16[4,4,128,640]{3,2,1,0:T(8,128)(2,1)}, bf16[3,4,4,128,1024]{4,3,2,1,0:T(8,128)(2,1)}, bf16[4,256,2048]{2,1,0:T(8,128)(2,1)}, bf16[1024,256]...) custom-call(bf16[4,128,640]{2,1,0:T(8,128)(2,1)} %pad_maximum_fusion, ...), custom_call_target="tpu_custom_call" | custom-call | tf_op jit(solution)/shard_map/pallas_call | solution.py:653
  216.8 1.4 multiply_reduce_fusion.2
  218.2 0.8 fusion.24
  219.0 93.9 %shard_map.204 = (f32[128,2048]{1,0:T(8,128)}, f32[128,2048]{1,0:T(8,128)}, bf16[3,128,2048]{2,1,0:T(8,128)(2,1)}, bf16[3,2048,1024]{2,1,0:T(8,128)(2,1)}) custom-call(bf16[128,2048]{1,0:T(8,128)(2,1)} %get-tuple-element.34.x, bf16[4,256,2048]{2,1,0:T(8,128)(2,1)} %bitcast.72, bf16[3,2048,1024]{2,1,0:T(8,128)(2,1)} %bitcast.70), custom_call_target="tpu_custom_call" | custom-call | tf_op jit(solution)/shard_map/pallas_call | solution.py:808
  312.9 1.7 multiply_reduce_fusion
  314.7 1.6 multiply_convert_fusion
  316.3 173.1 %shard_map.205 = (bf16[2,128,2048]{2,1,0:T(8,128)(2,1)}, f32[128,2048]{1,0:T(8,128)}, bf16[3,128,2048]{2,1,0:T(8,128)(2,1)}, bf16[3,128,4096]{2,1,0:T(8,128)(2,1...) custom-call(bf16[3,4,4,128,1024]{4,3,2,1,0:T(8,128)(2,1)} %bitcast.69, ...), custom_call_target="tpu_custom_call" | custom-call | tf_op jit(solution)/shard_map/pallas_call | solution.py:1131
  489.4 1.7 convert_reduce_fusion.1
  491.6 1.0 copy-done.11
  494.9 1.6 collective-permute-start.5
  496.6 2.4 collective-permute-start.4
  499.0 2.9 bitcast_convert_fusion
  501.9 0.8 collective-permute-done.3
  502.8 2.4 collective-permute-start.8
  505.1 2.7 collective-permute-start.7
  508.0 0.8 convert_element_type.130
  508.8 0.8 convert_element_type.137
  512.2 1.1 maximum_bitcast_fusion
  513.4 1.1 maximum_bitcast_fusion.1
  (92 shorter events, 9.7 us)
Async XLA Ops:
  0.6 8.2 %copy-start.17 = (f32[128,1024]{1,0:T(8,128)S(1)}, f32[128,1024]{1,0:T(8,128)}, u32[]{:S(2)}) copy-start(f32[128,1024]{1,0:T(8,128)} %param.19) | copy-start | bytes 1572868
  0.7 9.3 %copy-start.10 = (f32[128,4096]{1,0:T(8,128)S(1)}, f32[128,4096]{1,0:T(8,128)}, u32[]{:S(2)}) copy-start(f32[128,4096]{1,0:T(8,128)} %param.21) | copy-start | bytes 6291460
  8.9 1.2 copy-start.21
  11.4 4.4 copy-start.8
  11.4 4.4 copy-start.9
  16.1 2.0 copy-start.13
  16.1 2.0 copy-start.18
  16.1 3.0 copy-start.2
  16.1 3.0 copy-start.14
  219.0 93.9 %copy-start = (f32[128,2048]{1,0:T(8,128)S(1)}, f32[128,2048]{1,0:T(8,128)}, u32[]{:S(2)}) copy-start(f32[128,2048]{1,0:T(8,128)} %get-tuple-element.33) | copy-start | bytes 3145732
  312.9 1.8 copy-start.6
  312.9 1.8 copy-start.15
  489.4 1.7 copy-start.1
  489.4 1.8 copy-start.12
  491.1 1.4 copy-start.11
  491.5 1.4 copy-start.3
  491.5 1.7 copy-start.4
  491.5 20.6 %collective-permute-start = (bf16[128,2048]{1,0:T(8,128)(2,1)S(1)}, bf16[128,2048]{1,0:T(8,128)(2,1)S(1)}, u32[]{:S(2)}, u32[]{:S(2)}) collective-permute-start(bf16[128,2048]{1,0:T(8,128)(2,1)S(1)} %add_convert_fusion), channel_id=1, source_target_pairs={{0,1},{1,0},{2,3},{3,2},{4,5},{5,4},{6,7},{7,6},{8,9},{9,8},{10,11... | collective-permute-start | bytes 1572872 | tf_op jit(solution)/shard_map/ppermute | solution.py:838
  492.6 1.4 copy-start.5
  493.7 1.2 collective-permute-start.2
  494.0 5.0 copy-start.7
  494.4 18.9 %collective-permute-start.1 = (bf16[128,2048]{1,0:T(8,128)(2,1)S(1)}, bf16[128,2048]{1,0:T(8,128)(2,1)S(1)}, u32[]{:S(2)}, u32[]{:S(2)}) collective-permute-start(bf16[128,2048]{1,0:T(8,128)(2,1)S(1)} %fusion.7), channel_id=1, source_target_pairs={{0,1},{1,0},{2,3},{3,2},{4,5},{5,4},{6,7},{7,6},{8,9},{9,8},{10,11... | collective-permute-start | bytes 1572872 | tf_op jit(solution)/shard_map/ppermute | solution.py:838
  494.9 7.0 %collective-permute-start.5 = (f32[2,2048]{1,0:T(2,128)S(1)}, f32[2,2048]{1,0:T(2,128)S(1)}, u32[]{:S(2)}, u32[]{:S(2)}) collective-permute-start(f32[2,2048]{1,0:T(2,128)S(1)} %fusion.22), channel_id=1, source_target_pairs={{0,6},{2,4},{4,2},{6,0},{1,7},{3,5},{5,3},{7,1},{8,14},{10,12},{12... | collective-permute-start | bytes 49160 | tf_op jit(solution)/shard_map/ppermute | solution.py:838
  496.6 5.4 %collective-permute-start.4 = (f32[2,2048]{1,0:T(2,128)S(1)}, f32[2,2048]{1,0:T(2,128)S(1)}, u32[]{:S(2)}, u32[]{:S(2)}) collective-permute-start(f32[2,2048]{1,0:T(2,128)S(1)} %fusion.22), channel_id=1, source_target_pairs={{0,4},{2,6},{4,0},{6,2},{1,5},{3,7},{5,1},{7,3},{8,12},{10,14},{12... | collective-permute-start | bytes 49160 | tf_op jit(solution)/shard_map/ppermute | solution.py:838
  499.0 3.7 collective-permute-start.3
  499.0 8.9 %copy-start.16 = (bf16[4,128,128]{2,1,0:T(8,128)(2,1)S(1)}, bf16[4,128,128]{2,1,0:T(8,128)(2,1)}, u32[]{:S(2)}) copy-start(bf16[4,128,128]{2,1,0:T(8,128)(2,1)} %get-tuple-element.52) | copy-start | bytes 393220
  499.0 9.0 %copy-start.20 = (bf16[128,1024]{1,0:T(8,128)(2,1)S(1)}, bf16[128,1024]{1,0:T(8,128)(2,1)}, u32[]{:S(2)}) copy-start(bf16[128,1024]{1,0:T(8,128)(2,1)} %get-tuple-element.51) | copy-start | bytes 786436
  499.0 9.9 %copy-start.19 = (bf16[128,1024]{1,0:T(8,128)(2,1)S(1)}, bf16[128,1024]{1,0:T(8,128)(2,1)}, u32[]{:S(2)}) copy-start(bf16[128,1024]{1,0:T(8,128)(2,1)} %get-tuple-element.53) | copy-start | bytes 786436
  502.8 8.7 %collective-permute-start.8 = (f32[2,2048]{1,0:T(2,128)S(1)}, f32[2,2048]{1,0:T(2,128)S(1)}, u32[]{:S(2)}, u32[]{:S(2)}) collective-permute-start(f32[2,2048]{1,0:T(2,128)S(1)} %add_add_fusion), channel_id=1, source_target_pairs={{0,24},{8,16},{16,8},{24,0},{1,25},{9,17},{17,9},{25,1},{2,26},{10... | collective-permute-start | bytes 49160 | tf_op jit(solution)/shard_map/ppermute | solution.py:838
  505.1 6.3 %collective-permute-start.7 = (f32[2,2048]{1,0:T(2,128)S(1)}, f32[2,2048]{1,0:T(2,128)S(1)}, u32[]{:S(2)}, u32[]{:S(2)}) collective-permute-start(f32[2,2048]{1,0:T(2,128)S(1)} %add_add_fusion), channel_id=1, source_target_pairs={{0,16},{8,24},{16,0},{24,8},{1,17},{9,25},{17,1},{25,9},{2,18},{10... | collective-permute-start | bytes 49160 | tf_op jit(solution)/shard_map/ppermute | solution.py:838
  507.9 3.7 collective-permute-start.6

commit v8 on v7

--- a/solution.py
+++ b/solution.py
@@ -557,19 +557,22 @@
             >= lax.broadcasted_iota(jnp.int32, (rows, count), 1)
         )
         lane = lax.broadcasted_iota(jnp.int32, (rows, 128), 1)
-        log_sums = jnp.zeros((rows, 128), f32)
-        for p in range(q_cols // 128):
+
+        def pair(p, log_sums):
+            block = pl.ds(pl.multiple_of(p * 128, 128), 128)
             out = jnp.zeros((rows, 128), f32)
             for e in range(2):
-                scores = dot_tile(q[here, p * 128 : (p + 1) * 128], pairs[e, :count, :], 1, 1)
+                scores = dot_tile(q[here, block], pairs[e, :count, :], 1, 1)
                 scores = jnp.where(keep, scores * attention_mult, -1e30)
                 highest = jnp.max(scores, axis=-1, keepdims=True)
                 weight = jnp.exp(scores - highest)
                 total = jnp.sum(weight, axis=-1, keepdims=True)
                 out = out + dot_tile((weight / total).astype(bf16), pairs[2 + e, :count, :], 1, 0)
                 log_sums = jnp.where(lane == 2 * p + e, highest + jnp.log(total), log_sums)
-            attended[here, p * 128 : (p + 1) * 128] = out.astype(bf16)
-        logs[here, :] = log_sums
+            attended[here, block] = out.astype(bf16)
+            return log_sums
+
+        logs[here, :] = lax.fori_loop(0, q_cols // 128, pair, jnp.zeros((rows, 128), f32))
 
     attend(0)
     attend(1)
@@ -1021,8 +1024,9 @@
         lane = lax.broadcasted_iota(jnp.int32, (rows, 128), 1)
         cos_b, sin_b = cos[here, :], sin[here, :]
         quarter = low_lanes(cos_b.shape, HEAD // 2)
-        for p in range(q_cols // 128):
-            block = slice(p * 128, (p + 1) * 128)
+
+        def pair(p, carry):
+            block = pl.ds(pl.multiple_of(p * 128, 128), 128)
             grad = jnp.zeros((rows, 128), f32)
             for e in range(2):
                 scores = dot_tile(q[here, block], pairs[e, :count, :], 1, 1)
@@ -1036,6 +1040,9 @@
                 acc[e, :count, :] += dot_tile(score_grad, q[here, block], 0, 0)
                 acc[2 + e, :count, :] += dot_tile(prob.astype(bf16), mixed[here, block], 0, 0)
             dqkv[here, block] = (grad * cos_b + turn_lanes(grad * sin_b, quarter)).astype(bf16)
+            return carry
+
+        lax.fori_loop(0, q_cols // 128, pair, 0)
 
     attend(0)
     output_sums.hand_on()

time: 524 us -> 515 us (0.983); the launches traced: 515 us -> 514 us
  no operation moved by 1% of the time
where the time goes in v8:
time: 515 us; the launch traced here: 514 us
  Pallas kernels  464 us (90%)
  other arithmetic  27.2 us (5%)
  local copies, waits for them, and re-layouts  11.7 us (2%)
  starting transfers between devices  9.67 us (2%)
    pallas_call x1, Pallas kernels, attention_forward(): pl.pallas_call(attention_kernel, out_shape=[jax.ShapeDtypeStruct(shape, d...  197 us
    pallas_call x1, Pallas kernels, backward(): pl.pallas_call(backward_kernel, out_shape=[jax.ShapeDtypeStruct((2,) + al...  173 us
    pallas_call x1, Pallas kernels, feed_forward(): pl.pallas_call(feed_kernel, out_shape=[jax.ShapeDtypeStruct((part, width)...  93.9 us
  transfers between devices with their start and end apart: 9, of which 3 were waited for; matrix products, arithmetic and copies ran while one was open for 2% of the time, Pallas kernels for 0%

profile of v8, /device:TPU:0, one launch (start us, length us, event | category | flops | bytes accessed | tf_op | source)
XLA Modules:
  0.0 514.4 jit_solution(7841190761605912694)
XLA Ops:
  1.2 1.1 reduce-window.4
  3.6 0.9 broadcast_in_dim.27.seg_col
  4.5 1.0 copy.39
  5.7 1.0 copy.41
  6.7 0.8 copy.42
  7.5 1.2 copy.37
  9.1 0.9 copy.44
  11.4 1.0 broadcast_multiply_fusion
  12.4 2.0 sine_multiply_fusion
  14.5 1.3 pad_maximum_fusion.3
  16.1 2.0 pad_maximum_fusion.wf
  18.1 1.0 pad_maximum_fusion.1.wa
  19.1 1.0 fusion.9
  20.1 196.6 %shard_map.203 = (bf16[4,4,128,640]{3,2,1,0:T(8,128)(2,1)}, bf16[3,4,4,128,1024]{4,3,2,1,0:T(8,128)(2,1)}, bf16[4,256,2048]{2,1,0:T(8,128)(2,1)}, bf16[1024,256]...) custom-call(bf16[4,128,640]{2,1,0:T(8,128)(2,1)} %pad_maximum_fusion, ...), custom_call_target="tpu_custom_call" | custom-call | tf_op jit(solution)/shard_map/pallas_call | solution.py:656
  216.8 1.4 multiply_reduce_fusion.2
  218.2 0.8 fusion.24
  219.0 93.9 %shard_map.204 = (f32[128,2048]{1,0:T(8,128)}, f32[128,2048]{1,0:T(8,128)}, bf16[3,128,2048]{2,1,0:T(8,128)(2,1)}, bf16[3,2048,1024]{2,1,0:T(8,128)(2,1)}) custom-call(bf16[128,2048]{1,0:T(8,128)(2,1)} %get-tuple-element.34.x, bf16[4,256,2048]{2,1,0:T(8,128)(2,1)} %bitcast.72, bf16[3,2048,1024]{2,1,0:T(8,128)(2,1)} %bitcast.70), custom_call_target="tpu_custom_call" | custom-call | tf_op jit(solution)/shard_map/pallas_call | solution.py:811
  312.9 1.7 multiply_reduce_fusion
  314.8 1.6 multiply_convert_fusion
  316.3 173.1 %shard_map.205 = (bf16[2,128,2048]{2,1,0:T(8,128)(2,1)}, f32[128,2048]{1,0:T(8,128)}, bf16[3,128,2048]{2,1,0:T(8,128)(2,1)}, bf16[3,128,4096]{2,1,0:T(8,128)(2,1...) custom-call(bf16[3,4,4,128,1024]{4,3,2,1,0:T(8,128)(2,1)} %bitcast.69, ...), custom_call_target="tpu_custom_call" | custom-call | tf_op jit(solution)/shard_map/pallas_call | solution.py:1138
  489.4 1.7 convert_reduce_fusion.1
  491.6 1.0 copy-done.11
  494.9 1.6 collective-permute-start.5
  496.5 2.4 collective-permute-start.4
  499.0 2.9 bitcast_convert_fusion
  501.9 0.8 collective-permute-done.3
  502.7 2.4 collective-permute-start.8
  505.1 2.7 collective-permute-start.7
  508.0 0.8 convert_element_type.130
  508.8 0.8 convert_element_type.137
  512.2 1.1 maximum_bitcast_fusion
  513.4 1.1 maximum_bitcast_fusion.1
  (92 shorter events, 9.7 us)
Async XLA Ops:
  0.6 8.2 %copy-start.17 = (f32[128,1024]{1,0:T(8,128)S(1)}, f32[128,1024]{1,0:T(8,128)}, u32[]{:S(2)}) copy-start(f32[128,1024]{1,0:T(8,128)} %param.19) | copy-start | bytes 1572868
  0.7 9.3 %copy-start.10 = (f32[128,4096]{1,0:T(8,128)S(1)}, f32[128,4096]{1,0:T(8,128)}, u32[]{:S(2)}) copy-start(f32[128,4096]{1,0:T(8,128)} %param.21) | copy-start | bytes 6291460
  8.9 1.2 copy-start.21
  11.4 4.4 copy-start.8
  11.4 4.4 copy-start.9
  16.1 2.0 copy-start.13
  16.1 2.0 copy-start.18
  16.1 3.0 copy-start.2
  16.1 3.0 copy-start.14
  219.0 93.9 %copy-start = (f32[128,2048]{1,0:T(8,128)S(1)}, f32[128,2048]{1,0:T(8,128)}, u32[]{:S(2)}) copy-start(f32[128,2048]{1,0:T(8,128)} %get-tuple-element.33) | copy-start | bytes 3145732
  312.9 1.8 copy-start.6
  312.9 1.8 copy-start.15
  489.4 1.7 copy-start.1
  489.4 1.8 copy-start.12
  491.1 1.4 copy-start.11
  491.5 1.4 copy-start.3
  491.5 1.7 copy-start.4
  491.5 20.6 %collective-permute-start = (bf16[128,2048]{1,0:T(8,128)(2,1)S(1)}, bf16[128,2048]{1,0:T(8,128)(2,1)S(1)}, u32[]{:S(2)}, u32[]{:S(2)}) collective-permute-start(bf16[128,2048]{1,0:T(8,128)(2,1)S(1)} %add_convert_fusion), channel_id=1, source_target_pairs={{0,1},{1,0},{2,3},{3,2},{4,5},{5,4},{6,7},{7,6},{8,9},{9,8},{10,11... | collective-permute-start | bytes 1572872 | tf_op jit(solution)/shard_map/ppermute | solution.py:841
  492.5 1.4 copy-start.5
  493.6 1.2 collective-permute-start.2
  493.9 5.0 copy-start.7
  494.3 18.9 %collective-permute-start.1 = (bf16[128,2048]{1,0:T(8,128)(2,1)S(1)}, bf16[128,2048]{1,0:T(8,128)(2,1)S(1)}, u32[]{:S(2)}, u32[]{:S(2)}) collective-permute-start(bf16[128,2048]{1,0:T(8,128)(2,1)S(1)} %fusion.7), channel_id=1, source_target_pairs={{0,1},{1,0},{2,3},{3,2},{4,5},{5,4},{6,7},{7,6},{8,9},{9,8},{10,11... | collective-permute-start | bytes 1572872 | tf_op jit(solution)/shard_map/ppermute | solution.py:841
  494.9 7.0 %collective-permute-start.5 = (f32[2,2048]{1,0:T(2,128)S(1)}, f32[2,2048]{1,0:T(2,128)S(1)}, u32[]{:S(2)}, u32[]{:S(2)}) collective-permute-start(f32[2,2048]{1,0:T(2,128)S(1)} %fusion.22), channel_id=1, source_target_pairs={{0,6},{2,4},{4,2},{6,0},{1,7},{3,5},{5,3},{7,1},{8,14},{10,12},{12... | collective-permute-start | bytes 49160 | tf_op jit(solution)/shard_map/ppermute | solution.py:841
  496.5 5.4 %collective-permute-start.4 = (f32[2,2048]{1,0:T(2,128)S(1)}, f32[2,2048]{1,0:T(2,128)S(1)}, u32[]{:S(2)}, u32[]{:S(2)}) collective-permute-start(f32[2,2048]{1,0:T(2,128)S(1)} %fusion.22), channel_id=1, source_target_pairs={{0,4},{2,6},{4,0},{6,2},{1,5},{3,7},{5,1},{7,3},{8,12},{10,14},{12... | collective-permute-start | bytes 49160 | tf_op jit(solution)/shard_map/ppermute | solution.py:841
  498.9 3.7 collective-permute-start.3
  499.0 8.9 %copy-start.16 = (bf16[4,128,128]{2,1,0:T(8,128)(2,1)S(1)}, bf16[4,128,128]{2,1,0:T(8,128)(2,1)}, u32[]{:S(2)}) copy-start(bf16[4,128,128]{2,1,0:T(8,128)(2,1)} %get-tuple-element.52) | copy-start | bytes 393220
  499.0 9.0 %copy-start.20 = (bf16[128,1024]{1,0:T(8,128)(2,1)S(1)}, bf16[128,1024]{1,0:T(8,128)(2,1)}, u32[]{:S(2)}) copy-start(bf16[128,1024]{1,0:T(8,128)(2,1)} %get-tuple-element.51) | copy-start | bytes 786436
  499.0 9.9 %copy-start.19 = (bf16[128,1024]{1,0:T(8,128)(2,1)S(1)}, bf16[128,1024]{1,0:T(8,128)(2,1)}, u32[]{:S(2)}) copy-start(bf16[128,1024]{1,0:T(8,128)(2,1)} %get-tuple-element.53) | copy-start | bytes 786436
  502.7 8.7 %collective-permute-start.8 = (f32[2,2048]{1,0:T(2,128)S(1)}, f32[2,2048]{1,0:T(2,128)S(1)}, u32[]{:S(2)}, u32[]{:S(2)}) collective-permute-start(f32[2,2048]{1,0:T(2,128)S(1)} %add_add_fusion), channel_id=1, source_target_pairs={{0,24},{8,16},{16,8},{24,0},{1,25},{9,17},{17,9},{25,1},{2,26},{10... | collective-permute-start | bytes 49160 | tf_op jit(solution)/shard_map/ppermute | solution.py:841
  505.1 6.3 %collective-permute-start.7 = (f32[2,2048]{1,0:T(2,128)S(1)}, f32[2,2048]{1,0:T(2,128)S(1)}, u32[]{:S(2)}, u32[]{:S(2)}) collective-permute-start(f32[2,2048]{1,0:T(2,128)S(1)} %add_add_fusion), channel_id=1, source_target_pairs={{0,16},{8,24},{16,0},{24,8},{1,17},{9,25},{17,1},{25,9},{2,18},{10... | collective-permute-start | bytes 49160 | tf_op jit(solution)/shard_map/ppermute | solution.py:841
  507.9 3.7 collective-permute-start.6

commit v9 on v8

--- a/solution.py
+++ b/solution.py
@@ -1049,8 +1049,8 @@
     attend(1)
     owners(3)
     sides(1)
+    sides(0)
     attend(2)
-    sides(0)
     owners(2)
     filled = blocks * rows
     low = low_lanes((filled, 128), HEAD)
@@ -1060,6 +1060,15 @@
     key_grad = key_grad * cos[0:filled, :] + turned
     dqkv[0:filled, q_cols:] = jnp.where(low, key_grad, value_grad).astype(bf16)
 
+    def qkv_term(m, carry):
+        here = pl.ds(pl.multiple_of(m * wrows, wrows), wrows)
+        left = normed[:, :, here].reshape(filled, wrows)
+        value = dot_tile(left, dqkv[0:filled, :], 0, 0)
+        at_terms[lax.div(m, 4), lax.rem(m, 4), :, :qkv_cols] = value.astype(bf16)
+        return carry
+
+    lax.fori_loop(0, width // wrows, qkv_term, 0)
+    qkv_sums = terms_to(pl.ds(0, qkv_cols))
     crosses, outs = {}, {}
     for k in (3, 1, 2, 0):
         mine_rows = pl.ds(pl.multiple_of(flip(c, k) * rows, rows), rows)
@@ -1081,15 +1090,6 @@
     crosses[0].wait_recv()
     back_own[...] = mine[0] + crossed[0].astype(f32)
 
-    def qkv_term(m, carry):
-        here = pl.ds(pl.multiple_of(m * wrows, wrows), wrows)
-        left = normed[:, :, here].reshape(filled, wrows)
-        value = dot_tile(left, dqkv[0:filled, :], 0, 0)
-        at_terms[lax.div(m, 4), lax.rem(m, 4), :, :qkv_cols] = value.astype(bf16)
-        return carry
-
-    lax.fori_loop(0, width // wrows, qkv_term, 0)
-    qkv_sums = terms_to(pl.ds(0, qkv_cols))
     owners(1)
     owners(0)
     qkv_sums.hand_on()

time: 515 us -> 515 us (level)
  no operation moved by 1% of the time
where the time goes in v9:
time: 515 us; the launch traced here: 514 us
  Pallas kernels  459 us (89%)
  other arithmetic  27.2 us (5%)
  starting transfers between devices  14.5 us (3%)
  local copies, waits for them, and re-layouts  11.5 us (2%)
    pallas_call x1, Pallas kernels, attention_forward(): pl.pallas_call(attention_kernel, out_shape=[jax.ShapeDtypeStruct(shape, d...  197 us
    pallas_call x1, Pallas kernels, backward(): pl.pallas_call(backward_kernel, out_shape=[jax.ShapeDtypeStruct((2,) + al...  168 us
    pallas_call x1, Pallas kernels, feed_forward(): pl.pallas_call(feed_kernel, out_shape=[jax.ShapeDtypeStruct((part, width)...  93.9 us
    ppermute x9, starting transfers between devices, swap(): lax.ppermute(x, axis, [(i, i ^ k) for i in range(lax.axis_size(axis))])  14.5 us
  transfers between devices with their start and end apart: 9, of which 3 were waited for; matrix products, arithmetic and copies ran while one was open for 2% of the time, Pallas kernels for 0%

profile of v9, /device:TPU:0, one launch (start us, length us, event | category | flops | bytes accessed | tf_op | source)
XLA Modules:
  0.0 514.4 jit_solution(5814791271255468724)
XLA Ops:
  1.2 1.1 reduce-window.4
  3.6 0.9 broadcast_in_dim.27.seg_col
  4.5 1.0 copy.39
  5.7 1.0 copy.41
  6.7 0.8 copy.42
  7.5 1.2 copy.37
  9.1 0.9 copy.44
  11.4 1.0 broadcast_multiply_fusion
  12.4 2.0 sine_multiply_fusion
  14.5 1.3 pad_maximum_fusion.3
  16.1 2.0 pad_maximum_fusion.wf
  18.1 1.0 pad_maximum_fusion.1.wa
  19.1 1.0 fusion.9
  20.1 196.6 %shard_map.203 = (bf16[4,4,128,640]{3,2,1,0:T(8,128)(2,1)}, bf16[3,4,4,128,1024]{4,3,2,1,0:T(8,128)(2,1)}, bf16[4,256,2048]{2,1,0:T(8,128)(2,1)}, bf16[1024,256]...) custom-call(bf16[4,128,640]{2,1,0:T(8,128)(2,1)} %pad_maximum_fusion, ...), custom_call_target="tpu_custom_call" | custom-call | tf_op jit(solution)/shard_map/pallas_call | solution.py:656
  216.8 1.4 multiply_reduce_fusion.2
  218.2 0.8 fusion.24
  219.0 93.9 %shard_map.204 = (f32[128,2048]{1,0:T(8,128)}, f32[128,2048]{1,0:T(8,128)}, bf16[3,128,2048]{2,1,0:T(8,128)(2,1)}, bf16[3,2048,1024]{2,1,0:T(8,128)(2,1)}) custom-call(bf16[128,2048]{1,0:T(8,128)(2,1)} %get-tuple-element.34.x, bf16[4,256,2048]{2,1,0:T(8,128)(2,1)} %bitcast.72, bf16[3,2048,1024]{2,1,0:T(8,128)(2,1)} %bitcast.70), custom_call_target="tpu_custom_call" | custom-call | tf_op jit(solution)/shard_map/pallas_call | solution.py:811
  312.9 1.7 multiply_reduce_fusion
  314.8 1.6 multiply_convert_fusion
  316.3 168.5 %shard_map.205 = (bf16[2,128,2048]{2,1,0:T(8,128)(2,1)}, f32[128,2048]{1,0:T(8,128)}, bf16[3,128,2048]{2,1,0:T(8,128)(2,1)}, bf16[3,128,4096]{2,1,0:T(8,128)(2,1...) custom-call(bf16[3,4,4,128,1024]{4,3,2,1,0:T(8,128)(2,1)} %bitcast.69, ...), custom_call_target="tpu_custom_call" | custom-call | tf_op jit(solution)/shard_map/pallas_call | solution.py:1138
  484.8 1.7 convert_reduce_fusion.1
  487.1 0.9 copy-done.11
  490.3 1.6 collective-permute-start.5
  492.0 2.4 collective-permute-start.4
  494.4 2.9 bitcast_convert_fusion
  497.3 0.8 collective-permute-done.3
  498.1 2.4 collective-permute-start.8
  500.5 7.3 %collective-permute-start.7 = (f32[2,2048]{1,0:T(2,128)S(1)}, f32[2,2048]{1,0:T(2,128)S(1)}, u32[]{:S(2)}, u32[]{:S(2)}) collective-permute-start(f32[2,2048]{1,0:T(2,128)S(1)} %add_add_fusion), channel_id=1, source_target_pairs={{0,16},{8,24},{16,0},{24,8},{1,17},{9,25},{17,1},{25,9},{2,18},{10... | collective-permute-start | bytes 49160 | tf_op jit(solution)/shard_map/ppermute | solution.py:841
  508.0 0.8 convert_element_type.130
  508.8 0.8 convert_element_type.137
  512.2 1.1 maximum_bitcast_fusion
  513.4 1.1 maximum_bitcast_fusion.1
  (92 shorter events, 9.9 us)
Async XLA Ops:
  0.6 8.2 %copy-start.17 = (f32[128,1024]{1,0:T(8,128)S(1)}, f32[128,1024]{1,0:T(8,128)}, u32[]{:S(2)}) copy-start(f32[128,1024]{1,0:T(8,128)} %param.19) | copy-start | bytes 1572868
  0.7 9.3 %copy-start.10 = (f32[128,4096]{1,0:T(8,128)S(1)}, f32[128,4096]{1,0:T(8,128)}, u32[]{:S(2)}) copy-start(f32[128,4096]{1,0:T(8,128)} %param.21) | copy-start | bytes 6291460
  8.9 1.2 copy-start.21
  11.4 4.4 copy-start.8
  11.4 4.4 copy-start.9
  16.1 2.0 copy-start.13
  16.1 2.0 copy-start.18
  16.1 3.0 copy-start.2
  16.1 3.0 copy-start.14
  219.0 93.9 %copy-start = (f32[128,2048]{1,0:T(8,128)S(1)}, f32[128,2048]{1,0:T(8,128)}, u32[]{:S(2)}) copy-start(f32[128,2048]{1,0:T(8,128)} %get-tuple-element.33) | copy-start | bytes 3145732
  312.9 1.8 copy-start.6
  312.9 1.8 copy-start.15
  484.8 1.7 copy-start.1
  484.8 1.8 copy-start.12
  486.5 1.4 copy-start.11
  486.9 1.4 copy-start.3
  486.9 1.7 copy-start.4
  486.9 25.2 %collective-permute-start = (bf16[128,2048]{1,0:T(8,128)(2,1)S(1)}, bf16[128,2048]{1,0:T(8,128)(2,1)S(1)}, u32[]{:S(2)}, u32[]{:S(2)}) collective-permute-start(bf16[128,2048]{1,0:T(8,128)(2,1)S(1)} %add_convert_fusion), channel_id=1, source_target_pairs={{0,1},{1,0},{2,3},{3,2},{4,5},{5,4},{6,7},{7,6},{8,9},{9,8},{10,11... | collective-permute-start | bytes 1572872 | tf_op jit(solution)/shard_map/ppermute | solution.py:841
  488.0 1.4 copy-start.5
  489.1 1.2 collective-permute-start.2
  489.4 5.0 copy-start.7
  489.8 23.5 %collective-permute-start.1 = (bf16[128,2048]{1,0:T(8,128)(2,1)S(1)}, bf16[128,2048]{1,0:T(8,128)(2,1)S(1)}, u32[]{:S(2)}, u32[]{:S(2)}) collective-permute-start(bf16[128,2048]{1,0:T(8,128)(2,1)S(1)} %fusion.7), channel_id=1, source_target_pairs={{0,1},{1,0},{2,3},{3,2},{4,5},{5,4},{6,7},{7,6},{8,9},{9,8},{10,11... | collective-permute-start | bytes 1572872 | tf_op jit(solution)/shard_map/ppermute | solution.py:841
  490.3 7.0 %collective-permute-start.5 = (f32[2,2048]{1,0:T(2,128)S(1)}, f32[2,2048]{1,0:T(2,128)S(1)}, u32[]{:S(2)}, u32[]{:S(2)}) collective-permute-start(f32[2,2048]{1,0:T(2,128)S(1)} %fusion.22), channel_id=1, source_target_pairs={{0,6},{2,4},{4,2},{6,0},{1,7},{3,5},{5,3},{7,1},{8,14},{10,12},{12... | collective-permute-start | bytes 49160 | tf_op jit(solution)/shard_map/ppermute | solution.py:841
  492.0 5.4 %collective-permute-start.4 = (f32[2,2048]{1,0:T(2,128)S(1)}, f32[2,2048]{1,0:T(2,128)S(1)}, u32[]{:S(2)}, u32[]{:S(2)}) collective-permute-start(f32[2,2048]{1,0:T(2,128)S(1)} %fusion.22), channel_id=1, source_target_pairs={{0,4},{2,6},{4,0},{6,2},{1,5},{3,7},{5,1},{7,3},{8,12},{10,14},{12... | collective-permute-start | bytes 49160 | tf_op jit(solution)/shard_map/ppermute | solution.py:841
  494.4 3.7 collective-permute-start.3
  494.4 13.5 %copy-start.16 = (bf16[4,128,128]{2,1,0:T(8,128)(2,1)S(1)}, bf16[4,128,128]{2,1,0:T(8,128)(2,1)}, u32[]{:S(2)}) copy-start(bf16[4,128,128]{2,1,0:T(8,128)(2,1)} %get-tuple-element.52) | copy-start | bytes 393220
  494.4 13.6 %copy-start.20 = (bf16[128,1024]{1,0:T(8,128)(2,1)S(1)}, bf16[128,1024]{1,0:T(8,128)(2,1)}, u32[]{:S(2)}) copy-start(bf16[128,1024]{1,0:T(8,128)(2,1)} %get-tuple-element.51) | copy-start | bytes 786436
  494.4 14.4 %copy-start.19 = (bf16[128,1024]{1,0:T(8,128)(2,1)S(1)}, bf16[128,1024]{1,0:T(8,128)(2,1)}, u32[]{:S(2)}) copy-start(bf16[128,1024]{1,0:T(8,128)(2,1)} %get-tuple-element.53) | copy-start | bytes 786436
  498.1 13.3 %collective-permute-start.8 = (f32[2,2048]{1,0:T(2,128)S(1)}, f32[2,2048]{1,0:T(2,128)S(1)}, u32[]{:S(2)}, u32[]{:S(2)}) collective-permute-start(f32[2,2048]{1,0:T(2,128)S(1)} %add_add_fusion), channel_id=1, source_target_pairs={{0,24},{8,16},{16,8},{24,0},{1,25},{9,17},{17,9},{25,1},{2,26},{10... | collective-permute-start | bytes 49160 | tf_op jit(solution)/shard_map/ppermute | solution.py:841
  500.5 10.9 %collective-permute-start.7 = (f32[2,2048]{1,0:T(2,128)S(1)}, f32[2,2048]{1,0:T(2,128)S(1)}, u32[]{:S(2)}, u32[]{:S(2)}) collective-permute-start(f32[2,2048]{1,0:T(2,128)S(1)} %add_add_fusion), channel_id=1, source_target_pairs={{0,16},{8,24},{16,0},{24,8},{1,17},{9,25},{17,1},{25,9},{2,18},{10... | collective-permute-start | bytes 49160 | tf_op jit(solution)/shard_map/ppermute | solution.py:841
  507.8 3.7 collective-permute-start.6
